TPU v7x, 256 devices: a whole 4x4x8 slice. The times are simulated.
256 devices in a mesh: seq: 32 (over x, y, core), tp: 8 (over z).
Axes of the slice: x: 4, y: 4, z: 8, core: 2. Of those that a mesh axis runs over, the one named last changes fastest.
Arguments:
- queries: bfloat16 [16384, 8192], P('seq', 'tp'), may hold values from -6 to 6
- keys: bfloat16 [16384, 8192], P('seq', 'tp'), may hold values from -0.5 to 0.5
- values: bfloat16 [16384, 8192], P('seq', 'tp'), may hold values from -6 to 6
- gate: bfloat16 [16384, 8192], P('seq', 'tp'), may hold values from -6 to 6
- log_decay: float32 [16384, 64], P('seq', 'tp'), may hold values from -0.8 to 0
- out_grad: bfloat16 [16384, 8192], P('seq', 'tp'), may hold values from -6 to 6
Outputs:
- output: bfloat16 [16384, 8192], P('seq', 'tp')
- query_grad: bfloat16 [16384, 8192], P('seq', 'tp')
- key_grad: bfloat16 [16384, 8192], P('seq', 'tp')
- value_grad: bfloat16 [16384, 8192], P('seq', 'tp')
- gate_grad: bfloat16 [16384, 8192], P('seq', 'tp')
All inputs are finite; a program needn't handle non-finite values.
Results may differ from a plain program's by a relative error of at most 0.0051.
Values sent between devices are 32-bit elements; how exact they have to be, the bound alone decides.
No kernel may reach another device: no remote copies, remote signals or barrier semaphores. Data moves between devices by JAX's collectives and lax.ppermute only.
A program may use at most 128 MiB of HBM per device.

v0:
```python
import jax
import jax.numpy as jnp
from jax import lax
from jax.sharding import Mesh
from jax.sharding import PartitionSpec as P

HEAD_COUNT = 64
HEAD = 128
SEQ = ("seq_0", "seq_1", "seq_2")


HIGH = lax.Precision.HIGHEST


def nothing_yet(x, identity):
    return jax.tree.map(
        lambda part, zero: jnp.zeros_like(part) + jnp.asarray(zero, part.dtype), x, identity
    )


def prefix_by_axis(x, axes, combine, identity, reverse):
    before = start = nothing_yet(x, identity)
    subtotal = x
    for axis in reversed(axes):
        size, index = (lax.axis_size(axis), lax.axis_index(axis))
        pieces = jax.tree.map(lambda part: lax.all_gather(part, axis), subtotal)
        inside, subtotal = (start, start)
        for k in reversed(range(size)) if reverse else range(size):
            passed = k > index if reverse else k < index
            subtotal = combine(subtotal, jax.tree.map(lambda part: part[k], pieces))
            inside = jax.tree.map(lambda new, old: jnp.where(passed, new, old), subtotal, inside)
        before = combine(inside, before)
    return before


def from_everyone(x, axis):
    copies = jnp.broadcast_to(x, (lax.axis_size(axis), *x.shape))
    return lax.all_to_all(copies, axis, split_axis=0, concat_axis=0, tiled=True)


def over_copies(x, axis):
    return from_everyone(x, axis).sum(axis=0)


def decay_table(within):
    gap = within.T[:, :, None] - within.T[:, None, :]
    rows = lax.broadcasted_iota(jnp.int32, gap.shape, 1)
    cols = lax.broadcasted_iota(jnp.int32, gap.shape, 2)
    return jnp.where(rows >= cols, jnp.exp(jnp.minimum(gap, 0.0)), 0.0)


def combine(earlier, later):
    return (earlier[0] * later[0], later[0][:, None, None] * earlier[1] + later[1])


def shards(queries, keys, values, gate, log_decay, out_grad):
    tokens = queries.shape[0]
    heads = log_decay.shape[1]
    width = HEAD_COUNT * HEAD
    qh = queries.reshape(tokens, heads, HEAD)
    kh = keys.reshape(tokens, heads, HEAD)
    vh = values.reshape(tokens, heads, HEAD)
    within = jnp.cumsum(log_decay, axis=0)
    last = within[-1]
    decay = decay_table(within)
    scores = jnp.einsum("thd,shd->hts", qh, kh, preferred_element_type=jnp.float32)
    probs = (scores * decay).astype(jnp.bfloat16)
    intra = jnp.einsum("hts,shd->thd", probs, vh, preferred_element_type=jnp.float32)
    qf = qh.astype(jnp.float32)
    kf = kh.astype(jnp.float32)
    vf = vh.astype(jnp.float32)
    grow = jnp.exp(within)[:, :, None]
    tail = jnp.exp(last[None, :] - within)[:, :, None]
    local = jnp.einsum("thd,the->hde", kf * tail, vf, precision=HIGH)
    factor = jnp.exp(last)
    identity = (jnp.ones((heads,), jnp.float32), jnp.zeros((heads, HEAD, HEAD), jnp.float32))
    state = prefix_by_axis((factor, local), SEQ, combine, identity, False)[1]
    inter = grow * jnp.einsum("thd,hde->the", qf, state, precision=HIGH)
    attn = (intra + inter).reshape(tokens, heads * HEAD)
    squares = over_copies(jnp.sum(attn * attn, axis=1), "tp")
    scale = lax.rsqrt(squares / width + 1e-06)
    normed = attn * scale[:, None]
    sig = jax.nn.sigmoid(gate.astype(jnp.float32))
    output = (normed * sig).astype(jnp.bfloat16)
    upstream = out_grad.astype(jnp.float32)
    dnorm = upstream * sig
    gate_grad = (upstream * normed * sig * (1.0 - sig)).astype(jnp.bfloat16)
    center = over_copies(jnp.sum(dnorm * normed, axis=1), "tp") / width
    attn_grad = (scale[:, None] * (dnorm - normed * center[:, None])).astype(jnp.bfloat16)
    grad_h = attn_grad.reshape(tokens, heads, HEAD)
    gradf = grad_h.astype(jnp.float32)
    weighted = jnp.einsum("thd,the->hde", qf * grow, gradf, precision=HIGH)
    grad_state = prefix_by_axis((factor, weighted), SEQ, combine, identity, True)[1]
    pgrad = (
        jnp.einsum("thd,shd->hts", grad_h, vh, preferred_element_type=jnp.float32) * decay
    ).astype(jnp.bfloat16)
    query_grad = jnp.einsum(
        "hts,shd->thd", pgrad, kh, preferred_element_type=jnp.float32
    ) + grow * jnp.einsum("the,hde->thd", gradf, state, precision=HIGH)
    key_grad = jnp.einsum(
        "hts,thd->shd", pgrad, qh, preferred_element_type=jnp.float32
    ) + tail * jnp.einsum("the,hde->thd", vf, grad_state, precision=HIGH)
    value_grad = jnp.einsum(
        "hts,thd->shd", probs, grad_h, preferred_element_type=jnp.float32
    ) + tail * jnp.einsum("thd,hde->the", kf, grad_state, precision=HIGH)
    flat = heads * HEAD
    return (
        output,
        query_grad.reshape(tokens, flat).astype(jnp.bfloat16),
        key_grad.reshape(tokens, flat).astype(jnp.bfloat16),
        value_grad.reshape(tokens, flat).astype(jnp.bfloat16),
        gate_grad,
    )


def solution(mesh):
    split = Mesh(mesh.devices.reshape(4, 4, 2, mesh.shape["tp"]), ("seq_0", "seq_1", "seq_2", "tp"))
    return jax.shard_map(
        shards,
        mesh=split,
        in_specs=(
            P(SEQ, "tp"),
            P(SEQ, "tp"),
            P(SEQ, "tp"),
            P(SEQ, "tp"),
            P(SEQ, "tp"),
            P(SEQ, "tp"),
        ),
        out_specs=(P(SEQ, "tp"), P(SEQ, "tp"), P(SEQ, "tp"), P(SEQ, "tp"), P(SEQ, "tp")),
        check_vma=False,
    )
```

profile of v0, /device:TPU:1, one launch (start us, length us, event | category | flops | bytes accessed | tf_op | source)
XLA Modules:
  0.0 250.3 jit_solution(18211787594199454426)
XLA Ops:
  13.7 4.7 %all-gather.2 = f32[2,1,8]{2,1,0:T(1,128)S(1)} all-gather(f32[1,1,8]{2,1,0:T(1,128)S(1)} %bitcast.318), channel_id=1, replica_groups=mesh['seq_0'=4,'seq_1'=4,'seq_2'=2,'tp'=8] {'seq_2'}, dimensions={0}, use_global_device_ids=true | all-gather | bytes 96 | tf_op jit(solution)/shard_map/all_gather | solution.py:26
  18.5 6.2 %all-gather.3 = f32[4,1,8]{2,1,0:T(1,128)S(1)} all-gather(f32[1,1,8]{2,1,0:T(1,128)S(1)} %get-tuple-element.66), channel_id=1, replica_groups=mesh['seq_0'=4,'seq_1'=4,'seq_2'=2,'tp'=8] {'seq_1'}, dimensions={0}, use_global_device_ids=true | all-gather | bytes 160 | tf_op jit(solution)/shard_map/all_gather | solution.py:26
  24.6 8.1 %all-gather.21.cloned.1.call-done = f32[16,128,128]{2,1,0:T(8,128)} async-done(((f32[8,128,128]{2,1,0:T(8,128)}), f32[16,128,128]{2,1,0:T(8,128)}) %all-gather.21.cloned.1.call-update) | async-done | bytes 1048592 | tf_op jit(solution)/shard_map/all_gather | solution.py:26
  35.0 34.2 %all-gather.13.cloned.1.call-done = f32[4,8,128,128]{3,2,1,0:T(8,128)} async-done(((f32[1,8,128,128]{3,2,1,0:T(8,128)}), f32[4,8,128,128]{3,2,1,0:T(8,128)}) %all-gather.13.cloned.1.call-update) | async-done | bytes 2097168 | tf_op jit(solution)/shard_map/all_gather | solution.py:26
  69.1 2.5 %multiply_add_fusion.1 = f32[1,8,128,128]{3,2,1,0:T(8,128)} fusion(f32[4,8,128,128]{3,2,1,0:T(8,128)} %all-gather.13.cloned.1.call-done, f32[8]{0:T(128)S(1)} %get-tuple-element.53, f32[8]{0:T(128)S(1)} %get-tuple-element.57, f32[8]{0:T(128)S(1)} %get-tuple-element.56, f32[8]{0:T(128)S(1)} %get-tuple-element.55), kind=kLoop, calls=%fused_computation.85 | loop fusion | flops 917504 | bytes 2621568 | tf_op jit(solution)/shard_map/add | solution.py:53
  71.7 7.6 %all-gather.4 = f32[4,1,8]{2,1,0:T(1,128)S(1)} all-gather(f32[1,1,8]{2,1,0:T(1,128)S(1)} %get-tuple-element.51), channel_id=1, replica_groups=mesh['seq_0'=4,'seq_1'=4,'seq_2'=2,'tp'=8] {'seq_0'}, dimensions={0}, use_global_device_ids=true | all-gather | bytes 160 | tf_op jit(solution)/shard_map/all_gather | solution.py:26
  84.8 2.9 %fusion.16 = f32[8,512,128]{1,2,0:T(8,128)} fusion(bf16[8,512,512]{2,1,0:T(8,128)(2,1)S(1)} %multiply_convert_fusion.1, bf16[512,1024]{1,0:T(8,128)(2,1)S(1)} %copy-done), kind=kOutput, calls=%fused_computation.31 | convolution fusion | flops 536870912 | bytes 7340032 | tf_op jit(solution)/shard_map/hts,shd->thd/dot_general | solution.py:68
  87.7 17.5 %all-gather.15.cloned.1.call-done = f32[4,8,128,128]{3,2,1,0:T(8,128)} async-done(((f32[1,8,128,128]{3,2,1,0:T(8,128)}), f32[4,8,128,128]{3,2,1,0:T(8,128)}) %all-gather.15.cloned.1.call-update) | async-done | bytes 2097168 | tf_op jit(solution)/shard_map/all_gather | solution.py:26
  105.3 3.5 %fusion.37 = f32[8,128,128]{2,1,0:T(8,128)S(1)} fusion(f32[4,8,128,128]{3,2,1,0:T(8,128)} %all-gather.15.cloned.1.call-done, f32[4,8,128,128]{3,2,1,0:T(8,128)} %all-gather.13.cloned.1.call-done, f32[16,128,128]{2,1,0:T(8,128)S(1)} %copy-done.15, f32[8]{0:T(128)S(1)} %get-tuple-element.63, f32[8]{0:T(128)S(1)} %get-tuple-element.65, ...), kind=kLoop, calls=%fused_computation.57 | loop fusion | flops 4063232 | bytes 5767562 | tf_op jit(solution)/shard_map/add | solution.py:53
  108.8 2.6 %multiply_reduce_fusion.1 = (f32[512]{0:T(512)S(1)}, f32[512,8,128]{0,2,1:T(8,128)}) fusion(f32[8,128,128]{2,1,0:T(8,128)S(1)} %fusion.37, bf16[512,8,128]{0,2,1:T(8,128)(2,1)S(1)} %bitcast.302, f32[512,8]{0,1:T(8,128)S(1)} %get-tuple-element.39, f32[8,512,128]{1,2,0:T(8,128)S(1)} %copy-done.11), kind=kOutput, calls=%fused_computation.27 | convolution fusion | flops 807403008 | bytes 5785600 | tf_op jit(solution)/shard_map/thd,hde->the/dot_general | solution.py:78
  112.0 6.7 %all-to-all-start = ((f32[8,1,512]{2,1,0:T(1,128)}), f32[8,1,512]{2,1,0:T(1,128)S(1)}, u32[]{:S(2)}, u32[]{:S(2)}) async-start(f32[8,1,512]{2,1,0:T(1,128)} %broadcast_in_dim.15), calls=%async_computation | async-start | bytes 32768 | tf_op jit(solution)/shard_map/all_to_all | solution.py:38
  120.7 4.6 %all-to-all-done = f32[8,1,512]{2,1,0:T(1,128)S(1)} async-done(((f32[8,1,512]{2,1,0:T(1,128)}), f32[8,1,512]{2,1,0:T(1,128)S(1)}, u32[]{:S(2)}, u32[]{:S(2)}) %all-to-all-start) | async-done | bytes 16416 | tf_op jit(solution)/shard_map/all_to_all | solution.py:38
  125.4 2.3 multiply_reduce_fusion
  127.8 9.0 %all_to_all.12 = f32[8,1,512]{2,1,0:T(1,128)S(1)} all-to-all(f32[8,1,512]{2,1,0:T(1,128)S(1)} %broadcast_in_dim.30), channel_id=1, replica_groups=mesh['seq_0'=4,'seq_1'=4,'seq_2'=2,'tp'=8] {'tp'}, dimensions={0} | all-to-all | bytes 32768 | tf_op jit(solution)/shard_map/all_to_all | solution.py:38
  136.8 4.5 %fusion.2 = (bf16[512,1024]{1,0:T(8,128)(2,1)}, bf16[512,1024]{1,0:T(8,128)(2,1)}, bf16[512,1024]{1,0:T(8,128)(2,1)}) fusion(bf16[512,1024]{1,0:T(8,128)(2,1)} %param.11, f32[512,1024]{1,0:T(8,128)S(1)} %copy.124, f32[512]{0:T(512)S(1)} %add_rsqrt_fusion, bf16[512,1024]{1,0:T(8,128)(2,1)} %param.9, f32[512]{0:T(512)S(1)} %broadcast_multiply_fusion), kind=kLoop, calls=%fused_computation.8 | loop fusion | flops 9437184 | bytes 7344128 | tf_op jit(solution)/shard_map/convert_element_type | solution.py:87
  144.9 12.8 %all-gather.23.cloned.1.call-done = f32[16,128,128]{2,1,0:T(8,128)} async-done(((f32[8,128,128]{2,1,0:T(8,128)}), f32[16,128,128]{2,1,0:T(8,128)}) %all-gather.23.cloned.1.call-update) | async-done | bytes 1048592 | tf_op jit(solution)/shard_map/all_gather | solution.py:26
  160.0 33.9 %all-gather.17.cloned.1.call-done = f32[4,8,128,128]{3,2,1,0:T(8,128)} async-done(((f32[1,8,128,128]{3,2,1,0:T(8,128)}), f32[4,8,128,128]{3,2,1,0:T(8,128)}) %all-gather.17.cloned.1.call-update) | async-done | bytes 2097168 | tf_op jit(solution)/shard_map/all_gather | solution.py:26
  193.9 2.5 %multiply_add_fusion = f32[1,8,128,128]{3,2,1,0:T(8,128)} fusion(f32[4,8,128,128]{3,2,1,0:T(8,128)} %all-gather.17.cloned.1.call-done, f32[8]{0:T(128)S(1)} %get-tuple-element.52, f32[8]{0:T(128)S(1)} %get-tuple-element.54, f32[8]{0:T(128)S(1)} %get-tuple-element.57, f32[8]{0:T(128)S(1)} %get-tuple-element.56), kind=kLoop, calls=%fused_computation.84 | loop fusion | flops 917504 | bytes 2621568 | tf_op jit(solution)/shard_map/add | solution.py:53
  196.5 7.6 %all-gather.5 = f32[4,1,8]{2,1,0:T(1,128)S(1)} all-gather(f32[1,1,8]{2,1,0:T(1,128)S(1)} %get-tuple-element.50), channel_id=1, replica_groups=mesh['seq_0'=4,'seq_1'=4,'seq_2'=2,'tp'=8] {'seq_0'}, dimensions={0}, use_global_device_ids=true | all-gather | bytes 160 | tf_op jit(solution)/shard_map/all_gather | solution.py:26
  212.6 4.4 %fusion.59 = f32[8,128,512]{2,1,0:T(8,128)} fusion(bf16[512,8,128]{0,2,1:T(8,128)(2,1)S(1)} %bitcast.308, bf16[8,512,512]{2,1,0:T(8,128)(2,1)} %copy-done.1), kind=kOutput, calls=%fused_computation.139 | convolution fusion | flops 536870912 | bytes 7340032 | tf_op jit(solution)/shard_map/hts,thd->shd/dot_general | solution.py:103
  219.0 11.0 %all-gather.19.cloned.1.call-done = f32[4,8,128,128]{3,2,1,0:T(8,128)} async-done(((f32[1,8,128,128]{3,2,1,0:T(8,128)}), f32[4,8,128,128]{3,2,1,0:T(8,128)}) %all-gather.19.cloned.1.call-update) | async-done | bytes 2097168 | tf_op jit(solution)/shard_map/all_gather | solution.py:26
  230.0 3.5 %fusion.30 = f32[8,128,128]{2,1,0:T(8,128)S(1)} fusion(f32[4,8,128,128]{3,2,1,0:T(8,128)} %all-gather.19.cloned.1.call-done, f32[4,8,128,128]{3,2,1,0:T(8,128)} %all-gather.17.cloned.1.call-done, f32[16,128,128]{2,1,0:T(8,128)S(1)} %copy-done.16, f32[8]{0:T(128)S(1)} %get-tuple-element.62, f32[8]{0:T(128)S(1)} %get-tuple-element.64, ...), kind=kLoop, calls=%fused_computation.46 | loop fusion | flops 4063232 | bytes 5767562 | tf_op jit(solution)/shard_map/add | solution.py:53
  235.7 2.4 copy.136
  238.1 3.1 %fusion.6 = bf16[512,8,128]{0,2,1:T(8,128)(2,1)} fusion(f32[8,512,128]{1,2,0:T(8,128)S(1)} %copy-done.9, f32[8,128,128]{2,1,0:T(8,128)} %copy-done.12, f32[512,8]{0,1:T(8,128)S(1)} %subtract_exponential_fusion, bf16[512,1024]{1,0:T(8,128)(2,1)S(1)} %copy-done), kind=kOutput, calls=%fused_computation.14 | convolution fusion | flops 806879232 | bytes 4734976 | tf_op jit(solution)/shard_map/the,hde->thd/dot_general | solution.py:102
  (83 shorter events, 37.8 us)
Async XLA Ops:
  7.2 4.4 %copy-start = (bf16[512,1024]{1,0:T(8,128)(2,1)S(1)}, bf16[512,1024]{1,0:T(8,128)(2,1)}, u32[]{:S(2)}) copy-start(bf16[512,1024]{1,0:T(8,128)(2,1)} %param.8) | copy-start | bytes 3145732
  7.2 25.6 %all-gather.21.cloned.1.call-start = ((), (), s32[]{:S(2)}) async-start(), calls=%async_computation.6 | async-start | bytes 1572864 | tf_op jit(solution)/shard_map/all_gather | solution.py:26
  11.6 69.3 %copy-start.6 = (bf16[512,1024]{0,1:T(8,128)(2,1)}, bf16[512,1024]{0,1:T(8,128)(2,1)S(1)}, u32[]{:S(2)}) copy-start(bf16[512,1024]{0,1:T(8,128)(2,1)S(1)} %copy.116) | copy-start | bytes 3145732
  13.7 55.4 %all-gather.13.cloned.1.call-start = ((), (), s32[]{:S(2)}) async-start(), calls=%async_computation.2 | async-start | bytes 2621440 | tf_op jit(solution)/shard_map/all_gather | solution.py:26
  34.9 70.3 %all-gather.15.cloned.1.call-start = ((), (), s32[]{:S(2)}) async-start(), calls=%async_computation.3 | async-start | bytes 2621440 | tf_op jit(solution)/shard_map/all_gather | solution.py:26
  80.8 27.9 %copy-start.4 = (bf16[512,1024]{0,1:T(8,128)(2,1)}, bf16[512,1024]{0,1:T(8,128)(2,1)S(1)}, u32[]{:S(2)}) copy-start(bf16[512,1024]{0,1:T(8,128)(2,1)S(1)} %copy.115) | copy-start | bytes 3145732
  82.8 1.9 copy-start.1
  84.8 20.5 %copy-start.15 = (f32[16,128,128]{2,1,0:T(8,128)S(1)}, f32[16,128,128]{2,1,0:T(8,128)}, u32[]{:S(2)}) copy-start(f32[16,128,128]{2,1,0:T(8,128)} %all-gather.21.cloned.1.call-done) | copy-start | bytes 3145732
  105.3 3.5 %copy-start.11 = (f32[8,512,128]{1,2,0:T(8,128)S(1)}, f32[8,512,128]{1,2,0:T(8,128)}, u32[]{:S(2)}) copy-start(f32[8,512,128]{1,2,0:T(8,128)} %fusion.16) | copy-start | bytes 6291460
  108.7 2.7 %copy-start.13 = (f32[8,128,128]{2,1,0:T(8,128)}, f32[8,128,128]{2,1,0:T(8,128)S(1)}, u32[]{:S(2)}) copy-start(f32[8,128,128]{2,1,0:T(8,128)S(1)} %fusion.37) | copy-start | bytes 1572868
  112.0 13.4 %all-to-all-start = ((f32[8,1,512]{2,1,0:T(1,128)}), f32[8,1,512]{2,1,0:T(1,128)S(1)}, u32[]{:S(2)}, u32[]{:S(2)}) async-start(f32[8,1,512]{2,1,0:T(1,128)} %broadcast_in_dim.15), calls=%async_computation | async-start | bytes 32768 | tf_op jit(solution)/shard_map/all_to_all | solution.py:38
  118.8 38.9 %all-gather.23.cloned.1.call-start = ((), (), s32[]{:S(2)}) async-start(), calls=%async_computation.7 | async-start | bytes 1572864 | tf_op jit(solution)/shard_map/all_gather | solution.py:26
  141.2 1.6 copy-start.5
  144.8 49.1 %all-gather.17.cloned.1.call-start = ((), (), s32[]{:S(2)}) async-start(), calls=%async_computation.4 | async-start | bytes 2621440 | tf_op jit(solution)/shard_map/all_gather | solution.py:26
  159.8 70.2 %all-gather.19.cloned.1.call-start = ((), (), s32[]{:S(2)}) async-start(), calls=%async_computation.5 | async-start | bytes 2621440 | tf_op jit(solution)/shard_map/all_gather | solution.py:26
  204.1 2.1 copy-start.7
  206.2 2.0 copy-start.2
  206.2 2.0 copy-start.14
  212.6 4.4 %copy-start.3 = (bf16[8,512,512]{2,1,0:T(8,128)(2,1)S(1)}, bf16[8,512,512]{2,1,0:T(8,128)(2,1)}, u32[]{:S(2)}) copy-start(bf16[8,512,512]{2,1,0:T(8,128)(2,1)} %copy-done.2) | copy-start | bytes 12582916
  217.0 13.0 %copy-start.16 = (f32[16,128,128]{2,1,0:T(8,128)S(1)}, f32[16,128,128]{2,1,0:T(8,128)}, u32[]{:S(2)}) copy-start(f32[16,128,128]{2,1,0:T(8,128)} %all-gather.23.cloned.1.call-done) | copy-start | bytes 3145732
  230.0 3.5 %copy-start.8 = (bf16[512,1024]{0,1:T(8,128)(2,1)S(1)}, bf16[512,1024]{0,1:T(8,128)(2,1)}, u32[]{:S(2)}) copy-start(bf16[512,1024]{0,1:T(8,128)(2,1)} %copy-done.6) | copy-start | bytes 3145732
  230.0 3.5 %copy-start.10 = (f32[8,128,512]{2,1,0:T(8,128)S(1)}, f32[8,128,512]{2,1,0:T(8,128)}, u32[]{:S(2)}) copy-start(f32[8,128,512]{2,1,0:T(8,128)} %fusion.59) | copy-start | bytes 6291460
  233.5 2.2 copy-start.12
  235.7 2.4 copy-start.9
Sparse Core Ops, SparseCore 0:
  13.8 18.8 all-gather.20
  35.1 33.9 all-gather.12
  71.8 33.3 all-gather.14
  145.0 12.6 all-gather.22
  159.9 33.9 all-gather.16
  196.6 33.3 all-gather.18
where the time goes:
time: 251 us; the launch traced here: 250 us
  waiting for transfers between devices  122 us (49%)
  blocking collectives  35 us (14%)
  matrix products  28.9 us (12%)
  other arithmetic  25.7 us (10%)
  local copies, waits for them, and re-layouts  16.9 us (7%)
  between operations  14.4 us (6%)
  starting transfers between devices  7.15 us (3%)
    all_gather x6, waiting for transfers between devices, prefix_by_axis(): pieces = jax.tree.map(lambda part: lax.all_gather(part, axis), subtotal)  117 us
    all_gather x4, blocking collectives, prefix_by_axis(): pieces = jax.tree.map(lambda part: lax.all_gather(part, axis), subtotal)  26 us
    add x6, other arithmetic, combine(): later[0][:, None, None] * earlier[1] + later[1]  16.3 us
    unnamed x39, local copies, waits for them, and re-layouts  12.4 us
    all_to_all x1, blocking collectives, from_everyone(): return lax.all_to_all(copies, axis, split_axis=0, concat_axis=0, tiled=True)  8.98 us
    all_to_all x1, starting transfers between devices, from_everyone(): return lax.all_to_all(copies, axis, split_axis=0, concat_axis=0, tiled=True)  6.73 us
  transfers between devices with their start and end apart: 7, of which 7 were waited for; matrix products, arithmetic and copies ran while one was open for 9% of the time, Pallas kernels for 0%

commit v1 on v0

v1 whole, which is shorter than its diff:
```python
import jax
import jax.numpy as jnp
from jax import lax
from jax.experimental import pallas as pl
from jax.experimental.pallas import tpu as pltpu
from jax.sharding import Mesh
from jax.sharding import PartitionSpec as P

HEAD_COUNT = 64
HEAD = 128
SEQ = ("x", "y", "c")
CHIPS = ("x", "y")
HIGH = lax.Precision.HIGHEST
F32 = jnp.float32
BF16 = jnp.bfloat16
PAD = 8

NN = (((1,), (0,)), ((), ()))
NT = (((1,), (1,)), ((), ()))
TN = (((0,), (0,)), ((), ()))


def dot(a, b, dims, precision=None):
    return lax.dot_general(a, b, dims, precision=precision, preferred_element_type=F32)


def halves(x):
    high = x.astype(BF16)
    return high, (x - high.astype(F32)).astype(BF16)


def as_column(row):
    return jnp.transpose(jnp.broadcast_to(row, (HEAD, row.shape[1])))


def sigmoid(x):
    return 1.0 / (1.0 + jnp.exp(-x))


def params(mib=40):
    return pltpu.CompilerParams(
        dimension_semantics=("arbitrary",), vmem_limit_bytes=mib * 2**20
    )


def outer_state(wide, narrow):
    both = dot(narrow, jnp.concatenate(halves(wide), axis=1), TN)
    return both[:, :HEAD] + both[:, HEAD:]


def put_state(ref, i, state, factor):
    ref[i, 0:HEAD, :] = state
    ref[i, HEAD : HEAD + PAD, :] = jnp.broadcast_to(factor, (PAD, HEAD))


def local_kernel(core_ref, rate_ref, k_ref, v_ref, within_ref, theirs_ref, mine_ref):
    step = pl.program_id(0)
    tokens = rate_ref.shape[0]
    group = k_ref.shape[1] // HEAD

    @pl.when(step == 0)
    def _():
        early = lax.broadcasted_iota(jnp.int32, (tokens, tokens), 0)
        late = lax.broadcasted_iota(jnp.int32, (tokens, tokens), 1)
        upto = (early <= late).astype(F32)
        within_ref[...] = dot(rate_ref[...], upto, TN, HIGH)

    first = (core_ref[0] ^ (1 - step)) * group

    def part(out_ref):
        for i in range(group):
            within = within_ref[pl.ds(first + i, 1), :]
            last = within[:, tokens - 1 :]
            tail = as_column(jnp.exp(last - within))
            cols = slice(i * HEAD, (i + 1) * HEAD)
            scaled = k_ref[:, cols].astype(F32) * tail
            put_state(out_ref, i, outer_state(scaled, v_ref[:, cols]), jnp.exp(last))

    @pl.when(step == 0)
    def _():
        part(theirs_ref)

    @pl.when(step == 1)
    def _():
        part(mine_ref)


def combine_kernel(lead_ref, mine_ref, other_ref, out_ref):
    lead = lead_ref[0] == 1
    group = mine_ref.shape[0]
    rows = HEAD // 4
    for i in range(group):
        own = mine_ref[i, HEAD : HEAD + PAD, :]
        far = other_ref[i, HEAD : HEAD + PAD, :]
        mine = mine_ref[i, 0:HEAD, :]
        other = other_ref[i, 0:HEAD, :]
        both = jnp.where(lead, far[0:1] * mine + other, own[0:1] * other + mine)
        for j in range(4):
            out_ref[4 * i + j, 0:rows, :] = both[j * rows : (j + 1) * rows]
            out_ref[4 * i + j, rows : rows + PAD, :] = own * far


def scan_kernel(reverse, in_ref, out_ref):
    chips, rows = out_ref.shape[0], out_ref.shape[1]
    state = jnp.zeros(out_ref.shape[1:], F32)
    for n in reversed(range(chips)) if reverse else range(chips):
        out_ref[n] = state
        state = in_ref[n, rows : rows + 1, :] * state + in_ref[n, 0:rows, :]


def decay_block(within, column, start, size, width):
    gap = jnp.concatenate([column[start : start + size]] * (width // HEAD), axis=1)
    gap = gap - within[:, :width]
    rows = start + lax.broadcasted_iota(jnp.int32, gap.shape, 0)
    cols = lax.broadcasted_iota(jnp.int32, gap.shape, 1)
    return jnp.where(rows >= cols, jnp.exp(jnp.minimum(gap, 0.0)), 0.0)


def inside_kernel(within_ref, q_ref, k_ref, v_ref, probs_ref, intra_ref):
    within = within_ref[pl.ds(pl.program_id(0), 1), :]
    column = as_column(within)
    tokens = q_ref.shape[0]
    size = tokens // 2
    for start in (0, size):
        width = start + size
        scores = dot(q_ref[start:width, :], k_ref[0:width, :], NT)
        probs = (scores * decay_block(within, column, start, size, width)).astype(BF16)
        probs_ref[0, start:width, 0:width] = probs
        intra_ref[start:width, :] = dot(probs, v_ref[0:width, :], NN)


def pick_state(follows, chip_ref, lead_ref, i):
    chip = chip_ref[i]
    return jnp.where(
        follows, lead_ref[i, HEAD : HEAD + 1, :] * chip + lead_ref[i, 0:HEAD, :], chip
    )


def attn_kernel(
    core_ref, within_ref, q_ref, intra_ref, gate_ref, up_ref,
    chip_mine_ref, chip_other_ref, lead_mine_ref, lead_other_ref,
    attn_ref, state_ref, sums_ref, square_ref, inner_ref,
):
    step = pl.program_id(0)
    group = chip_mine_ref.shape[0]
    first = (core_ref[0] ^ step) * group

    @pl.when(step == 0)
    def _():
        square_ref[...] = jnp.zeros_like(square_ref)
        inner_ref[...] = jnp.zeros_like(inner_ref)

    def part(chip_ref, lead_ref):
        for i in range(group):
            cols = slice(i * HEAD, (i + 1) * HEAD)
            state = pick_state(core_ref[0] == 1, chip_ref, lead_ref, i)
            state_ref[i] = state
            grow = as_column(jnp.exp(within_ref[pl.ds(first + i, 1), :]))
            q = q_ref[:, cols]
            inter = dot(
                jnp.concatenate([q, q], axis=1), jnp.concatenate(halves(state), axis=1), NT
            )
            attn = intra_ref[:, cols] + grow * inter
            attn_ref[:, cols] = attn
            dnorm = up_ref[:, cols].astype(F32) * sigmoid(gate_ref[:, cols].astype(F32))
            square_ref[...] += attn * attn
            inner_ref[...] += dnorm * attn

    @pl.when(step == 0)
    def _():
        part(chip_mine_ref, lead_mine_ref)

    @pl.when(step == 1)
    def _():
        part(chip_other_ref, lead_other_ref)
        ones = jnp.ones((8, HEAD), F32)
        square = dot(ones, square_ref[...], NT, HIGH)
        inner = dot(ones, inner_ref[...], NT, HIGH)
        rows = lax.broadcasted_iota(jnp.int32, (8, HEAD), 0)
        packed = jnp.zeros((8, HEAD), F32)
        for i in range(4):
            cols = slice(i * HEAD, (i + 1) * HEAD)
            packed = jnp.where(rows == i, square[:, cols], packed)
            packed = jnp.where(rows == i + 4, inner[:, cols], packed)
        sums_ref[...] = jnp.broadcast_to(packed[None], sums_ref.shape)


def token_columns(table):
    def column(first):
        return jnp.concatenate([as_column(table[i : i + 1]) for i in range(first, first + 4)], axis=0)

    return column(0), column(4)


def grad_kernel(
    core_ref, sums_ref, within_ref, q_ref, attn_ref, gate_ref, up_ref,
    grad_ref, theirs_ref, mine_ref, table_ref,
):
    step = pl.program_id(0)
    tokens = q_ref.shape[0]
    group = q_ref.shape[1] // HEAD
    first = (core_ref[0] ^ (1 - step)) * group

    @pl.when(step == 0)
    def _():
        total = jnp.sum(sums_ref[...], axis=0) / (HEAD_COUNT * HEAD)
        scale = lax.rsqrt(total[0:4] + 1e-06)
        table_ref[0:4] = scale
        table_ref[4:8] = scale * total[4:8]

    scale, center = token_columns(table_ref[...])

    def part(out_ref):
        for i in range(group):
            cols = slice(i * HEAD, (i + 1) * HEAD)
            dnorm = up_ref[:, cols].astype(F32) * sigmoid(gate_ref[:, cols].astype(F32))
            normed = attn_ref[:, cols] * scale
            grad = (scale * (dnorm - normed * center)).astype(BF16)
            grad_ref[:, cols] = grad
            within = within_ref[pl.ds(first + i, 1), :]
            grown = q_ref[:, cols].astype(F32) * as_column(jnp.exp(within))
            put_state(out_ref, i, outer_state(grown, grad), jnp.exp(within[:, tokens - 1 :]))

    @pl.when(step == 0)
    def _():
        part(theirs_ref)

    @pl.when(step == 1)
    def _():
        part(mine_ref)


def gate_kernel(table_ref, attn_ref, gate_ref, up_ref, output_ref, gate_grad_ref):
    scale, _ = token_columns(table_ref[...])
    for i in range(attn_ref.shape[1] // HEAD):
        cols = slice(i * HEAD, (i + 1) * HEAD)
        normed = attn_ref[:, cols] * scale
        sig = sigmoid(gate_ref[:, cols].astype(F32))
        output_ref[:, cols] = (normed * sig).astype(BF16)
        gate_grad_ref[:, cols] = (
            up_ref[:, cols].astype(F32) * normed * sig * (1.0 - sig)
        ).astype(BF16)


def back_kernel(
    within_ref, q_ref, k_ref, v_ref, grad_ref, probs_ref, state_ref,
    query_grad_ref, key_ref, value_ref,
):
    within = within_ref[pl.ds(pl.program_id(0), 1), :]
    column = as_column(within)
    grow = jnp.exp(column)
    tokens = q_ref.shape[0]
    size = tokens // 2
    state = jnp.concatenate(halves(state_ref[0]), axis=0)
    for start in (0, size):
        width = start + size
        grad = grad_ref[start:width, :]
        pgrad = dot(grad, v_ref[0:width, :], NT)
        pgrad = (pgrad * decay_block(within, column, start, size, width)).astype(BF16)
        inter = dot(jnp.concatenate([grad, grad], axis=1), state, NN)
        query_grad_ref[start:width, :] = (
            dot(pgrad, k_ref[0:width, :], NN) + grow[start:width] * inter
        ).astype(BF16)
        key_part = dot(pgrad, q_ref[start:width, :], TN)
        value_part = dot(probs_ref[0, start:width, 0:width], grad, TN)
        if start == 0:
            key_ref[0:width, :] = key_part
            value_ref[0:width, :] = value_part
        else:
            key_ref[0:start, :] += key_part[0:start]
            value_ref[0:start, :] += value_part[0:start]
            key_ref[start:width, :] = key_part[start:width]
            value_ref[start:width, :] = value_part[start:width]


def final_kernel(
    core_ref, within_ref, k_ref, v_ref, key_part_ref, value_part_ref,
    chip_mine_ref, chip_other_ref, lead_mine_ref, lead_other_ref,
    key_grad_ref, value_grad_ref,
):
    step = pl.program_id(0)
    group = chip_mine_ref.shape[0]
    tokens = k_ref.shape[0]
    first = (core_ref[0] ^ step) * group

    def part(chip_ref, lead_ref):
        for i in range(group):
            cols = slice(i * HEAD, (i + 1) * HEAD)
            state = halves(pick_state(core_ref[0] == 0, chip_ref, lead_ref, i))
            within = within_ref[pl.ds(first + i, 1), :]
            tail = as_column(jnp.exp(within[:, tokens - 1 :] - within))
            k, v = k_ref[:, cols], v_ref[:, cols]
            key_inter = dot(
                jnp.concatenate([v, v], axis=1), jnp.concatenate(state, axis=0), NN
            )
            value_inter = dot(
                jnp.concatenate([k, k], axis=1), jnp.concatenate(state, axis=1), NT
            )
            key_grad_ref[:, cols] = (key_part_ref[:, cols] + tail * key_inter).astype(BF16)
            value_grad_ref[:, cols] = (
                value_part_ref[:, cols] + tail * value_inter
            ).astype(BF16)

    @pl.when(step == 0)
    def _():
        part(chip_mine_ref, lead_mine_ref)

    @pl.when(step == 1)
    def _():
        part(chip_other_ref, lead_other_ref)


def shape(dims, dtype=F32):
    return jax.ShapeDtypeStruct(dims, dtype)


def whole(dims):
    return pl.BlockSpec(dims, lambda *_: (0,) * len(dims))


def swap(x):
    return lax.ppermute(x, "c", [(0, 1), (1, 0)])


def spread(x):
    return lax.all_to_all(x, CHIPS, split_axis=0, concat_axis=0, tiled=True)


def shards(queries, keys, values, gate, log_decay, out_grad):
    tokens, flat = queries.shape
    heads = log_decay.shape[1]
    group = heads // 2
    half = group * HEAD
    chips = lax.axis_size("x") * lax.axis_size("y")
    rows = group * HEAD // chips
    core = lax.axis_index("c").astype(jnp.int32).reshape(1)
    packed = (group, HEAD + PAD, HEAD)
    states = (group, HEAD, HEAD)

    other_first = pl.BlockSpec((tokens, half), lambda s, c: (0, c[0] ^ (1 - s)))
    mine_first = pl.BlockSpec((tokens, half), lambda s, c: (0, c[0] ^ s))
    by_head = pl.BlockSpec((tokens, HEAD), lambda h: (0, h))

    def grid_of(inputs, outputs, scratch=()):
        return pltpu.PrefetchScalarGridSpec(
            num_scalar_prefetch=1,
            grid=(2,),
            in_specs=inputs,
            out_specs=outputs,
            scratch_shapes=list(scratch),
        )

    def combined(lead, mine, other):
        return pl.pallas_call(
            combine_kernel,
            grid_spec=pltpu.PrefetchScalarGridSpec(
                num_scalar_prefetch=1,
                grid=(1,),
                in_specs=[whole(packed)] * 2,
                out_specs=whole((chips, rows + PAD, HEAD)),
            ),
            out_shape=shape((chips, rows + PAD, HEAD)),
            compiler_params=params(),
            name="combine",
        )(lead, mine, other)

    def scanned(x, reverse):
        return pl.pallas_call(
            lambda i, o: scan_kernel(reverse, i, o),
            out_shape=shape((chips, rows, HEAD)),
            name="scan",
        )(x)

    within, theirs, mine = pl.pallas_call(
        local_kernel,
        grid_spec=grid_of(
            [whole((tokens, heads)), other_first, other_first],
            [whole((heads, tokens)), whole(packed), whole(packed)],
        ),
        out_shape=[shape((heads, tokens)), shape(packed), shape(packed)],
        compiler_params=params(),
        name="local",
    )(core, log_decay, keys, values)
    lead_mine = swap(theirs)
    chip_state = spread(combined(1 - core, mine, lead_mine))
    lead_other = swap(mine)
    probs, intra = pl.pallas_call(
        inside_kernel,
        grid=(heads,),
        in_specs=[whole((heads, tokens)), by_head, by_head, by_head],
        out_specs=[pl.BlockSpec((1, tokens, tokens), lambda h: (h, 0, 0)), by_head],
        out_shape=[shape((heads, tokens, tokens), BF16), shape((tokens, flat))],
        compiler_params=params(),
        name="inside",
    )(within, queries, keys, values)
    chip_mine = spread(scanned(chip_state, False)).reshape(states)
    chip_other = swap(chip_mine)
    attn, state, sums = pl.pallas_call(
        attn_kernel,
        grid_spec=grid_of(
            [whole((heads, tokens))] + [mine_first] * 4 + [whole(states)] * 2 + [whole(packed)] * 2,
            [
                mine_first,
                pl.BlockSpec(states, lambda s, c: (c[0] ^ s, 0, 0)),
                whole((8, 8, HEAD)),
            ],
            [pltpu.VMEM((tokens, HEAD), F32)] * 2,
        ),
        out_shape=[shape((tokens, flat)), shape((heads, HEAD, HEAD)), shape((8, 8, HEAD))],
        compiler_params=params(),
        name="attn",
    )(core, within, queries, intra, gate, out_grad, chip_mine, chip_other, lead_mine, lead_other)
    sums = lax.all_to_all(sums, "tp", split_axis=0, concat_axis=0, tiled=True)
    grad, theirs, mine, table = pl.pallas_call(
        grad_kernel,
        grid_spec=grid_of(
            [whole((8, 8, HEAD)), whole((heads, tokens))] + [other_first] * 4,
            [other_first, whole(packed), whole(packed), whole((8, HEAD))],
        ),
        out_shape=[shape((tokens, flat), BF16), shape(packed), shape(packed), shape((8, HEAD))],
        compiler_params=params(),
        name="grad",
    )(core, sums, within, queries, attn, gate, out_grad)
    lead_mine = swap(theirs)
    chip_state = spread(combined(core, mine, lead_mine))
    lead_other = swap(mine)
    query_grad, key_part, value_part = pl.pallas_call(
        back_kernel,
        grid=(heads,),
        in_specs=[whole((heads, tokens))]
        + [by_head] * 4
        + [
            pl.BlockSpec((1, tokens, tokens), lambda h: (h, 0, 0)),
            pl.BlockSpec((1, HEAD, HEAD), lambda h: (h, 0, 0)),
        ],
        out_specs=[by_head] * 3,
        out_shape=[shape((tokens, flat), BF16), shape((tokens, flat)), shape((tokens, flat))],
        compiler_params=params(),
        name="back",
    )(within, queries, keys, values, grad, probs, state)
    by_half = pl.BlockSpec((tokens, half), lambda s: (0, s))
    output, gate_grad = pl.pallas_call(
        gate_kernel,
        grid=(2,),
        in_specs=[whole((8, HEAD))] + [by_half] * 3,
        out_specs=[by_half] * 2,
        out_shape=[shape((tokens, flat), BF16)] * 2,
        compiler_params=params(),
        name="gate",
    )(table, attn, gate, out_grad)
    chip_mine = spread(scanned(chip_state, True)).reshape(states)
    chip_other = swap(chip_mine)
    key_grad, value_grad = pl.pallas_call(
        final_kernel,
        grid_spec=grid_of(
            [whole((heads, tokens))] + [mine_first] * 4 + [whole(states)] * 2 + [whole(packed)] * 2,
            [mine_first] * 2,
        ),
        out_shape=[shape((tokens, flat), BF16)] * 2,
        compiler_params=params(),
        name="final",
    )(core, within, keys, values, key_part, value_part, chip_mine, chip_other, lead_mine, lead_other)
    return output, query_grad, key_grad, value_grad, gate_grad


def solution(mesh):
    split = Mesh(mesh.devices.reshape(4, 4, 2, mesh.shape["tp"]), ("x", "y", "c", "tp"))
    return jax.shard_map(
        shards,
        mesh=split,
        in_specs=(P(SEQ, "tp"),) * 6,
        out_specs=(P(SEQ, "tp"),) * 5,
        check_vma=False,
    )
```

time: 251 us -> 124 us (0.49)
  waiting for transfers between devices: 122 us -> 12.6 us
  Pallas kernels: 0 us -> 32.4 us
  matrix products: 28.9 us -> 0 us
  other arithmetic: 25.7 us -> 0 us
  starting transfers between devices: 7.15 us -> 24.3 us
  between operations: 14.4 us -> 0.81 us
  blocking collectives: 35 us -> 38.9 us
    all_gather x6 -> x0, waiting for transfers between devices: 117 us -> none  [prefix_by_axis(): pieces = jax.tree.map(lambda part: lax.all_gather(part, axis), subtotal)]
    pallas_call x0 -> x11, Pallas kernels: none -> 32.4 us  [the longest x1 8.89 us: shards(): pl.pallas_call(back_kernel, grid=(heads,), in_specs=[whole((heads, tokens...]
    all_to_all x1 -> x3, blocking collectives: 8.98 us -> 38.9 us  [the longest x2 24.1 us: spread(): return lax.all_to_all(x, CHIPS, split_axis=0, concat_axis=0, tiled=True)]
    dot_general x12 -> x0, matrix products: 28.9 us -> none  [the longest x1 4.4 us: shards(): jnp.einsum('hts,thd->shd', probs, grad_h, preferred_element_type=jnp.floa...]
    all_gather x4 -> x0, blocking collectives: 26 us -> none  [prefix_by_axis(): pieces = jax.tree.map(lambda part: lax.all_gather(part, axis), subtotal)]
    add x6 -> x0, other arithmetic: 16.3 us -> none  [combine(): later[0][:, None, None] * earlier[1] + later[1]]
    ppermute x0 -> x6, starting transfers between devices: none -> 15.9 us  [swap(): return lax.ppermute(x, 'c', [(0, 1), (1, 0)])]
    all_to_all x1 -> x2, waiting for transfers between devices: 4.65 us -> 10.2 us  [spread(): return lax.all_to_all(x, CHIPS, split_axis=0, concat_axis=0, tiled=True)]
  transfers between devices with their start and end apart: 7 -> 8, of which waited for: 7 -> 4; matrix products, arithmetic and copies ran while one was open for 9% -> 0% of each run, Pallas kernels for 0% -> 13%
where the time goes in v1:
time: 124 us
  blocking collectives  38.9 us (31%)
  Pallas kernels  32.4 us (26%)
  starting transfers between devices  24.3 us (20%)
  local copies, waits for them, and re-layouts  14.5 us (12%)
  waiting for transfers between devices  12.6 us (10%)
    all_to_all x2, blocking collectives, spread(): return lax.all_to_all(x, CHIPS, split_axis=0, concat_axis=0, tiled=True)  24.1 us
    ppermute x6, starting transfers between devices, swap(): return lax.ppermute(x, 'c', [(0, 1), (1, 0)])  15.9 us
    all_to_all x1, blocking collectives, shards(): sums = lax.all_to_all(sums, 'tp', split_axis=0, concat_axis=0, tiled=True)  14.9 us
    unnamed x39, local copies, waits for them, and re-layouts  14.5 us
    all_to_all x2, waiting for transfers between devices, spread(): return lax.all_to_all(x, CHIPS, split_axis=0, concat_axis=0, tiled=True)  10.2 us
    pallas_call x1, Pallas kernels, shards(): pl.pallas_call(back_kernel, grid=(heads,), in_specs=[whole((heads, tokens...  8.89 us
    all_to_all x2, starting transfers between devices, spread(): return lax.all_to_all(x, CHIPS, split_axis=0, concat_axis=0, tiled=True)  8.4 us
    pallas_call x1, Pallas kernels, shards(): pl.pallas_call(inside_kernel, grid=(heads,), in_specs=[whole((heads, toke...  5.4 us
  transfers between devices with their start and end apart: 8, of which 4 were waited for; matrix products, arithmetic and copies ran while one was open for 0% of the time, Pallas kernels for 13%

profile of v1, /device:TPU:1, one launch (start us, length us, event | category | flops | bytes accessed | tf_op | source)
XLA Modules:
  0.0 123.5 jit_solution(8143464825418790410)
XLA Ops:
  3.9 2.3 %local.1 = (f32[8,512]{1,0:T(8,128)S(1)}, f32[4,136,128]{2,1,0:T(8,128)S(1)}, f32[4,136,128]{2,1,0:T(8,128)S(1)}) custom-call(s32[1]{0:T(128)} %bitcast.core_ref.lead_ref, f32[512,8]{1,0:T(8,128)S(1)} %copy.11.rate_ref, bf16[512,1024]{1,0:T(8,128)(2,1)S(1)} %copy-done.1, bf16[512,1024]{1,0:T(8,128)(2,1)S(1)} %copy-done.3), custom_call_target="tpu_custom_call" | custom-call | tf_op jit(solution)/shard_map/local/pallas_call | solution.py:374
  6.2 3.3 %collective-permute-start = (f32[4,136,128]{2,1,0:T(8,128)S(1)}, f32[4,136,128]{2,1,0:T(8,128)S(1)}, u32[]{:S(2)}, u32[]{:S(2)}) collective-permute-start(f32[4,136,128]{2,1,0:T(8,128)S(1)} %get-tuple-element.27), channel_id=1, source_target_pairs={{0,8},{8,0},{1,9},{9,1},{2,10},{10,2},{3,11},{11,3},{4,12},{12,4},... | collective-permute-start | bytes 835592 | tf_op jit(solution)/shard_map/ppermute | solution.py:322
  11.5 12.8 %all_to_all.25.i = f32[16,40,128]{2,1,0:T(8,128)} all-to-all(f32[16,40,128]{2,1,0:T(8,128)S(1)} %combine.2), channel_id=1, replica_groups=mesh['x'=4,'y'=4,'c'=2,'tp'=8] {'x','y'}, dimensions={0} | all-to-all | bytes 655360 | tf_op jit(solution)/shard_map/all_to_all | solution.py:326
  24.4 1.7 %scan.2 = f32[16,32,128]{2,1,0:T(8,128)} custom-call(f32[16,40,128]{2,1,0:T(8,128)} %all_to_all.25.i), custom_call_target="tpu_custom_call" | custom-call | tf_op jit(solution)/shard_map/scan/pallas_call | solution.py:368
  26.1 4.2 %all-to-all-start.1 = ((f32[16,32,128]{2,1,0:T(8,128)}), f32[16,32,128]{2,1,0:T(8,128)}, u32[]{:S(2)}, u32[]{:S(2)}) async-start(f32[16,32,128]{2,1,0:T(8,128)} %scan.2), calls=%async_computation.1 | async-start | bytes 524288 | tf_op jit(solution)/shard_map/all_to_all | solution.py:326
  30.3 2.3 %collective-permute-start.2 = (f32[4,136,128]{2,1,0:T(8,128)}, f32[4,136,128]{2,1,0:T(8,128)}, u32[]{:S(2)}, u32[]{:S(2)}) collective-permute-start(f32[4,136,128]{2,1,0:T(8,128)} %copy-done.18), channel_id=1, source_target_pairs={{0,8},{8,0},{1,9},{9,1},{2,10},{10,2},{3,11},{11,3},{4,12},{12,4},... | collective-permute-start | bytes 835592 | tf_op jit(solution)/shard_map/ppermute | solution.py:322
  32.6 5.1 %all-to-all-done.1 = f32[16,32,128]{2,1,0:T(8,128)} async-done(((f32[16,32,128]{2,1,0:T(8,128)}), f32[16,32,128]{2,1,0:T(8,128)}, u32[]{:S(2)}, u32[]{:S(2)}) %all-to-all-start.1) | async-done | bytes 262176 | tf_op jit(solution)/shard_map/all_to_all | solution.py:326
  37.7 3.3 %collective-permute-start.1 = (f32[4,128,128]{2,1,0:T(8,128)}, f32[4,128,128]{2,1,0:T(8,128)S(1)}, u32[]{:S(2)}, u32[]{:S(2)}) collective-permute-start(f32[4,128,128]{2,1,0:T(8,128)} %bitcast.1.chip_mine_ref), channel_id=1, source_target_pairs={{0,8},{8,0},{1,9},{9,1},{2,10},{10,2},{3,11},{11,3},{4,12},{12,4},... | collective-permute-start | bytes 786440 | tf_op jit(solution)/shard_map/ppermute | solution.py:322
  41.0 5.4 %inside.1 = (bf16[8,512,512]{2,1,0:T(8,128)(2,1)S(1)}, f32[512,1024]{1,0:T(8,128)S(1)}) custom-call(f32[8,512]{1,0:T(8,128)S(1)} %get-tuple-element.24.within_ref, bf16[512,1024]{1,0:T(8,128)(2,1)S(1)} %copy-done, bf16[512,1024]{1,0:T(8,128)(2,1)S(1)} %copy-done.2, bf16[512,1024]{1,0:T(8,128)(2,1)S(1)} %copy-done.4), custom_call_target="tpu_custom_call" | custom-call | tf_op jit(solution)/shard_map/inside/pallas_call | solution.py:387
  46.4 2.0 %copy-done.11 = bf16[8,512,512]{2,1,0:T(8,128)(2,1)} copy-done((bf16[8,512,512]{2,1,0:T(8,128)(2,1)}, bf16[8,512,512]{2,1,0:T(8,128)(2,1)S(1)}, u32[]{:S(2)}) %copy-start.11) | copy-done | bytes 4194328
  48.4 3.3 %attn.1 = (f32[512,1024]{1,0:T(8,128)S(1)}, f32[8,128,128]{2,1,0:T(8,128)S(1)}, f32[8,8,128]{2,1,0:T(8,128)S(1)}) custom-call(s32[1]{0:T(128)} %bitcast.core_ref.lead_ref, f32[8,512]{1,0:T(8,128)S(1)} %get-tuple-element.24.within_ref, bf16[512,1024]{1,0:T(8,128)(2,1)S(1)} %copy-done, f32[512,1024]{1,0:T(8,128)S(1)} %get-tuple-element.25.intra_ref, ...), custom_call_target="tpu_custom_call" | custom-call | tf_op jit(solution)/shard_map/attn/pallas_call | solution.py:398
  51.7 14.9 %all_to_all.26.sums_ref = f32[8,8,128]{2,1,0:T(8,128)S(1)} all-to-all(f32[8,8,128]{2,1,0:T(8,128)S(1)} %get-tuple-element.28), channel_id=1, replica_groups=mesh['x'=4,'y'=4,'c'=2,'tp'=8] {'tp'}, dimensions={0} | all-to-all | bytes 65536 | tf_op jit(solution)/shard_map/all_to_all | solution.py:413
  66.5 2.8 %grad.1 = (bf16[512,1024]{1,0:T(8,128)(2,1)S(1)}, f32[4,136,128]{2,1,0:T(8,128)S(1)}, f32[4,136,128]{2,1,0:T(8,128)S(1)}, f32[8,128]{1,0:T(8,128)S(1)}) custom-call(s32[1]{0:T(128)} %bitcast.core_ref.lead_ref, f32[8,8,128]{2,1,0:T(8,128)S(1)} %all_to_all.26.sums_ref, f32[8,512]{1,0:T(8,128)S(1)} %get-tuple-element.24.within_ref, ...), custom_call_target="tpu_custom_call" | custom-call | tf_op jit(solution)/shard_map/grad/pallas_call | solution.py:414
  70.3 1.5 %collective-permute-start.3 = (f32[4,136,128]{2,1,0:T(8,128)S(1)}, f32[4,136,128]{2,1,0:T(8,128)S(1)}, u32[]{:S(2)}, u32[]{:S(2)}) collective-permute-start(f32[4,136,128]{2,1,0:T(8,128)S(1)} %get-tuple-element.39), channel_id=1, source_target_pairs={{0,8},{8,0},{1,9},{9,1},{2,10},{10,2},{3,11},{11,3},{4,12},{12,4},... | collective-permute-start | bytes 835592 | tf_op jit(solution)/shard_map/ppermute | solution.py:322
  73.8 11.2 %all_to_all.27.i = f32[16,40,128]{2,1,0:T(8,128)} all-to-all(f32[16,40,128]{2,1,0:T(8,128)S(1)} %combine.3), channel_id=1, replica_groups=mesh['x'=4,'y'=4,'c'=2,'tp'=8] {'x','y'}, dimensions={0} | all-to-all | bytes 655360 | tf_op jit(solution)/shard_map/all_to_all | solution.py:326
  85.0 1.7 %scan.3 = f32[16,32,128]{2,1,0:T(8,128)} custom-call(f32[16,40,128]{2,1,0:T(8,128)} %all_to_all.27.i), custom_call_target="tpu_custom_call" | custom-call | tf_op jit(solution)/shard_map/scan/pallas_call | solution.py:368
  86.7 4.2 %all-to-all-start.4 = ((f32[16,32,128]{2,1,0:T(8,128)}), f32[16,32,128]{2,1,0:T(8,128)}, u32[]{:S(2)}, u32[]{:S(2)}) async-start(f32[16,32,128]{2,1,0:T(8,128)} %scan.3), calls=%async_computation.4 | async-start | bytes 524288 | tf_op jit(solution)/shard_map/all_to_all | solution.py:326
  90.9 2.3 %collective-permute-start.5 = (f32[4,136,128]{2,1,0:T(8,128)}, f32[4,136,128]{2,1,0:T(8,128)}, u32[]{:S(2)}, u32[]{:S(2)}) collective-permute-start(f32[4,136,128]{2,1,0:T(8,128)} %copy-done.17), channel_id=1, source_target_pairs={{0,8},{8,0},{1,9},{9,1},{2,10},{10,2},{3,11},{11,3},{4,12},{12,4},... | collective-permute-start | bytes 835592 | tf_op jit(solution)/shard_map/ppermute | solution.py:322
  93.2 5.1 %all-to-all-done.4 = f32[16,32,128]{2,1,0:T(8,128)} async-done(((f32[16,32,128]{2,1,0:T(8,128)}), f32[16,32,128]{2,1,0:T(8,128)}, u32[]{:S(2)}, u32[]{:S(2)}) %all-to-all-start.4) | async-done | bytes 262176 | tf_op jit(solution)/shard_map/all_to_all | solution.py:326
  98.3 3.3 %collective-permute-start.4 = (f32[4,128,128]{2,1,0:T(8,128)}, f32[4,128,128]{2,1,0:T(8,128)S(1)}, u32[]{:S(2)}, u32[]{:S(2)}) collective-permute-start(f32[4,128,128]{2,1,0:T(8,128)} %bitcast.2.chip_mine_ref), channel_id=1, source_target_pairs={{0,8},{8,0},{1,9},{9,1},{2,10},{10,2},{3,11},{11,3},{4,12},{12,4},... | collective-permute-start | bytes 786440 | tf_op jit(solution)/shard_map/ppermute | solution.py:322
  104.0 1.6 %copy-done.10 = f32[512,1024]{1,0:T(8,128)S(1)} copy-done((f32[512,1024]{1,0:T(8,128)S(1)}, f32[512,1024]{1,0:T(8,128)}, u32[]{:S(2)}) %copy-start.10) | copy-done | bytes 2097176
  105.6 2.3 %gate.1 = (bf16[512,1024]{1,0:T(8,128)(2,1)}, bf16[512,1024]{1,0:T(8,128)(2,1)}) custom-call(f32[8,128]{1,0:T(8,128)S(1)} %get-tuple-element.30.table_ref, f32[512,1024]{1,0:T(8,128)S(1)} %copy-done.10, bf16[512,1024]{1,0:T(8,128)(2,1)S(1)} %copy-done.6, bf16[512,1024]{1,0:T(8,128)(2,1)S(1)} %copy-done.8), custom_call_target="tpu_custom_call" | custom-call | tf_op jit(solution)/shard_map/gate/pallas_call | solution.py:442
  110.8 8.9 %back.1 = (bf16[512,1024]{1,0:T(8,128)(2,1)}, f32[512,1024]{1,0:T(8,128)S(1)}, f32[512,1024]{1,0:T(8,128)S(1)}) custom-call(f32[8,512]{1,0:T(8,128)S(1)} %get-tuple-element.24.within_ref, bf16[512,1024]{1,0:T(8,128)(2,1)S(1)} %copy-done, bf16[512,1024]{1,0:T(8,128)(2,1)S(1)} %copy-done.2, bf16[512,1024]{1,0:T(8,128)(2,1)S(1)} %copy-done.4, ...), custom_call_target="tpu_custom_call" | custom-call | tf_op jit(solution)/shard_map/back/pallas_call | solution.py:427
  119.7 3.8 %final.1 = (bf16[512,1024]{1,0:T(8,128)(2,1)}, bf16[512,1024]{1,0:T(8,128)(2,1)}) custom-call(s32[1]{0:T(128)} %bitcast.core_ref.lead_ref, f32[8,512]{1,0:T(8,128)S(1)} %get-tuple-element.24.within_ref, bf16[512,1024]{1,0:T(8,128)(2,1)S(1)} %copy-done.2, bf16[512,1024]{1,0:T(8,128)(2,1)S(1)} %copy-done.4, f32[512,1024]{1,0:T(8,128)S(1)} %get-tuple-element.36.key_part_ref, ...), custom_call_target="tpu_custom_call" | custom-call | tf_op jit(solution)/shard_map/final/pallas_call | solution.py:453
  (45 shorter events, 13.5 us)
Async XLA Ops:
  1.5 1.2 copy-start.1
  2.7 1.2 copy-start.3
  3.9 37.0 %copy-start = (bf16[512,1024]{1,0:T(8,128)(2,1)S(1)}, bf16[512,1024]{1,0:T(8,128)(2,1)}, u32[]{:S(2)}) copy-start(bf16[512,1024]{1,0:T(8,128)(2,1)} %q_ref.7) | copy-start | bytes 3145732
  3.9 37.0 %copy-start.2 = (bf16[512,1024]{1,0:T(8,128)(2,1)S(1)}, bf16[512,1024]{1,0:T(8,128)(2,1)}, u32[]{:S(2)}) copy-start(bf16[512,1024]{1,0:T(8,128)(2,1)} %k_ref.7) | copy-start | bytes 3145732
  3.9 37.0 %copy-start.4 = (bf16[512,1024]{1,0:T(8,128)(2,1)S(1)}, bf16[512,1024]{1,0:T(8,128)(2,1)}, u32[]{:S(2)}) copy-start(bf16[512,1024]{1,0:T(8,128)(2,1)} %v_ref.7) | copy-start | bytes 3145732
  6.2 4.5 %collective-permute-start = (f32[4,136,128]{2,1,0:T(8,128)S(1)}, f32[4,136,128]{2,1,0:T(8,128)S(1)}, u32[]{:S(2)}, u32[]{:S(2)}) collective-permute-start(f32[4,136,128]{2,1,0:T(8,128)S(1)} %get-tuple-element.27), channel_id=1, source_target_pairs={{0,8},{8,0},{1,9},{9,1},{2,10},{10,2},{3,11},{11,3},{4,12},{12,4},... | collective-permute-start | bytes 835592 | tf_op jit(solution)/shard_map/ppermute | solution.py:322
  26.1 11.6 %all-to-all-start.1 = ((f32[16,32,128]{2,1,0:T(8,128)}), f32[16,32,128]{2,1,0:T(8,128)}, u32[]{:S(2)}, u32[]{:S(2)}) async-start(f32[16,32,128]{2,1,0:T(8,128)} %scan.2), calls=%async_computation.1 | async-start | bytes 524288 | tf_op jit(solution)/shard_map/all_to_all | solution.py:326
  30.3 18.1 %collective-permute-start.2 = (f32[4,136,128]{2,1,0:T(8,128)}, f32[4,136,128]{2,1,0:T(8,128)}, u32[]{:S(2)}, u32[]{:S(2)}) collective-permute-start(f32[4,136,128]{2,1,0:T(8,128)} %copy-done.18), channel_id=1, source_target_pairs={{0,8},{8,0},{1,9},{9,1},{2,10},{10,2},{3,11},{11,3},{4,12},{12,4},... | collective-permute-start | bytes 835592 | tf_op jit(solution)/shard_map/ppermute | solution.py:322
  37.7 10.7 %copy-start.5 = (bf16[512,1024]{1,0:T(8,128)(2,1)S(1)}, bf16[512,1024]{1,0:T(8,128)(2,1)}, u32[]{:S(2)}) copy-start(bf16[512,1024]{1,0:T(8,128)(2,1)} %gate_ref.5) | copy-start | bytes 3145732
  37.7 10.7 %copy-start.7 = (bf16[512,1024]{1,0:T(8,128)(2,1)S(1)}, bf16[512,1024]{1,0:T(8,128)(2,1)}, u32[]{:S(2)}) copy-start(bf16[512,1024]{1,0:T(8,128)(2,1)} %up_ref.5) | copy-start | bytes 3145732
  37.7 10.7 %collective-permute-start.1 = (f32[4,128,128]{2,1,0:T(8,128)}, f32[4,128,128]{2,1,0:T(8,128)S(1)}, u32[]{:S(2)}, u32[]{:S(2)}) collective-permute-start(f32[4,128,128]{2,1,0:T(8,128)} %bitcast.1.chip_mine_ref), channel_id=1, source_target_pairs={{0,8},{8,0},{1,9},{9,1},{2,10},{10,2},{3,11},{11,3},{4,12},{12,4},... | collective-permute-start | bytes 786440 | tf_op jit(solution)/shard_map/ppermute | solution.py:322
  46.4 2.0 %copy-start.11 = (bf16[8,512,512]{2,1,0:T(8,128)(2,1)}, bf16[8,512,512]{2,1,0:T(8,128)(2,1)S(1)}, u32[]{:S(2)}) copy-start(bf16[8,512,512]{2,1,0:T(8,128)(2,1)S(1)} %get-tuple-element.33.probs_ref) | copy-start | bytes 12582916
  51.6 17.7 %copy-start.9 = (f32[512,1024]{1,0:T(8,128)}, f32[512,1024]{1,0:T(8,128)S(1)}, u32[]{:S(2)}) copy-start(f32[512,1024]{1,0:T(8,128)S(1)} %get-tuple-element.29.attn_ref) | copy-start | bytes 6291460
  51.6 17.7 %copy-start.15 = (f32[8,128,128]{2,1,0:T(8,128)}, f32[8,128,128]{2,1,0:T(8,128)S(1)}, u32[]{:S(2)}) copy-start(f32[8,128,128]{2,1,0:T(8,128)S(1)} %get-tuple-element.34.state_ref) | copy-start | bytes 1572868
  70.3 2.6 %collective-permute-start.3 = (f32[4,136,128]{2,1,0:T(8,128)S(1)}, f32[4,136,128]{2,1,0:T(8,128)S(1)}, u32[]{:S(2)}, u32[]{:S(2)}) collective-permute-start(f32[4,136,128]{2,1,0:T(8,128)S(1)} %get-tuple-element.39), channel_id=1, source_target_pairs={{0,8},{8,0},{1,9},{9,1},{2,10},{10,2},{3,11},{11,3},{4,12},{12,4},... | collective-permute-start | bytes 835592 | tf_op jit(solution)/shard_map/ppermute | solution.py:322
  86.7 11.6 %all-to-all-start.4 = ((f32[16,32,128]{2,1,0:T(8,128)}), f32[16,32,128]{2,1,0:T(8,128)}, u32[]{:S(2)}, u32[]{:S(2)}) async-start(f32[16,32,128]{2,1,0:T(8,128)} %scan.3), calls=%async_computation.4 | async-start | bytes 524288 | tf_op jit(solution)/shard_map/all_to_all | solution.py:326
  90.9 28.8 %collective-permute-start.5 = (f32[4,136,128]{2,1,0:T(8,128)}, f32[4,136,128]{2,1,0:T(8,128)}, u32[]{:S(2)}, u32[]{:S(2)}) collective-permute-start(f32[4,136,128]{2,1,0:T(8,128)} %copy-done.17), channel_id=1, source_target_pairs={{0,8},{8,0},{1,9},{9,1},{2,10},{10,2},{3,11},{11,3},{4,12},{12,4},... | collective-permute-start | bytes 835592 | tf_op jit(solution)/shard_map/ppermute | solution.py:322
  98.3 21.4 %collective-permute-start.4 = (f32[4,128,128]{2,1,0:T(8,128)}, f32[4,128,128]{2,1,0:T(8,128)S(1)}, u32[]{:S(2)}, u32[]{:S(2)}) collective-permute-start(f32[4,128,128]{2,1,0:T(8,128)} %bitcast.2.chip_mine_ref), channel_id=1, source_target_pairs={{0,8},{8,0},{1,9},{9,1},{2,10},{10,2},{3,11},{11,3},{4,12},{12,4},... | collective-permute-start | bytes 786440 | tf_op jit(solution)/shard_map/ppermute | solution.py:322
  101.5 1.2 copy-start.6
  102.8 1.2 copy-start.8
  104.0 1.6 %copy-start.10 = (f32[512,1024]{1,0:T(8,128)S(1)}, f32[512,1024]{1,0:T(8,128)}, u32[]{:S(2)}) copy-start(f32[512,1024]{1,0:T(8,128)} %copy-done.9) | copy-start | bytes 6291460
  105.6 2.9 %copy-start.12 = (bf16[8,512,512]{2,1,0:T(8,128)(2,1)S(1)}, bf16[8,512,512]{2,1,0:T(8,128)(2,1)}, u32[]{:S(2)}) copy-start(bf16[8,512,512]{2,1,0:T(8,128)(2,1)} %copy-done.11) | copy-start | bytes 12582916
  108.5 1.2 copy-start.14
  109.8 1.0 copy-start.16
  (3 other events, 2.4 us)

commit v2 on v0

v2 whole, which is shorter than its diff:
```python
import jax
import jax.numpy as jnp
from jax import lax
from jax.experimental import pallas as pl
from jax.experimental.pallas import tpu as pltpu
from jax.sharding import Mesh
from jax.sharding import PartitionSpec as P

HEAD_COUNT = 64
HEAD = 128
SEQ = ("x", "y", "c")
CHIPS = ("x", "y")
HIGH = lax.Precision.HIGHEST
F32 = jnp.float32
BF16 = jnp.bfloat16
PAD = 8

NN = (((1,), (0,)), ((), ()))
NT = (((1,), (1,)), ((), ()))
TN = (((0,), (0,)), ((), ()))


def dot(a, b, dims, precision=None):
    return lax.dot_general(a, b, dims, precision=precision, preferred_element_type=F32)


def halves(x):
    high = x.astype(BF16)
    return high, (x - high.astype(F32)).astype(BF16)


def as_column(row):
    return jnp.transpose(jnp.broadcast_to(row, (HEAD, row.shape[1])))


def sigmoid(x):
    return 1.0 / (1.0 + jnp.exp(-x))


def lanes(head, count=1):
    return pl.ds(pl.multiple_of(head * (count * HEAD), HEAD), count * HEAD)


def put_state(ref, i, state, factor):
    ref[i, 0:HEAD, :] = state
    ref[i, HEAD : HEAD + PAD, :] = jnp.broadcast_to(factor, (PAD, HEAD))


def outer_state(wide, narrow):
    both = dot(narrow, wide, TN)
    return both[:, :HEAD] + both[:, HEAD:]


def sum_kernel(rate_ref, within_ref):
    heads, tokens = rate_ref.shape
    early = lax.broadcasted_iota(jnp.int32, (tokens, tokens), 0)
    late = lax.broadcasted_iota(jnp.int32, (tokens, tokens), 1)
    upto = (early <= late).astype(F32).astype(BF16)
    rate = rate_ref[...]
    high, rest = halves(rate)
    low = (rate - high.astype(F32) - rest.astype(F32)).astype(BF16)
    parts = jnp.concatenate([x.astype(F32) for x in (high, rest, low)], axis=0).astype(BF16)
    sums = dot(parts, upto, NN)
    within_ref[...] = sums[0:heads] + sums[heads : 2 * heads] + sums[2 * heads :]


def local_part(first, step, within_ref, k_ref, v_ref, out_ref):
    count = k_ref.shape[1] // HEAD
    tokens = k_ref.shape[0]
    for i in range(count):
        within = within_ref[pl.ds(first + step * count + i, 1), :]
        last = within[:, tokens - 1 :]
        tail = as_column(jnp.exp(last - within))
        cols = slice(i * HEAD, (i + 1) * HEAD)
        scaled = jnp.concatenate(halves(k_ref[:, cols].astype(F32) * tail), axis=1)
        put_state(out_ref, step * count + i, outer_state(scaled, v_ref[:, cols]), jnp.exp(last))


def local_other_kernel(core_ref, rate_ref, k_ref, v_ref, within_ref, out_ref):
    step = pl.program_id(0)

    @pl.when(step == 0)
    def _():
        sum_kernel(rate_ref, within_ref)

    first = (1 - core_ref[0]) * out_ref.shape[0]
    local_part(first, step, within_ref, k_ref, v_ref, out_ref)


def copy_pair(step, count, from_ref, to_ref):
    for i in range(count):
        to_ref[i] = from_ref[step * count + i]


def local_mine_kernel(core_ref, within_ref, k_ref, v_ref, out_ref, copy_ref):
    first = core_ref[0] * out_ref.shape[0]
    step = pl.program_id(0)
    local_part(first, step, within_ref, k_ref, v_ref, out_ref)
    copy_pair(step, copy_ref.shape[0], out_ref, copy_ref)


def combine_kernel(lead_ref, mine_ref, other_ref, out_ref, copy_ref):
    copy_ref[...] = other_ref[...]
    lead = lead_ref[0] == 1
    group = mine_ref.shape[0]
    rows = HEAD // 4
    for i in range(group):
        own = mine_ref[i, HEAD : HEAD + PAD, :]
        far = other_ref[i, HEAD : HEAD + PAD, :]
        mine = mine_ref[i, 0:HEAD, :]
        other = other_ref[i, 0:HEAD, :]
        both = jnp.where(lead, far[0:1] * mine + other, own[0:1] * other + mine)
        for j in range(4):
            out_ref[4 * i + j, 0:rows, :] = both[j * rows : (j + 1) * rows]
            out_ref[4 * i + j, rows : rows + PAD, :] = own * far


def scan_kernel(reverse, in_ref, out_ref):
    chips, rows = out_ref.shape[0], out_ref.shape[1]
    state = jnp.zeros(out_ref.shape[1:], F32)
    for n in reversed(range(chips)) if reverse else range(chips):
        out_ref[n] = state
        state = in_ref[n, rows : rows + 1, :] * state + in_ref[n, 0:rows, :]


def decay_block(within, column, start, size, width):
    gap = jnp.concatenate([column[start : start + size]] * (width // HEAD), axis=1)
    gap = gap - within[:, :width]
    rows = start + lax.broadcasted_iota(jnp.int32, gap.shape, 0)
    cols = lax.broadcasted_iota(jnp.int32, gap.shape, 1)
    return jnp.where(rows >= cols, jnp.exp(jnp.minimum(gap, 0.0)), 0.0)


def inside_kernel(within_ref, q_ref, k_ref, v_ref, probs_ref, intra_ref):
    head = pl.program_id(0)
    within = within_ref[pl.ds(head, 1), :]
    column = as_column(within)
    tokens = q_ref.shape[0]
    size = tokens // 2
    for start in (0, size):
        width = start + size
        scores = dot(q_ref[start:width, :], k_ref[0:width, :], NT)
        probs = (scores * decay_block(within, column, start, size, width)).astype(BF16)
        probs_ref[0, start:width, 0:width] = probs
        intra_ref[start:width, :] = dot(probs, v_ref[0:width, :], NN)


def pick_state(follows, chip_ref, lead_ref, i):
    chip = chip_ref[i]
    return jnp.where(
        follows, lead_ref[i, HEAD : HEAD + 1, :] * chip + lead_ref[i, 0:HEAD, :], chip
    )


def attn_part(core_ref, head, own, at, within_ref, q_ref, gate_ref, up_ref, intra_ref, chip_ref, lead_ref, outs):
    attn_ref, dnorm_ref, grown_ref, state_ref = outs
    state = pick_state(core_ref[0] == 1, chip_ref, lead_ref, own)
    state_ref[head] = state
    high, low = halves(state)
    grown = q_ref[:, at].astype(F32) * as_column(jnp.exp(within_ref[pl.ds(head, 1), :]))
    grown = jnp.concatenate(halves(grown), axis=1)
    grown_ref[:, lanes(head, 2)] = grown
    attn = intra_ref[:, at] + dot(
        jnp.concatenate([grown, grown[:, :HEAD]], axis=1),
        jnp.concatenate([high, high, low], axis=1),
        NT,
    )
    attn_ref[:, lanes(head)] = attn
    dnorm = up_ref[:, at].astype(F32) * sigmoid(gate_ref[:, at].astype(F32))
    dnorm_ref[:, lanes(head)] = dnorm
    return attn * attn, dnorm * attn


def fetches(core_ref, sources, targets, sems):
    half = targets[0].shape[1]
    cols = pl.ds(pl.multiple_of((1 - core_ref[0]) * half, HEAD), half)
    return [
        pltpu.make_async_copy(source.at[:, cols], target, sems.at[i])
        for i, (source, target) in enumerate(zip(sources, targets))
    ]


def attn_mine_kernel(
    core_ref, within_ref, q_ref, gate_ref, up_ref, intra_ref, chip_ref, lead_ref,
    q_hbm, gate_hbm, up_hbm, intra_hbm,
    attn_ref, dnorm_ref, grown_ref, state_ref, square_ref, inner_ref,
    q_far, gate_far, up_far, intra_far, sems,
):
    step = pl.program_id(0)
    count = q_ref.shape[1] // HEAD
    copies = fetches(
        core_ref, (q_hbm, gate_hbm, up_hbm, intra_hbm), (q_far, gate_far, up_far, intra_far), sems
    )

    @pl.when(step == 0)
    def _():
        for copy in copies:
            copy.start()
        square_ref[...] = jnp.zeros_like(square_ref)
        inner_ref[...] = jnp.zeros_like(inner_ref)

    for i in range(count):
        own = step * count + i
        square, inner = attn_part(
            core_ref, core_ref[0] * chip_ref.shape[0] + own, own, slice(i * HEAD, (i + 1) * HEAD),
            within_ref, q_ref, gate_ref, up_ref, intra_ref, chip_ref, lead_ref,
            (attn_ref, dnorm_ref, grown_ref, state_ref),
        )
        square_ref[...] += square
        inner_ref[...] += inner

    @pl.when(step == pl.num_programs(0) - 1)
    def _():
        for copy in copies:
            copy.wait()


def attn_other_kernel(
    core_ref, within_ref, q_ref, gate_ref, up_ref, intra_ref, chip_ref, lead_ref,
    square_ref, inner_ref, attn_in, dnorm_in, grown_in, state_in,
    attn_ref, dnorm_ref, grown_ref, state_ref, sums_ref,
):
    total_square, total_inner = square_ref[...], inner_ref[...]
    for i in range(chip_ref.shape[0]):
        square, inner = attn_part(
            core_ref, (1 - core_ref[0]) * chip_ref.shape[0] + i, i, slice(i * HEAD, (i + 1) * HEAD),
            within_ref, q_ref, gate_ref, up_ref, intra_ref, chip_ref, lead_ref,
            (attn_ref, dnorm_ref, grown_ref, state_ref),
        )
        total_square = total_square + square
        total_inner = total_inner + inner
    ones = jnp.ones((8, HEAD), F32)
    square = dot(ones, total_square, NT, HIGH)
    inner = dot(ones, total_inner, NT, HIGH)
    rows = lax.broadcasted_iota(jnp.int32, (8, HEAD), 0)
    packed = jnp.zeros((8, HEAD), F32)
    for i in range(4):
        cols = slice(i * HEAD, (i + 1) * HEAD)
        packed = jnp.where(rows == i, square[:, cols], packed)
        packed = jnp.where(rows == i + 4, inner[:, cols], packed)
    sums_ref[...] = jnp.broadcast_to(packed[None], sums_ref.shape)


def grad_part(half, grown_ref, attn_ref, dnorm_ref, within_ref, scale_ref, center_ref, grad_ref, out_ref):
    step = pl.program_id(0)
    tokens = attn_ref.shape[0]
    count = grad_ref.shape[1] // HEAD
    for i in range(count):
        own = step * count + i
        head = half * out_ref.shape[0] + own
        scale = scale_ref[...]
        normed = attn_ref[:, lanes(head)] * scale
        grad = (scale * (dnorm_ref[:, lanes(head)] - normed * center_ref[...])).astype(BF16)
        grad_ref[:, i * HEAD : (i + 1) * HEAD] = grad
        last = within_ref[pl.ds(head, 1), :][:, tokens - 1 :]
        put_state(out_ref, own, outer_state(grown_ref[:, lanes(head, 2)], grad), jnp.exp(last))


def grad_other_kernel(
    core_ref, sums_ref, within_ref, grown_ref, attn_ref, dnorm_ref,
    grad_ref, out_ref, scale_ref, center_ref, table_ref,
):
    @pl.when(pl.program_id(0) == 0)
    def _():
        total = jnp.sum(sums_ref[...], axis=0) / (HEAD_COUNT * HEAD)
        scale = lax.rsqrt(total[0:4] + 1e-06)
        center = scale * total[4:8]
        table_ref[0:4] = scale
        table_ref[4:8] = center
        for i in range(4):
            rows = slice(i * HEAD, (i + 1) * HEAD)
            scale_ref[rows] = as_column(scale[i : i + 1])
            center_ref[rows] = as_column(center[i : i + 1])

    grad_part(
        1 - core_ref[0], grown_ref, attn_ref, dnorm_ref, within_ref, scale_ref, center_ref,
        grad_ref, out_ref,
    )


def grad_mine_kernel(
    core_ref, scale_ref, center_ref, within_ref, grown_ref, attn_ref, dnorm_ref, grad_in_ref,
    grad_ref, out_ref, copy_ref,
):
    grad_part(
        core_ref[0], grown_ref, attn_ref, dnorm_ref, within_ref, scale_ref, center_ref,
        grad_ref, out_ref,
    )
    copy_pair(pl.program_id(0), copy_ref.shape[0], out_ref, copy_ref)


def gate_kernel(table_ref, attn_ref, gate_ref, up_ref, output_ref, gate_grad_ref):
    table = table_ref[...]
    scale = jnp.concatenate([as_column(table[i : i + 1]) for i in range(4)], axis=0)
    count = gate_ref.shape[1] // HEAD
    for i in range(count):
        cols = slice(i * HEAD, (i + 1) * HEAD)
        normed = attn_ref[:, cols] * scale
        sig = sigmoid(gate_ref[:, cols].astype(F32))
        output_ref[:, cols] = (normed * sig).astype(BF16)
        gate_grad_ref[:, cols] = (
            up_ref[:, cols].astype(F32) * normed * sig * (1.0 - sig)
        ).astype(BF16)


def back_kernel(within_ref, q_ref, k_ref, v_ref, grad_ref, state_ref, query_grad_ref, key_ref):
    head = pl.program_id(0)
    within = within_ref[pl.ds(head, 1), :]
    column = as_column(within)
    grow = jnp.exp(column)
    tokens = q_ref.shape[0]
    size = tokens // 2
    state = jnp.concatenate(halves(state_ref[0]), axis=0)
    for start in (0, size):
        width = start + size
        grad = grad_ref[start:width, :]
        pgrad = dot(grad, v_ref[0:width, :], NT)
        pgrad = (pgrad * decay_block(within, column, start, size, width)).astype(BF16)
        inter = dot(jnp.concatenate([grad, grad], axis=1), state, NN)
        query_grad_ref[start:width, :] = (
            dot(pgrad, k_ref[0:width, :], NN) + grow[start:width] * inter
        ).astype(BF16)
        key_part = dot(pgrad, q_ref[start:width, :], TN)
        if start == 0:
            key_ref[0:width, :] = key_part
        else:
            key_ref[0:start, :] += key_part[0:start]
            key_ref[start:width, :] = key_part[start:width]


def value_kernel(grad_ref, probs_ref, value_ref):
    tokens = grad_ref.shape[0]
    size = tokens // 2
    late = dot(probs_ref[0, size:tokens, :], grad_ref[size:tokens, :], TN)
    early = dot(probs_ref[0, 0:size, 0:size], grad_ref[0:size, :], TN)
    value_ref[0:size, :] = late[0:size] + early
    value_ref[size:tokens, :] = late[size:tokens]


def final_part(
    core_ref, head, own, at, within_ref, k_ref, v_ref, key_part_ref, value_part_ref,
    chip_ref, lead_ref, key_grad_ref, value_grad_ref, to,
):
    tokens = k_ref.shape[0]
    state = halves(pick_state(core_ref[0] == 0, chip_ref, lead_ref, own))
    within = within_ref[pl.ds(head, 1), :]
    tail = as_column(jnp.exp(within[:, tokens - 1 :] - within))
    k, v = k_ref[:, at], v_ref[:, at]
    key_inter = dot(jnp.concatenate([v, v], axis=1), jnp.concatenate(state, axis=0), NN)
    value_inter = dot(jnp.concatenate([k, k], axis=1), jnp.concatenate(state, axis=1), NT)
    key_grad_ref[:, to] = (key_part_ref[:, at] + tail * key_inter).astype(BF16)
    value_grad_ref[:, to] = (value_part_ref[:, at] + tail * value_inter).astype(BF16)


def final_mine_kernel(
    core_ref, within_ref, k_ref, v_ref, key_part_ref, value_part_ref, chip_ref, lead_ref,
    k_hbm, v_hbm, key_part_hbm, value_part_hbm,
    key_grad_ref, value_grad_ref, k_far, v_far, key_part_far, value_part_far, sems,
):
    step = pl.program_id(0)
    count = k_ref.shape[1] // HEAD
    copies = fetches(
        core_ref, (k_hbm, v_hbm, key_part_hbm, value_part_hbm),
        (k_far, v_far, key_part_far, value_part_far), sems,
    )

    @pl.when(step == 0)
    def _():
        for copy in copies:
            copy.start()

    for i in range(count):
        own = step * count + i
        cols = slice(i * HEAD, (i + 1) * HEAD)
        final_part(
            core_ref, core_ref[0] * chip_ref.shape[0] + own, own, cols, within_ref, k_ref, v_ref,
            key_part_ref, value_part_ref, chip_ref, lead_ref, key_grad_ref, value_grad_ref, cols,
        )

    @pl.when(step == pl.num_programs(0) - 1)
    def _():
        for copy in copies:
            copy.wait()


def final_other_kernel(
    core_ref, within_ref, k_ref, v_ref, key_part_ref, value_part_ref, chip_ref, lead_ref,
    key_grad_in, value_grad_in, key_grad_ref, value_grad_ref,
):
    step = pl.program_id(0)
    count = key_grad_ref.shape[1] // HEAD
    for i in range(count):
        own = step * count + i
        final_part(
            core_ref, (1 - core_ref[0]) * chip_ref.shape[0] + own, own, lanes(own), within_ref,
            k_ref, v_ref, key_part_ref, value_part_ref, chip_ref, lead_ref,
            key_grad_ref, value_grad_ref, slice(i * HEAD, (i + 1) * HEAD),
        )


def shape(dims, dtype=F32):
    return jax.ShapeDtypeStruct(dims, dtype)


def swap(x):
    return lax.ppermute(x, "c", [(0, 1), (1, 0)])


def spread(x):
    return lax.all_to_all(x, CHIPS, split_axis=0, concat_axis=0, tiled=True)


VMEM = pl.BlockSpec(memory_space=pltpu.VMEM)
HBM = pl.BlockSpec(memory_space=pl.ANY)


def call(kernel, name, grid, inputs, outputs, core=None, aliases=(), scratch=(), mib=12):
    def place(x, spec):
        return x if spec is VMEM else pltpu.with_memory_space_constraint(x, pltpu.HBM)

    scalars = () if core is None else (core,)
    return pl.pallas_call(
        kernel,
        grid_spec=pltpu.PrefetchScalarGridSpec(
            num_scalar_prefetch=len(scalars),
            grid=grid,
            in_specs=[spec for _, spec in inputs],
            out_specs=[spec for _, spec in outputs],
            scratch_shapes=list(scratch),
        ),
        out_shape=[
            (pltpu.VMEM if spec is VMEM else pltpu.HBM)(x.shape, x.dtype) for x, spec in outputs
        ],
        input_output_aliases=dict(aliases),
        compiler_params=pltpu.CompilerParams(
            dimension_semantics=("arbitrary",) * len(grid), vmem_limit_bytes=mib * 2**20
        ),
        name=name,
    )(*scalars, *(place(x, spec) for x, spec in inputs))


def shards(queries, keys, values, gate, log_decay, out_grad):
    tokens, flat = queries.shape
    heads = log_decay.shape[1]
    group = heads // 2
    chips = lax.axis_size("x") * lax.axis_size("y")
    rows = group * HEAD // chips
    core = lax.axis_index("c").astype(jnp.int32).reshape(1)
    packed = shape((group, HEAD + PAD, HEAD))
    states = shape((group, HEAD, HEAD))
    sliced = shape((chips, rows, HEAD))
    wide = shape((tokens, flat))
    narrow = shape((tokens, flat), BF16)
    column = shape((tokens, HEAD))

    half = shape((tokens, flat // 2))
    half_narrow = shape((tokens, flat // 2), BF16)
    full = shape((heads, HEAD, HEAD))

    by_head = pl.BlockSpec((tokens, HEAD), lambda h: (0, h))
    by_pair = pl.BlockSpec((tokens, 2 * HEAD), lambda s: (0, s))
    state_by_head = pl.BlockSpec((1, HEAD, HEAD), lambda h: (h, 0, 0))
    probs_by_head = pl.BlockSpec((1, tokens, tokens), lambda h: (h, 0, 0))
    pairs = group // 2
    mine_pair = pl.BlockSpec((tokens, 2 * HEAD), lambda s, c: (0, c[0] * pairs + s))
    other_pair = pl.BlockSpec((tokens, 2 * HEAD), lambda s, c: (0, (1 - c[0]) * pairs + s))
    packed_pair = pl.BlockSpec((2, HEAD + PAD, HEAD), lambda s, c: (s, 0, 0))

    def in_vmem(*xs):
        return [(x, VMEM) for x in xs]

    def in_hbm(*xs):
        return [(x, pl.BlockSpec(x.shape, lambda *_: (0,) * len(x.shape))) for x in xs]

    def combined(lead, mine, other):
        return call(
            combine_kernel, "combine", (1,), in_vmem(mine, other),
            in_hbm(shape((chips, rows + PAD, HEAD)), packed), lead,
        )

    def scanned(x, reverse):
        return call(
            lambda i, o: scan_kernel(reverse, i, o), "scan", (1,), in_vmem(x), in_hbm(sliced)
        )[0]

    within, theirs = call(
        local_other_kernel, "local_other", (pairs,),
        [(log_decay.T, VMEM), (keys, other_pair), (values, other_pair)],
        in_vmem(shape((heads, tokens)), packed), core,
    )
    lead_mine = swap(theirs)
    mine, mine_copy = call(
        local_mine_kernel, "local_mine", (pairs,),
        [(within, VMEM), (keys, mine_pair), (values, mine_pair)],
        in_vmem(packed) + [(packed, packed_pair)], core,
    )
    chip_state, lead_mine = combined(1 - core, mine, lead_mine)
    chip_state = spread(chip_state)
    probs, intra = call(
        inside_kernel, "inside", (heads,),
        in_hbm(within) + [(queries, by_head), (keys, by_head), (values, by_head)],
        [(shape((heads, tokens, tokens), BF16), probs_by_head), (wide, by_head)],
    )
    chip_state, probs, intra, mine_copy = lax.optimization_barrier(
        (chip_state, probs, intra, mine_copy)
    )
    chip_mine = spread(scanned(chip_state, False))
    lead_other = swap(mine_copy)
    chip_mine, lead_other, intra, within = lax.optimization_barrier(
        (chip_mine, lead_other, intra, within)
    )
    chip_mine = chip_mine.reshape(states.shape)
    chip_other = swap(chip_mine)
    attn, dnorm, grown, state, square, inner, *far = call(
        attn_mine_kernel, "attn_mine", (pairs,),
        in_hbm(within)
        + [(queries, mine_pair), (gate, mine_pair), (out_grad, mine_pair), (intra, mine_pair)]
        + in_vmem(chip_mine) + in_hbm(lead_mine)
        + [(queries, HBM), (gate, HBM), (out_grad, HBM), (intra, HBM)],
        in_vmem(
            wide, wide, shape((tokens, 2 * flat), BF16), full, column, column,
            half_narrow, half_narrow, half_narrow, half,
        ),
        core, scratch=[pltpu.SemaphoreType.DMA((4,))],
    )
    attn, dnorm, grown, state, sums = call(
        attn_other_kernel, "attn_other", (1,),
        in_hbm(within) + in_vmem(*far, chip_other, lead_other)
        + in_vmem(square, inner, attn, dnorm, grown, state),
        in_vmem(wide, wide, shape((tokens, 2 * flat), BF16), full, shape((8, 8, HEAD))),
        core, {10: 0, 11: 1, 12: 2, 13: 3},
    )
    sums = lax.all_to_all(sums, "tp", split_axis=0, concat_axis=0, tiled=True)
    grad, theirs, scale, center, table = call(
        grad_other_kernel, "grad_other", (pairs,),
        in_vmem(sums) + in_hbm(within) + in_vmem(grown, attn, dnorm),
        [(narrow, other_pair)] + in_vmem(packed, column, column) + in_hbm(shape((8, HEAD))), core,
    )
    lead_mine = swap(theirs)
    grad, mine, mine_copy = call(
        grad_mine_kernel, "grad_mine", (pairs,),
        in_vmem(scale, center) + in_hbm(within) + in_vmem(grown, attn, dnorm) + [(grad, HBM)],
        [(narrow, mine_pair)] + in_vmem(packed) + [(packed, packed_pair)], core, {7: 0},
    )
    chip_state, lead_mine = combined(core, mine, lead_mine)
    chip_state = spread(chip_state)
    query_grad, key_part = call(
        back_kernel, "back", (heads,),
        in_hbm(within)
        + [(queries, by_head), (keys, by_head), (values, by_head), (grad, by_head), (state, state_by_head)],
        [(narrow, by_head), (wide, by_head)],
    )
    chip_state, key_part, mine_copy, grad, table = lax.optimization_barrier(
        (chip_state, key_part, mine_copy, grad, table)
    )
    chip_mine = spread(scanned(chip_state, True))
    lead_other = swap(mine_copy)
    (value_part,) = call(
        value_kernel, "value", (heads,), [(grad, by_head), (probs, probs_by_head)],
        [(wide, by_head)],
    )
    output, gate_grad = call(
        gate_kernel, "gate", (heads // 2,),
        in_hbm(table) + [(attn, by_pair), (gate, by_pair), (out_grad, by_pair)],
        [(narrow, by_pair)] * 2,
    )
    chip_mine, value_part, output, gate_grad, lead_other = lax.optimization_barrier(
        (chip_mine, value_part, output, gate_grad, lead_other)
    )
    chip_mine = chip_mine.reshape(states.shape)
    chip_other = swap(chip_mine)
    key_grad, value_grad, *far = call(
        final_mine_kernel, "final_mine", (pairs,),
        in_hbm(within)
        + [(keys, mine_pair), (values, mine_pair), (key_part, mine_pair), (value_part, mine_pair)]
        + in_vmem(chip_mine) + in_hbm(lead_mine)
        + [(keys, HBM), (values, HBM), (key_part, HBM), (value_part, HBM)],
        [(narrow, mine_pair)] * 2 + in_vmem(half_narrow, half_narrow, half, half),
        core, scratch=[pltpu.SemaphoreType.DMA((4,))],
    )
    key_grad, value_grad = call(
        final_other_kernel, "final_other", (pairs,),
        in_hbm(within) + in_vmem(*far, chip_other, lead_other)
        + [(key_grad, HBM), (value_grad, HBM)],
        [(narrow, other_pair)] * 2, core, {8: 0, 9: 1},
    )
    return output, query_grad, key_grad, value_grad, gate_grad


def solution(mesh):
    split = Mesh(mesh.devices.reshape(4, 4, 2, mesh.shape["tp"]), ("x", "y", "c", "tp"))
    return jax.shard_map(
        shards,
        mesh=split,
        in_specs=(P(SEQ, "tp"),) * 6,
        out_specs=(P(SEQ, "tp"),) * 5,
        check_vma=False,
    )
```

time: 251 us -> 111 us (0.44)
  waiting for transfers between devices: 122 us -> 0.02 us
  Pallas kernels: 0 us -> 55.2 us
  matrix products: 28.9 us -> 0 us
  other arithmetic: 25.7 us -> 0 us
  starting transfers between devices: 7.15 us -> 24.3 us
  local copies, waits for them, and re-layouts: 16.9 us -> 0.73 us
  between operations: 14.4 us -> 0.77 us
  blocking collectives: 35 us -> 28.3 us
    all_gather x6 -> x0, waiting for transfers between devices: 117 us -> none  [prefix_by_axis(): pieces = jax.tree.map(lambda part: lax.all_gather(part, axis), subtotal)]
    pallas_call x0 -> x16, Pallas kernels: none -> 55.2 us  [call(): pl.pallas_call(kernel, grid_spec=pltpu.PrefetchScalarGridSpec(num_scalar_...]
    dot_general x12 -> x0, matrix products: 28.9 us -> none  [the longest x1 4.4 us: shards(): jnp.einsum('hts,thd->shd', probs, grad_h, preferred_element_type=jnp.floa...]
    all_gather x4 -> x0, blocking collectives: 26 us -> none  [prefix_by_axis(): pieces = jax.tree.map(lambda part: lax.all_gather(part, axis), subtotal)]
    all_to_all x1 -> x2, blocking collectives: 8.98 us -> 28.3 us  [the longest x1 14.9 us: shards(): sums = lax.all_to_all(sums, 'tp', split_axis=0, concat_axis=0, tiled=True)]
    add x6 -> x0, other arithmetic: 16.3 us -> none  [combine(): later[0][:, None, None] * earlier[1] + later[1]]
    unnamed x39 -> x12, local copies, waits for them, and re-layouts: 12.4 us -> 0.73 us
    ppermute x0 -> x6, starting transfers between devices: none -> 9.36 us  [swap(): return lax.ppermute(x, 'c', [(0, 1), (1, 0)])]
  transfers between devices with their start and end apart: 7 -> 9, of which waited for: 7 -> 0; matrix products, arithmetic and copies ran while one was open for 9% -> 0% of each run, Pallas kernels for 0% -> 40%
where the time goes in v2:
time: 111 us; the launch traced here: 109 us
  Pallas kernels  55.2 us (50%)
  blocking collectives  28.3 us (25%)
  starting transfers between devices  24.3 us (22%)
    pallas_call x16, Pallas kernels, call(): pl.pallas_call(kernel, grid_spec=pltpu.PrefetchScalarGridSpec(num_scalar_...  55.2 us
    all_to_all x3, starting transfers between devices, spread(): return lax.all_to_all(x, CHIPS, split_axis=0, concat_axis=0, tiled=True)  14.9 us
    all_to_all x1, blocking collectives, shards(): sums = lax.all_to_all(sums, 'tp', split_axis=0, concat_axis=0, tiled=True)  14.9 us
    all_to_all x1, blocking collectives, spread(): return lax.all_to_all(x, CHIPS, split_axis=0, concat_axis=0, tiled=True)  13.4 us
    ppermute x6, starting transfers between devices, swap(): return lax.ppermute(x, 'c', [(0, 1), (1, 0)])  9.36 us
  transfers between devices with their start and end apart: 9, of which 0 were waited for; matrix products, arithmetic and copies ran while one was open for 0% of the time, Pallas kernels for 40%

profile of v2, /device:TPU:1, one launch (start us, length us, event | category | flops | bytes accessed | tf_op | source)
XLA Modules:
  0.0 109.3 jit_solution(617693043556767687)
XLA Ops:
  1.4 2.3 %local_other.1 = (f32[8,512]{1,0:T(8,128)S(1)}, f32[4,136,128]{2,1,0:T(8,128)S(1)}) custom-call(s32[1]{0:T(128)} %bitcast.core_ref.lead_ref, f32[8,512]{1,0:T(8,128)S(1)} %bitcast.8, bf16[512,1024]{1,0:T(8,128)(2,1)} %k_hbm.1, bf16[512,1024]{1,0:T(8,128)(2,1)} %v_hbm.1), custom_call_target="tpu_custom_call" | custom-call | tf_op jit(solution)/shard_map/local_other/pallas_call | solution.py:422
  3.7 3.3 %collective-permute-start = (f32[4,136,128]{2,1,0:T(8,128)S(1)}, f32[4,136,128]{2,1,0:T(8,128)S(1)}, u32[]{:S(2)}, u32[]{:S(2)}) collective-permute-start(f32[4,136,128]{2,1,0:T(8,128)S(1)} %get-tuple-element.70), channel_id=1, source_target_pairs={{0,8},{8,0},{1,9},{9,1},{2,10},{10,2},{3,11},{11,3},{4,12},{12,4},... | collective-permute-start | bytes 835592 | tf_op jit(solution)/shard_map/ppermute | solution.py:406
  7.0 2.8 %local_mine.1 = (f32[4,136,128]{2,1,0:T(8,128)S(1)}, f32[4,136,128]{2,1,0:T(8,128)}) custom-call(s32[1]{0:T(128)} %bitcast.core_ref.lead_ref, f32[8,512]{1,0:T(8,128)S(1)} %get-tuple-element.78.within_ref, bf16[512,1024]{1,0:T(8,128)(2,1)} %k_hbm.1, bf16[512,1024]{1,0:T(8,128)(2,1)} %v_hbm.1), custom_call_target="tpu_custom_call" | custom-call | tf_op jit(solution)/shard_map/local_mine/pallas_call | solution.py:422
  9.8 0.9 combine.2
  10.7 5.0 %all-to-all-start = ((f32[16,40,128]{2,1,0:T(8,128)}), f32[16,40,128]{2,1,0:T(8,128)S(1)}, u32[]{:S(2)}, u32[]{:S(2)}) async-start(f32[16,40,128]{2,1,0:T(8,128)} %get-tuple-element.71), calls=%async_computation | async-start | bytes 655360 | tf_op jit(solution)/shard_map/all_to_all | solution.py:410
  15.7 8.4 %inside.1 = (bf16[8,512,512]{2,1,0:T(8,128)(2,1)}, f32[512,1024]{1,0:T(8,128)}) custom-call(f32[8,512]{1,0:T(8,128)} %copy-done.2, bf16[512,1024]{1,0:T(8,128)(2,1)} %q_ref.5, bf16[512,1024]{1,0:T(8,128)(2,1)} %k_hbm.1, bf16[512,1024]{1,0:T(8,128)(2,1)} %v_hbm.1), custom_call_target="tpu_custom_call" | custom-call | tf_op jit(solution)/shard_map/inside/pallas_call | solution.py:422
  24.1 1.7 %collective-permute-start.1 = (f32[4,136,128]{2,1,0:T(8,128)S(1)}, f32[4,136,128]{2,1,0:T(8,128)S(1)}, u32[]{:S(2)}, u32[]{:S(2)}) collective-permute-start(f32[4,136,128]{2,1,0:T(8,128)S(1)} %copy-done.5), channel_id=1, source_target_pairs={{0,8},{8,0},{1,9},{9,1},{2,10},{10,2},{3,11},{11,3},{4,12},{12,4},... | collective-permute-start | bytes 835592 | tf_op jit(solution)/shard_map/ppermute | solution.py:406
  26.6 13.4 %all_to_all.25 = f32[16,32,128]{2,1,0:T(8,128)S(1)} all-to-all(f32[16,32,128]{2,1,0:T(8,128)} %scan.2), channel_id=1, replica_groups=mesh['x'=4,'y'=4,'c'=2,'tp'=8] {'x','y'}, dimensions={0} | all-to-all | bytes 524288 | tf_op jit(solution)/shard_map/all_to_all | solution.py:410
  40.0 1.6 %collective-permute-start.2 = (f32[4,128,128]{2,1,0:T(8,128)S(1)}, f32[4,128,128]{2,1,0:T(8,128)S(1)}, u32[]{:S(2)}, u32[]{:S(2)}) collective-permute-start(f32[4,128,128]{2,1,0:T(8,128)S(1)} %bitcast.6), channel_id=1, source_target_pairs={{0,8},{8,0},{1,9},{9,1},{2,10},{10,2},{3,11},{11,3},{4,12},{12,4},... | collective-permute-start | bytes 786440 | tf_op jit(solution)/shard_map/ppermute | solution.py:406
  41.6 3.3 %attn_mine.1 = (f32[512,1024]{1,0:T(8,128)S(1)}, f32[512,1024]{1,0:T(8,128)S(1)}, bf16[512,2048]{1,0:T(8,128)(2,1)S(1)}, f32[8,128,128]{2,1,0:T(8,128)S(1)}, f32...) custom-call(s32[1]{0:T(128)} %bitcast.core_ref.lead_ref, ...), custom_call_target="tpu_custom_call" | custom-call | tf_op jit(solution)/shard_map/attn_mine/pallas_call | solution.py:422
  44.9 2.1 %attn_other.1 = (f32[512,1024]{1,0:T(8,128)S(1)}, f32[512,1024]{1,0:T(8,128)S(1)}, bf16[512,2048]{1,0:T(8,128)(2,1)S(1)}, f32[8,128,128]{2,1,0:T(8,128)S(1)}, f32[8,8,128]{2,1,0:T(8,128)S(1)}) custom-call(s32[1]{0:T(128)} %bitcast.core_ref.lead_ref, f32[8,512]{1,0:T(8,128)} %copy-done.2, ...), custom_call_target="tpu_custom_call", output_to_operand_aliasing={{0}: (10, {}), {1}: (11, {}), {2}: (12, {}), {3}: (13, {})} | custom-call | tf_op jit(solution)/shard_map/attn_other/pallas_call | solution.py:422
  47.1 14.9 %all_to_all.26.sums_ref = f32[8,8,128]{2,1,0:T(8,128)S(1)} all-to-all(f32[8,8,128]{2,1,0:T(8,128)S(1)} %get-tuple-element.93), channel_id=1, replica_groups=mesh['x'=4,'y'=4,'c'=2,'tp'=8] {'tp'}, dimensions={0} | all-to-all | bytes 65536 | tf_op jit(solution)/shard_map/all_to_all | solution.py:533
  61.9 2.3 %grad_other.1 = (bf16[512,1024]{1,0:T(8,128)(2,1)}, f32[4,136,128]{2,1,0:T(8,128)S(1)}, f32[512,128]{1,0:T(8,128)S(1)}, f32[512,128]{1,0:T(8,128)S(1)}, f32[8,128]{1,0:T(8,128)}) custom-call(s32[1]{0:T(128)} %bitcast.core_ref.lead_ref, f32[8,8,128]{2,1,0:T(8,128)S(1)} %all_to_all.26.sums_ref, f32[8,512]{1,0:T(8,128)} %copy-done.2, ...), custom_call_target="tpu_custom_call" | custom-call | tf_op jit(solution)/shard_map/grad_other/pallas_call | solution.py:422
  64.3 1.5 %collective-permute-start.3 = (f32[4,136,128]{2,1,0:T(8,128)S(1)}, f32[4,136,128]{2,1,0:T(8,128)S(1)}, u32[]{:S(2)}, u32[]{:S(2)}) collective-permute-start(f32[4,136,128]{2,1,0:T(8,128)S(1)} %get-tuple-element.101), channel_id=1, source_target_pairs={{0,8},{8,0},{1,9},{9,1},{2,10},{10,2},{3,11},{11,3},{4,12},{12,4},... | collective-permute-start | bytes 835592 | tf_op jit(solution)/shard_map/ppermute | solution.py:406
  65.7 2.2 %grad_mine.1 = (bf16[512,1024]{1,0:T(8,128)(2,1)}, f32[4,136,128]{2,1,0:T(8,128)S(1)}, f32[4,136,128]{2,1,0:T(8,128)}) custom-call(s32[1]{0:T(128)} %bitcast.core_ref.lead_ref, f32[512,128]{1,0:T(8,128)S(1)} %get-tuple-element.97.scale_ref, f32[512,128]{1,0:T(8,128)S(1)} %get-tuple-element.98.center_ref, ...), custom_call_target="tpu_custom_call", output_to_operand_aliasing={{0}: (7, {})} | custom-call | tf_op jit(solution)/shard_map/grad_mine/pallas_call | solution.py:422
  68.0 0.9 combine.3
  68.8 3.5 %all-to-all-start.3 = ((f32[16,40,128]{2,1,0:T(8,128)}), f32[16,40,128]{2,1,0:T(8,128)S(1)}, u32[]{:S(2)}, u32[]{:S(2)}) async-start(f32[16,40,128]{2,1,0:T(8,128)} %get-tuple-element.102), calls=%async_computation.3 | async-start | bytes 655360 | tf_op jit(solution)/shard_map/all_to_all | solution.py:410
  72.4 9.2 %back.1 = (bf16[512,1024]{1,0:T(8,128)(2,1)}, f32[512,1024]{1,0:T(8,128)}) custom-call(f32[8,512]{1,0:T(8,128)} %copy-done.2, bf16[512,1024]{1,0:T(8,128)(2,1)} %q_ref.5, bf16[512,1024]{1,0:T(8,128)(2,1)} %k_hbm.1, bf16[512,1024]{1,0:T(8,128)(2,1)} %v_hbm.1, bf16[512,1024]{1,0:T(8,128)(2,1)} %get-tuple-element.109.grad_ref, f32[8,128,128]{2,1,0:T(8,128)} %copy-done.1), custom_call_target="tpu_custom_call" | custom-call | tf_op jit(solution)/shard_map/back/pallas_call | solution.py:422
  81.6 0.8 collective-permute-start.4
  83.2 6.4 %all-to-all-start.4 = ((f32[16,32,128]{2,1,0:T(8,128)}), f32[16,32,128]{2,1,0:T(8,128)S(1)}, u32[]{:S(2)}, u32[]{:S(2)}) async-start(f32[16,32,128]{2,1,0:T(8,128)} %scan.3), calls=%async_computation.4 | async-start | bytes 524288 | tf_op jit(solution)/shard_map/all_to_all | solution.py:410
  89.5 4.6 %gate.1 = (bf16[512,1024]{1,0:T(8,128)(2,1)}, bf16[512,1024]{1,0:T(8,128)(2,1)}) custom-call(f32[8,128]{1,0:T(8,128)} %get-tuple-element.111.table_ref, f32[512,1024]{1,0:T(8,128)} %copy-done, bf16[512,1024]{1,0:T(8,128)(2,1)} %gate_ref.3, bf16[512,1024]{1,0:T(8,128)(2,1)} %up_ref.3), custom_call_target="tpu_custom_call" | custom-call | tf_op jit(solution)/shard_map/gate/pallas_call | solution.py:422
  94.2 7.4 %value.1.value_part_ref.value_part_hbm = f32[512,1024]{1,0:T(8,128)} custom-call(bf16[512,1024]{1,0:T(8,128)(2,1)} %get-tuple-element.109.grad_ref, bf16[8,512,512]{2,1,0:T(8,128)(2,1)} %get-tuple-element.110.probs_ref), custom_call_target="tpu_custom_call" | custom-call | tf_op jit(solution)/shard_map/value/pallas_call | solution.py:422
  102.0 4.8 %final_mine.1 = (bf16[512,1024]{1,0:T(8,128)(2,1)}, bf16[512,1024]{1,0:T(8,128)(2,1)}, bf16[512,512]{1,0:T(8,128)(2,1)S(1)}, bf16[512,512]{1,0:T(8,128)(2,1)S(1)...) custom-call(s32[1]{0:T(128)} %bitcast.core_ref.lead_ref, f32[8,512]{1,0:T(8,128)} %copy-done.2, ...), custom_call_target="tpu_custom_call" | custom-call | tf_op jit(solution)/shard_map/final_mine/pallas_call | solution.py:422
  106.8 2.5 %final_other.1 = (bf16[512,1024]{1,0:T(8,128)(2,1)}, bf16[512,1024]{1,0:T(8,128)(2,1)}) custom-call(s32[1]{0:T(128)} %bitcast.core_ref.lead_ref, f32[8,512]{1,0:T(8,128)} %copy-done.2, bf16[512,512]{1,0:T(8,128)(2,1)S(1)} %get-tuple-element.121.k_ref, bf16[512,512]{1,0:T(8,128)(2,1)S(1)} %get-tuple-element.122.v_ref, ...), custom_call_target="tpu_custom_call", output_to_operand_aliasing={{0}: (8, {}), {1}: (9, {})} | custom-call | tf_op jit(solution)/shard_map/final_other/pallas_call | solution.py:422
  (24 shorter events, 2.6 us)
Async XLA Ops:
  0.6 0.7 copy-start.3
  3.7 12.0 %copy-start.2 = (f32[8,512]{1,0:T(8,128)}, f32[8,512]{1,0:T(8,128)S(1)}, u32[]{:S(2)}) copy-start(f32[8,512]{1,0:T(8,128)S(1)} %get-tuple-element.78.within_ref) | copy-start | bytes 49156
  3.7 6.1 %collective-permute-start = (f32[4,136,128]{2,1,0:T(8,128)S(1)}, f32[4,136,128]{2,1,0:T(8,128)S(1)}, u32[]{:S(2)}, u32[]{:S(2)}) collective-permute-start(f32[4,136,128]{2,1,0:T(8,128)S(1)} %get-tuple-element.70), channel_id=1, source_target_pairs={{0,8},{8,0},{1,9},{9,1},{2,10},{10,2},{3,11},{11,3},{4,12},{12,4},... | collective-permute-start | bytes 835592 | tf_op jit(solution)/shard_map/ppermute | solution.py:406
  9.8 14.3 %copy-start.5 = (f32[4,136,128]{2,1,0:T(8,128)S(1)}, f32[4,136,128]{2,1,0:T(8,128)}, u32[]{:S(2)}) copy-start(f32[4,136,128]{2,1,0:T(8,128)} %get-tuple-element.76) | copy-start | bytes 835588
  10.7 13.4 %all-to-all-start = ((f32[16,40,128]{2,1,0:T(8,128)}), f32[16,40,128]{2,1,0:T(8,128)S(1)}, u32[]{:S(2)}, u32[]{:S(2)}) async-start(f32[16,40,128]{2,1,0:T(8,128)} %get-tuple-element.71), calls=%async_computation | async-start | bytes 655360 | tf_op jit(solution)/shard_map/all_to_all | solution.py:410
  24.1 15.9 %collective-permute-start.1 = (f32[4,136,128]{2,1,0:T(8,128)S(1)}, f32[4,136,128]{2,1,0:T(8,128)S(1)}, u32[]{:S(2)}, u32[]{:S(2)}) collective-permute-start(f32[4,136,128]{2,1,0:T(8,128)S(1)} %copy-done.5), channel_id=1, source_target_pairs={{0,8},{8,0},{1,9},{9,1},{2,10},{10,2},{3,11},{11,3},{4,12},{12,4},... | collective-permute-start | bytes 835592 | tf_op jit(solution)/shard_map/ppermute | solution.py:406
  40.0 5.0 %collective-permute-start.2 = (f32[4,128,128]{2,1,0:T(8,128)S(1)}, f32[4,128,128]{2,1,0:T(8,128)S(1)}, u32[]{:S(2)}, u32[]{:S(2)}) collective-permute-start(f32[4,128,128]{2,1,0:T(8,128)S(1)} %bitcast.6), channel_id=1, source_target_pairs={{0,8},{8,0},{1,9},{9,1},{2,10},{10,2},{3,11},{11,3},{4,12},{12,4},... | collective-permute-start | bytes 786440 | tf_op jit(solution)/shard_map/ppermute | solution.py:406
  47.1 17.2 %copy-start.1 = (f32[8,128,128]{2,1,0:T(8,128)}, f32[8,128,128]{2,1,0:T(8,128)S(1)}, u32[]{:S(2)}) copy-start(f32[8,128,128]{2,1,0:T(8,128)S(1)} %get-tuple-element.104.state_ref) | copy-start | bytes 1572868
  47.1 18.7 %copy-start = (f32[512,1024]{1,0:T(8,128)}, f32[512,1024]{1,0:T(8,128)S(1)}, u32[]{:S(2)}) copy-start(f32[512,1024]{1,0:T(8,128)S(1)} %get-tuple-element.95.attn_ref) | copy-start | bytes 6291460
  64.3 3.7 %collective-permute-start.3 = (f32[4,136,128]{2,1,0:T(8,128)S(1)}, f32[4,136,128]{2,1,0:T(8,128)S(1)}, u32[]{:S(2)}, u32[]{:S(2)}) collective-permute-start(f32[4,136,128]{2,1,0:T(8,128)S(1)} %get-tuple-element.101), channel_id=1, source_target_pairs={{0,8},{8,0},{1,9},{9,1},{2,10},{10,2},{3,11},{11,3},{4,12},{12,4},... | collective-permute-start | bytes 835592 | tf_op jit(solution)/shard_map/ppermute | solution.py:406
  68.8 12.8 %all-to-all-start.3 = ((f32[16,40,128]{2,1,0:T(8,128)}), f32[16,40,128]{2,1,0:T(8,128)S(1)}, u32[]{:S(2)}, u32[]{:S(2)}) async-start(f32[16,40,128]{2,1,0:T(8,128)} %get-tuple-element.102), calls=%async_computation.3 | async-start | bytes 655360 | tf_op jit(solution)/shard_map/all_to_all | solution.py:410
  72.4 9.3 %copy-start.4 = (f32[4,136,128]{2,1,0:T(8,128)S(1)}, f32[4,136,128]{2,1,0:T(8,128)}, u32[]{:S(2)}) copy-start(f32[4,136,128]{2,1,0:T(8,128)} %get-tuple-element.114) | copy-start | bytes 835588
  81.6 20.0 %collective-permute-start.4 = (f32[4,136,128]{2,1,0:T(8,128)S(1)}, f32[4,136,128]{2,1,0:T(8,128)S(1)}, u32[]{:S(2)}, u32[]{:S(2)}) collective-permute-start(f32[4,136,128]{2,1,0:T(8,128)S(1)} %copy-done.4), channel_id=1, source_target_pairs={{0,8},{8,0},{1,9},{9,1},{2,10},{10,2},{3,11},{11,3},{4,12},{12,4},... | collective-permute-start | bytes 835592 | tf_op jit(solution)/shard_map/ppermute | solution.py:406
  83.2 18.4 %all-to-all-start.4 = ((f32[16,32,128]{2,1,0:T(8,128)}), f32[16,32,128]{2,1,0:T(8,128)S(1)}, u32[]{:S(2)}, u32[]{:S(2)}) async-start(f32[16,32,128]{2,1,0:T(8,128)} %scan.3), calls=%async_computation.4 | async-start | bytes 524288 | tf_op jit(solution)/shard_map/all_to_all | solution.py:410
  101.6 5.2 %collective-permute-start.5 = (f32[4,128,128]{2,1,0:T(8,128)S(1)}, f32[4,128,128]{2,1,0:T(8,128)S(1)}, u32[]{:S(2)}, u32[]{:S(2)}) collective-permute-start(f32[4,128,128]{2,1,0:T(8,128)S(1)} %bitcast.4), channel_id=1, source_target_pairs={{0,8},{8,0},{1,9},{9,1},{2,10},{10,2},{3,11},{11,3},{4,12},{12,4},... | collective-permute-start | bytes 786440 | tf_op jit(solution)/shard_map/ppermute | solution.py:406

commit v3 on v0

v3 whole, which is shorter than its diff:
```python
import jax
import jax.numpy as jnp
from jax import lax
from jax.experimental import pallas as pl
from jax.experimental.pallas import tpu as pltpu
from jax.sharding import Mesh
from jax.sharding import PartitionSpec as P

HEAD_COUNT = 64
HEAD = 128
SEQ = ("x", "y", "c")
CHIPS = ("x", "y")
HIGH = lax.Precision.HIGHEST
F32 = jnp.float32
BF16 = jnp.bfloat16
PAD = 8

NN = (((1,), (0,)), ((), ()))
NT = (((1,), (1,)), ((), ()))
TN = (((0,), (0,)), ((), ()))


def dot(a, b, dims, precision=None):
    return lax.dot_general(a, b, dims, precision=precision, preferred_element_type=F32)


def halves(x):
    high = x.astype(BF16)
    return high, (x - high.astype(F32)).astype(BF16)


def as_column(row):
    return jnp.transpose(jnp.broadcast_to(row, (HEAD, row.shape[1])))


def sigmoid(x):
    return 1.0 / (1.0 + jnp.exp(-x))


def lanes(head, count=1):
    return pl.ds(pl.multiple_of(head * (count * HEAD), HEAD), count * HEAD)


def put_state(ref, i, state, factor):
    ref[i, 0:HEAD, :] = state
    ref[i, HEAD : HEAD + PAD, :] = jnp.broadcast_to(factor, (PAD, HEAD))


def outer_state(wide, narrow):
    both = dot(narrow, wide, TN)
    return both[:, :HEAD] + both[:, HEAD:]


def sum_kernel(rate_ref, within_ref):
    heads, tokens = rate_ref.shape
    early = lax.broadcasted_iota(jnp.int32, (tokens, tokens), 0)
    late = lax.broadcasted_iota(jnp.int32, (tokens, tokens), 1)
    upto = (early <= late).astype(F32).astype(BF16)
    rate = rate_ref[...]
    high, rest = halves(rate)
    low = (rate - high.astype(F32) - rest.astype(F32)).astype(BF16)
    parts = jnp.concatenate([x.astype(F32) for x in (high, rest, low)], axis=0).astype(BF16)
    sums = dot(parts, upto, NN)
    within_ref[...] = sums[0:heads] + sums[heads : 2 * heads] + sums[2 * heads :]


def half_of(half, group, count=1):
    width = group * count * HEAD
    return pl.ds(pl.multiple_of(half * width, HEAD), width)


def copies(pairs, sems):
    return [pltpu.make_async_copy(a, b, sems.at[i]) for i, (a, b) in enumerate(pairs)]


def start(group):
    for copy in group:
        copy.start()


def wait(group):
    for copy in group:
        copy.wait()


def each_head(heads, body):
    def step(head, carry):
        body(head)
        return carry

    lax.fori_loop(0, heads, step, 0)


def head_copies(arrays, sems, head):
    made = []
    for i, (a, b, count) in enumerate(arrays):
        at = (head,) if count == 0 else (slice(None), lanes(head, count))
        made.append(pltpu.make_async_copy(a.at[at], b.at[at], sems.at[i, head]))
    return made


def local_state(head, cols, within_ref, k_ref, v_ref, out_ref, i):
    tokens = k_ref.shape[0]
    within = within_ref[pl.ds(head, 1), :]
    last = within[:, tokens - 1 :]
    tail = as_column(jnp.exp(last - within))
    scaled = jnp.concatenate(halves(k_ref[:, cols].astype(F32) * tail), axis=1)
    put_state(out_ref, i, outer_state(scaled, v_ref[:, cols]), jnp.exp(last))


def local_other_kernel(
    core_ref, rate_hbm, k_hbm, v_hbm, within_ref, out_ref, k_near, v_near, rate_ref, k_ref, v_ref, sems
):
    group = out_ref.shape[0]
    core = core_ref[0]
    far, near = half_of(1 - core, group), half_of(core, group)
    made = copies(
        [
            (rate_hbm, rate_ref),
            (v_hbm.at[:, far], v_ref),
            (k_hbm.at[:, far], k_ref),
            (v_hbm.at[:, near], v_near),
            (k_hbm.at[:, near], k_near),
        ],
        sems,
    )
    start(made)
    made[0].wait()
    sum_kernel(rate_ref, within_ref)
    wait(made[1:3])
    for i in range(group):
        cols = slice(i * HEAD, (i + 1) * HEAD)
        local_state((1 - core) * group + i, cols, within_ref, k_ref, v_ref, out_ref, i)
    wait(made[3:])


def local_mine_kernel(core_ref, within_ref, k_ref, v_ref, out_ref):
    group = out_ref.shape[0]
    for i in range(group):
        cols = slice(i * HEAD, (i + 1) * HEAD)
        local_state(core_ref[0] * group + i, cols, within_ref, k_ref, v_ref, out_ref, i)


def combine_kernel(
    lead_ref, mine_ref, other_ref, out_hbm, mine_hbm, other_hbm, out_ref, sems
):
    made = copies([(mine_ref, mine_hbm), (other_ref, other_hbm), (out_ref, out_hbm)], sems)
    start(made[:2])
    lead = lead_ref[0] == 1
    group = mine_ref.shape[0]
    rows = HEAD // 4
    for i in range(group):
        own = mine_ref[i, HEAD : HEAD + PAD, :]
        far = other_ref[i, HEAD : HEAD + PAD, :]
        mine = mine_ref[i, 0:HEAD, :]
        other = other_ref[i, 0:HEAD, :]
        both = jnp.where(lead, far[0:1] * mine + other, own[0:1] * other + mine)
        for j in range(4):
            out_ref[4 * i + j, 0:rows, :] = both[j * rows : (j + 1) * rows]
            out_ref[4 * i + j, rows : rows + PAD, :] = own * far
    made[2].start()
    wait(made)


def scan_kernel(reverse, in_ref, out_hbm, out_ref, sems):
    chips, rows = out_ref.shape[0], out_ref.shape[1]
    state = jnp.zeros(out_ref.shape[1:], F32)
    made = []
    for n in reversed(range(chips)) if reverse else range(chips):
        out_ref[n] = state
        state = in_ref[n, rows : rows + 1, :] * state + in_ref[n, 0:rows, :]
    made = copies([(out_ref, out_hbm)], sems)
    start(made)
    wait(made)


def decay_block(within, column, first, size, width):
    gap = jnp.concatenate([column[first : first + size]] * (width // HEAD), axis=1)
    gap = gap - within[:, :width]
    rows = first + lax.broadcasted_iota(jnp.int32, gap.shape, 0)
    cols = lax.broadcasted_iota(jnp.int32, gap.shape, 1)
    return jnp.where(rows >= cols, jnp.exp(jnp.minimum(gap, 0.0)), 0.0)


def inside_kernel(
    within_hbm, q_hbm, k_hbm, v_hbm, probs_hbm, intra_hbm,
    within_ref, q_ref, k_ref, v_ref, probs_ref, intra_ref, sem, in_sems, out_sems,
):
    heads = within_ref.shape[0]
    tokens = q_ref.shape[0]
    size = tokens // 2
    small = copies([(within_hbm, within_ref)], sem)
    start(small)
    loads = [(q_hbm, q_ref, 1), (k_hbm, k_ref, 1), (v_hbm, v_ref, 1)]
    each_head(heads, lambda h: start(head_copies(loads, in_sems, h)))
    wait(small)

    def results(h):
        upper, lower = pl.ds(0, size), pl.ds(size, size)
        pairs = [
            (probs_ref.at[h, upper, upper], probs_hbm.at[h, upper, upper]),
            (probs_ref.at[h, lower], probs_hbm.at[h, lower]),
            (intra_ref.at[:, lanes(h)], intra_hbm.at[:, lanes(h)]),
        ]
        return [pltpu.make_async_copy(a, b, out_sems.at[i, h]) for i, (a, b) in enumerate(pairs)]

    def one(h):
        within = within_ref[pl.ds(h, 1), :]
        column = as_column(within)
        wait(head_copies(loads, in_sems, h))
        q, k, v = q_ref[:, lanes(h)], k_ref[:, lanes(h)], v_ref[:, lanes(h)]
        for first in (0, size):
            width = first + size
            scores = dot(q[first:width], k[0:width], NT)
            probs = (scores * decay_block(within, column, first, size, width)).astype(BF16)
            probs_ref[h, first:width, 0:width] = probs
            intra_ref[first:width, lanes(h)] = dot(probs, v[0:width], NN)
        start(results(h))

    each_head(heads, one)
    each_head(heads, lambda h: wait(results(h)))


def prepare_kernel(
    within_hbm, q_hbm, gate_hbm, up_hbm, dnorm_hbm, grown_hbm,
    within_ref, q_ref, gate_ref, up_ref, dnorm_ref, grown_ref, sem, in_sems, out_sems,
):
    heads = within_ref.shape[0]
    small = copies([(within_hbm, within_ref)], sem)
    start(small)
    loads = [(q_hbm, q_ref, 1), (gate_hbm, gate_ref, 1), (up_hbm, up_ref, 1)]
    stores = [(dnorm_ref, dnorm_hbm, 1), (grown_ref, grown_hbm, 2)]
    each_head(heads, lambda h: start(head_copies(loads, in_sems, h)))
    wait(small)

    def one(h):
        grow = as_column(jnp.exp(within_ref[pl.ds(h, 1), :]))
        wait(head_copies(loads, in_sems, h))
        dnorm_ref[:, lanes(h)] = up_ref[:, lanes(h)].astype(F32) * sigmoid(
            gate_ref[:, lanes(h)].astype(F32)
        )
        grown = q_ref[:, lanes(h)].astype(F32) * grow
        grown_ref[:, lanes(h, 2)] = jnp.concatenate(halves(grown), axis=1)
        start(head_copies(stores, out_sems, h))

    each_head(heads, one)
    each_head(heads, lambda h: wait(head_copies(stores, out_sems, h)))


def pick_state(follows, chip_ref, lead_ref, i):
    chip = chip_ref[i]
    return jnp.where(
        follows, lead_ref[i, HEAD : HEAD + 1, :] * chip + lead_ref[i, 0:HEAD, :], chip
    )


def attn_head(core, head, i, at, grown_ref, intra_ref, dnorm_ref, chip_ref, lead_ref, attn_ref, state_ref):
    state = pick_state(core == 1, chip_ref, lead_ref, i)
    state_ref[head] = state
    high, low = halves(state)
    grown = grown_ref[:, lanes(head, 2)]
    attn = intra_ref[:, at] + dot(
        jnp.concatenate([grown, grown[:, :HEAD]], axis=1),
        jnp.concatenate([high, high, low], axis=1),
        NT,
    )
    attn_ref[:, lanes(head)] = attn
    return attn * attn, dnorm_ref[:, lanes(head)] * attn


def attn_mine_kernel(
    core_ref, chip_ref, within_hbm, lead_hbm, grown_hbm, intra_hbm, dnorm_hbm,
    attn_ref, dnorm_ref, grown_ref, state_ref, square_ref, inner_ref, intra_far, within_ref,
    lead_ref, intra_ref, sems,
):
    core = core_ref[0]
    group = chip_ref.shape[0]
    pairs = [(lead_hbm, lead_ref)]
    for half, target in ((core, intra_ref), (1 - core, intra_far)):
        wide, two = half_of(half, group), half_of(half, group, 2)
        pairs += [
            (grown_hbm.at[:, two], grown_ref.at[:, two]),
            (intra_hbm.at[:, wide], target),
            (dnorm_hbm.at[:, wide], dnorm_ref.at[:, wide]),
        ]
    made = copies(pairs + [(within_hbm, within_ref)], sems)
    start(made)
    wait(made[:4])
    square = inner = jnp.zeros(square_ref.shape, F32)
    for i in range(group):
        more = attn_head(
            core, core * group + i, i, slice(i * HEAD, (i + 1) * HEAD), grown_ref, intra_ref,
            dnorm_ref, chip_ref, lead_ref, attn_ref, state_ref,
        )
        square, inner = square + more[0], inner + more[1]
    square_ref[...] = square
    inner_ref[...] = inner
    wait(made[4:])


def attn_other_kernel(
    core_ref, chip_ref, lead_ref, intra_ref, square_ref, inner_ref, dnorm_ref, grown_ref, attn_in, state_in,
    attn_ref, state_ref, sums_ref,
):
    core = core_ref[0]
    group = chip_ref.shape[0]
    square, inner = square_ref[...], inner_ref[...]
    for i in range(group):
        more = attn_head(
            core, (1 - core) * group + i, i, slice(i * HEAD, (i + 1) * HEAD), grown_ref, intra_ref,
            dnorm_ref, chip_ref, lead_ref, attn_ref, state_ref,
        )
        square, inner = square + more[0], inner + more[1]
    ones = jnp.ones((8, HEAD), F32)
    square = dot(ones, square, NT, HIGH)
    inner = dot(ones, inner, NT, HIGH)
    rows = lax.broadcasted_iota(jnp.int32, (8, HEAD), 0)
    packed = jnp.zeros((8, HEAD), F32)
    for i in range(4):
        cols = slice(i * HEAD, (i + 1) * HEAD)
        packed = jnp.where(rows == i, square[:, cols], packed)
        packed = jnp.where(rows == i + 4, inner[:, cols], packed)
    sums_ref[...] = jnp.broadcast_to(packed[None], sums_ref.shape)


def grad_head(head, i, within_ref, grown_ref, attn_ref, dnorm_ref, scale_ref, center_ref, out_ref):
    tokens = attn_ref.shape[0]
    scale = scale_ref[...]
    normed = attn_ref[:, lanes(head)] * scale
    grad = (scale * (dnorm_ref[:, lanes(head)] - normed * center_ref[...])).astype(BF16)
    last = within_ref[pl.ds(head, 1), :][:, tokens - 1 :]
    put_state(out_ref, i, outer_state(grown_ref[:, lanes(head, 2)], grad), jnp.exp(last))
    return grad


def grad_other_kernel(
    core_ref, sums_ref, within_ref, grown_ref, attn_ref, dnorm_ref,
    grad_ref, out_ref, scale_ref, center_ref, table_ref,
):
    total = jnp.sum(sums_ref[...], axis=0) / (HEAD_COUNT * HEAD)
    scale = lax.rsqrt(total[0:4] + 1e-06)
    center = scale * total[4:8]
    table_ref[0:4] = scale
    table_ref[4:8] = center
    for i in range(4):
        rows = slice(i * HEAD, (i + 1) * HEAD)
        scale_ref[rows] = as_column(scale[i : i + 1])
        center_ref[rows] = as_column(center[i : i + 1])
    group = out_ref.shape[0]
    for i in range(group):
        grad_ref[:, i * HEAD : (i + 1) * HEAD] = grad_head(
            (1 - core_ref[0]) * group + i, i, within_ref, grown_ref, attn_ref, dnorm_ref,
            scale_ref, center_ref, out_ref,
        )


def grad_mine_kernel(
    core_ref, scale_ref, center_ref, table_ref, within_ref, grown_ref, attn_ref, dnorm_ref, grad_far,
    grad_hbm, table_hbm, out_ref, grad_ref, sems, far_sems,
):
    core = core_ref[0]
    group = out_ref.shape[0]
    made = copies(
        [(grad_far, grad_hbm.at[:, half_of(1 - core, group)]), (table_ref, table_hbm)], far_sems
    )
    start(made)
    stores = []
    for i in range(group):
        head = core * group + i
        cols = slice(i * HEAD, (i + 1) * HEAD)
        grad_ref[:, cols] = grad_head(
            head, i, within_ref, grown_ref, attn_ref, dnorm_ref, scale_ref, center_ref, out_ref
        )
        store = pltpu.make_async_copy(
            grad_ref.at[:, cols], grad_hbm.at[:, lanes(head)], sems.at[i]
        )
        store.start()
        stores.append(store)
    wait(made + stores)


def gate_kernel(
    table_hbm, attn_hbm, gate_hbm, up_hbm, output_hbm, gate_grad_hbm,
    table_ref, attn_ref, gate_ref, up_ref, output_ref, gate_grad_ref, scale_ref, sem, in_sems, out_sems,
):
    heads = in_sems.shape[1]
    small = copies([(table_hbm, table_ref)], sem)
    start(small)
    loads = [(attn_hbm, attn_ref, 1), (gate_hbm, gate_ref, 1), (up_hbm, up_ref, 1)]
    stores = [(output_ref, output_hbm, 1), (gate_grad_ref, gate_grad_hbm, 1)]
    each_head(heads, lambda h: start(head_copies(loads, in_sems, h)))
    wait(small)
    for i in range(4):
        scale_ref[i * HEAD : (i + 1) * HEAD] = as_column(table_ref[i : i + 1])

    def one(h):
        wait(head_copies(loads, in_sems, h))
        normed = attn_ref[:, lanes(h)] * scale_ref[...]
        sig = sigmoid(gate_ref[:, lanes(h)].astype(F32))
        output_ref[:, lanes(h)] = (normed * sig).astype(BF16)
        gate_grad_ref[:, lanes(h)] = (
            up_ref[:, lanes(h)].astype(F32) * normed * sig * (1.0 - sig)
        ).astype(BF16)
        start(head_copies(stores, out_sems, h))

    each_head(heads, one)
    each_head(heads, lambda h: wait(head_copies(stores, out_sems, h)))


def back_kernel(
    within_hbm, q_hbm, k_hbm, v_hbm, grad_hbm, state_hbm, query_grad_hbm, key_hbm,
    within_ref, q_ref, k_ref, v_ref, grad_ref, state_ref, query_grad_ref, key_ref, sem, in_sems, out_sems,
):
    heads = within_ref.shape[0]
    tokens = q_ref.shape[0]
    size = tokens // 2
    small = copies([(within_hbm, within_ref)], sem)
    start(small)
    loads = [
        (grad_hbm, grad_ref, 1), (v_hbm, v_ref, 1), (k_hbm, k_ref, 1), (q_hbm, q_ref, 1),
        (state_hbm, state_ref, 0),
    ]
    stores = [(query_grad_ref, query_grad_hbm, 1), (key_ref, key_hbm, 1)]
    each_head(heads, lambda h: start(head_copies(loads, in_sems, h)))
    wait(small)

    def one(h):
        within = within_ref[pl.ds(h, 1), :]
        column = as_column(within)
        grow = jnp.exp(column)
        wait(head_copies(loads, in_sems, h))
        at = lanes(h)
        q, k, v = q_ref[:, at], k_ref[:, at], v_ref[:, at]
        state = jnp.concatenate(halves(state_ref[h]), axis=0)
        for first in (0, size):
            width = first + size
            grad = grad_ref[first:width, at]
            pgrad = dot(grad, v[0:width], NT)
            pgrad = (pgrad * decay_block(within, column, first, size, width)).astype(BF16)
            inter = dot(jnp.concatenate([grad, grad], axis=1), state, NN)
            query_grad_ref[first:width, at] = (
                dot(pgrad, k[0:width], NN) + grow[first:width] * inter
            ).astype(BF16)
            key_part = dot(pgrad, q[first:width], TN)
            if first == 0:
                key_ref[0:width, at] = key_part
            else:
                key_ref[0:first, at] += key_part[0:first]
                key_ref[first:width, at] = key_part[first:width]
        start(head_copies(stores, out_sems, h))

    each_head(heads, one)
    each_head(heads, lambda h: wait(head_copies(stores, out_sems, h)))


def value_kernel(
    grad_hbm, probs_hbm, value_hbm, grad_ref, probs_ref, value_ref, in_sems, out_sems
):
    heads = probs_ref.shape[0]
    tokens = grad_ref.shape[0]
    size = tokens // 2

    def loads(h):
        upper, lower = pl.ds(0, size), pl.ds(size, size)
        pairs = [
            (grad_hbm.at[:, lanes(h)], grad_ref.at[:, lanes(h)]),
            (probs_hbm.at[h, upper, upper], probs_ref.at[h, upper, upper]),
            (probs_hbm.at[h, lower], probs_ref.at[h, lower]),
        ]
        return [pltpu.make_async_copy(a, b, in_sems.at[i, h]) for i, (a, b) in enumerate(pairs)]

    stores = [(value_ref, value_hbm, 1)]
    each_head(heads, lambda h: start(loads(h)))

    def one(h):
        wait(loads(h))
        at = lanes(h)
        late = dot(probs_ref[h, size:tokens, :], grad_ref[size:tokens, at], TN)
        early = dot(probs_ref[h, 0:size, 0:size], grad_ref[0:size, at], TN)
        value_ref[0:size, at] = late[0:size] + early
        value_ref[size:tokens, at] = late[size:tokens]
        start(head_copies(stores, out_sems, h))

    each_head(heads, one)
    each_head(heads, lambda h: wait(head_copies(stores, out_sems, h)))


def final_head(core, head, i, within_ref, k_ref, v_ref, key_part_ref, value_part_ref, chip_ref, lead_ref):
    tokens = k_ref.shape[0]
    at = slice(i * HEAD, (i + 1) * HEAD)
    state = halves(pick_state(core == 0, chip_ref, lead_ref, i))
    within = within_ref[pl.ds(head, 1), :]
    tail = as_column(jnp.exp(within[:, tokens - 1 :] - within))
    k, v = k_ref[:, at], v_ref[:, at]
    key_inter = dot(jnp.concatenate([v, v], axis=1), jnp.concatenate(state, axis=0), NN)
    value_inter = dot(jnp.concatenate([k, k], axis=1), jnp.concatenate(state, axis=1), NT)
    return (
        (key_part_ref[:, at] + tail * key_inter).astype(BF16),
        (value_part_ref[:, at] + tail * value_inter).astype(BF16),
    )


def final_mine_kernel(
    core_ref, chip_ref, within_hbm, lead_hbm, k_hbm, v_hbm, key_part_hbm, value_part_hbm,
    key_grad_ref, value_grad_ref, k_far, v_far, key_part_far, value_part_far, within_ref,
    lead_ref, k_ref, v_ref, key_part_ref, value_part_ref, sems,
):
    core = core_ref[0]
    group = chip_ref.shape[0]
    sources = (k_hbm, v_hbm, key_part_hbm, value_part_hbm)
    near, far = half_of(core, group), half_of(1 - core, group)
    pairs = [(within_hbm, within_ref), (lead_hbm, lead_ref)]
    pairs += [(a.at[:, near], b) for a, b in zip(sources, (k_ref, v_ref, key_part_ref, value_part_ref))]
    pairs += [(a.at[:, far], b) for a, b in zip(sources, (k_far, v_far, key_part_far, value_part_far))]
    made = copies(pairs, sems)
    start(made)
    wait(made[:6])
    for i in range(group):
        cols = slice(i * HEAD, (i + 1) * HEAD)
        key_grad_ref[:, cols], value_grad_ref[:, cols] = final_head(
            core, core * group + i, i, within_ref, k_ref, v_ref, key_part_ref, value_part_ref,
            chip_ref, lead_ref,
        )
    wait(made[6:])


def final_other_kernel(
    core_ref, chip_ref, lead_ref, within_ref, k_ref, v_ref, key_part_ref, value_part_ref, key_near, value_near,
    key_grad_hbm, value_grad_hbm, key_grad_ref, value_grad_ref, near_sems, sems,
):
    core = core_ref[0]
    group = chip_ref.shape[0]
    near = half_of(core, group)
    made = copies(
        [(key_near, key_grad_hbm.at[:, near]), (value_near, value_grad_hbm.at[:, near])], near_sems
    )
    start(made)
    for i in range(group):
        cols = slice(i * HEAD, (i + 1) * HEAD)
        head = (1 - core) * group + i
        key_grad_ref[:, cols], value_grad_ref[:, cols] = final_head(
            core, head, i, within_ref, k_ref, v_ref, key_part_ref, value_part_ref, chip_ref, lead_ref
        )
        stores = [
            pltpu.make_async_copy(a.at[:, cols], b.at[:, lanes(head)], sems.at[j, i])
            for j, (a, b) in enumerate(((key_grad_ref, key_grad_hbm), (value_grad_ref, value_grad_hbm)))
        ]
        start(stores)
        made = made + stores
    wait(made)


def shape(dims, dtype=F32):
    return jax.ShapeDtypeStruct(dims, dtype)


def swap(x):
    return lax.ppermute(x, "c", [(0, 1), (1, 0)])


def spread(x):
    return lax.all_to_all(x, CHIPS, split_axis=0, concat_axis=0, tiled=True)


def call(kernel, name, near, far, near_out, far_out, buffers, sems, core=None, aliases=(), mib=16):
    scalars = () if core is None else (core,)
    vmem = pl.BlockSpec(memory_space=pltpu.VMEM)
    hbm = pl.BlockSpec(memory_space=pl.ANY)
    return pl.pallas_call(
        kernel,
        grid_spec=pltpu.PrefetchScalarGridSpec(
            num_scalar_prefetch=len(scalars),
            grid=(1,),
            in_specs=[vmem] * len(near) + [hbm] * len(far),
            out_specs=[hbm] * len(far_out) + [vmem] * len(near_out),
            scratch_shapes=[pltpu.VMEM(x.shape, x.dtype) for x in buffers]
            + [pltpu.SemaphoreType.DMA(dims) for dims in sems],
        ),
        out_shape=[pltpu.HBM(x.shape, x.dtype) for x in far_out]
        + [pltpu.VMEM(x.shape, x.dtype) for x in near_out],
        input_output_aliases=dict(aliases),
        compiler_params=pltpu.CompilerParams(
            dimension_semantics=("arbitrary",), vmem_limit_bytes=mib * 2**20
        ),
        name=name,
    )(*scalars, *near, *(pltpu.with_memory_space_constraint(x, pltpu.HBM) for x in far))


def shards(queries, keys, values, gate, log_decay, out_grad):
    tokens, flat = queries.shape
    heads = log_decay.shape[1]
    group = heads // 2
    chips = lax.axis_size("x") * lax.axis_size("y")
    rows = group * HEAD // chips
    core = lax.axis_index("c").astype(jnp.int32).reshape(1)
    packed = shape((group, HEAD + PAD, HEAD))
    sliced = shape((chips, rows, HEAD))
    carried = shape((chips, rows + PAD, HEAD))
    wide = shape((tokens, flat))
    narrow = shape((tokens, flat), BF16)
    double = shape((tokens, 2 * flat), BF16)
    half = shape((tokens, flat // 2))
    half_narrow = shape((tokens, flat // 2), BF16)
    column = shape((tokens, HEAD))
    states = shape((heads, HEAD, HEAD))
    table_rows = shape((8, HEAD))
    sums_rows = shape((8, 8, HEAD))
    rates = shape((heads, tokens))
    table_of = shape((heads, tokens, tokens), BF16)

    def combined(lead, mine, other):
        return call(
            combine_kernel, "combine", (mine, other), (), (), (carried, packed, packed), (carried,), ((3,),),
            lead,
        )

    def scanned(x, reverse):
        (out,) = call(
            lambda *refs: scan_kernel(reverse, *refs), "scan", (x,), (), (), (sliced,), (sliced,), ((1,),)
        )
        return out

    within, theirs, k_near, v_near = call(
        local_other_kernel, "local_other", (), (log_decay.T, keys, values),
        (rates, packed, half_narrow, half_narrow), (), (rates, half_narrow, half_narrow), ((5,),), core,
    )
    lead_mine = swap(theirs)
    (mine,) = call(
        local_mine_kernel, "local_mine", (within, k_near, v_near), (), (packed,), (), (), (), core
    )
    chip_state, mine, lead_mine = combined(1 - core, mine, lead_mine)
    chip_state = spread(chip_state)
    probs, intra = call(
        inside_kernel, "inside", (), (within, queries, keys, values), (), (table_of, wide),
        (rates, narrow, narrow, narrow, table_of, wide), ((1,), (3, heads), (3, heads)),
    )
    chip_state, probs, intra, mine, within = lax.optimization_barrier(
        (chip_state, probs, intra, mine, within)
    )
    chip_state, within = lax.optimization_barrier((scanned(chip_state, False), within))
    chip_mine = spread(chip_state)
    dnorm, grown = call(
        prepare_kernel, "prepare", (), (within, queries, gate, out_grad), (), (wide, double),
        (rates, narrow, narrow, narrow, wide, double), ((1,), (3, heads), (2, heads)),
    )
    chip_mine, mine, dnorm, grown = lax.optimization_barrier((chip_mine, mine, dnorm, grown))
    chip_mine = chip_mine.reshape(group, HEAD, HEAD)
    chip_other, lead_other = swap(chip_mine), swap(mine)
    attn, dnorm, grown, state, square, inner, intra_far, within_near = call(
        attn_mine_kernel, "attn_mine", (chip_mine,), (within, lead_mine, grown, intra, dnorm),
        (wide, wide, double, states, column, column, half, rates), (), (packed, half), ((8,),), core,
    )
    attn, state, sums = call(
        attn_other_kernel, "attn_other",
        (chip_other, lead_other, intra_far, square, inner, dnorm, grown, attn, state), (),
        (wide, states, sums_rows), (), (), (), core, {8: 0, 9: 1},
    )
    sums = lax.all_to_all(sums, "tp", split_axis=0, concat_axis=0, tiled=True)
    grad_far, theirs, scale, center, table = call(
        grad_other_kernel, "grad_other", (sums, within_near, grown, attn, dnorm), (),
        (half_narrow, packed, column, column, table_rows), (), (), (), core,
    )
    lead_mine = swap(theirs)
    grad, table, mine = call(
        grad_mine_kernel, "grad_mine",
        (scale, center, table, within_near, grown, attn, dnorm, grad_far), (),
        (packed,), (narrow, table_rows), (half_narrow,), ((group,), (2,)), core,
    )
    chip_state, mine, lead_mine = combined(core, mine, lead_mine)
    chip_state = spread(chip_state)
    query_grad, key_part = call(
        back_kernel, "back", (), (within, queries, keys, values, grad, state), (), (narrow, wide),
        (rates, narrow, narrow, narrow, narrow, states, narrow, wide), ((1,), (5, heads), (2, heads)),
    )
    chip_state, key_part, mine, grad, table = lax.optimization_barrier(
        (chip_state, key_part, mine, grad, table)
    )
    chip_state, grad, table = lax.optimization_barrier((scanned(chip_state, True), grad, table))
    chip_mine = spread(chip_state)
    (value_part,) = call(
        value_kernel, "value", (), (grad, probs), (), (wide,), (narrow, table_of, wide), ((3, heads), (1, heads))
    )
    output, gate_grad = call(
        gate_kernel, "gate", (), (table, attn, gate, out_grad), (), (narrow, narrow),
        (table_rows, wide, narrow, narrow, narrow, narrow, column), ((1,), (3, heads), (2, heads)),
    )
    chip_mine, value_part, output, gate_grad, mine = lax.optimization_barrier(
        (chip_mine, value_part, output, gate_grad, mine)
    )
    chip_mine = chip_mine.reshape(group, HEAD, HEAD)
    chip_other, lead_other = swap(chip_mine), swap(mine)
    key_near, value_near, *far, within_near = call(
        final_mine_kernel, "final_mine", (chip_mine,), (within, lead_mine, keys, values, key_part, value_part),
        (half_narrow, half_narrow, half_narrow, half_narrow, half, half, rates), (),
        (packed, half_narrow, half_narrow, half, half), ((10,),), core,
    )
    key_grad, value_grad = call(
        final_other_kernel, "final_other", (chip_other, lead_other, within_near, *far, key_near, value_near), (),
        (), (narrow, narrow), (half_narrow, half_narrow), ((2,), (2, group)), core,
    )
    return output, query_grad, key_grad, value_grad, gate_grad


def solution(mesh):
    split = Mesh(mesh.devices.reshape(4, 4, 2, mesh.shape["tp"]), ("x", "y", "c", "tp"))
    return jax.shard_map(
        shards,
        mesh=split,
        in_specs=(P(SEQ, "tp"),) * 6,
        out_specs=(P(SEQ, "tp"),) * 5,
        check_vma=False,
    )
```

time: 251 us -> 97.9 us (0.39)
  waiting for transfers between devices: 122 us -> 3.76 us
  Pallas kernels: 0 us -> 47 us
  matrix products: 28.9 us -> 0 us
  other arithmetic: 25.7 us -> 0 us
  starting transfers between devices: 7.15 us -> 30.4 us
  blocking collectives: 35 us -> 14.9 us
  local copies, waits for them, and re-layouts: 16.9 us -> 0.02 us
  between operations: 14.4 us -> 0.89 us
    all_gather x6 -> x0, waiting for transfers between devices: 117 us -> none  [prefix_by_axis(): pieces = jax.tree.map(lambda part: lax.all_gather(part, axis), subtotal)]
    pallas_call x0 -> x17, Pallas kernels: none -> 47 us  [call(): pl.pallas_call(kernel, grid_spec=pltpu.PrefetchScalarGridSpec(num_scalar_...]
    dot_general x12 -> x0, matrix products: 28.9 us -> none  [the longest x1 4.4 us: shards(): jnp.einsum('hts,thd->shd', probs, grad_h, preferred_element_type=jnp.floa...]
    all_gather x4 -> x0, blocking collectives: 26 us -> none  [prefix_by_axis(): pieces = jax.tree.map(lambda part: lax.all_gather(part, axis), subtotal)]
    add x6 -> x0, other arithmetic: 16.3 us -> none  [combine(): later[0][:, None, None] * earlier[1] + later[1]]
    all_to_all x1 -> x4, starting transfers between devices: 6.73 us -> 21.6 us  [spread(): return lax.all_to_all(x, CHIPS, split_axis=0, concat_axis=0, tiled=True)]
    unnamed x39 -> x10, local copies, waits for them, and re-layouts: 12.4 us -> 0.02 us
    ppermute x0 -> x6, starting transfers between devices: none -> 8.75 us  [swap(): return lax.ppermute(x, 'c', [(0, 1), (1, 0)])]
  transfers between devices with their start and end apart: 7 -> 10, of which waited for: 7 -> 3; matrix products, arithmetic and copies ran while one was open for 9% -> 0% of each run, Pallas kernels for 0% -> 39%
where the time goes in v3:
time: 97.9 us; the launch traced here: 97 us
  Pallas kernels  47 us (48%)
  starting transfers between devices  30.4 us (31%)
  blocking collectives  14.9 us (15%)
  waiting for transfers between devices  3.76 us (4%)
    pallas_call x17, Pallas kernels, call(): pl.pallas_call(kernel, grid_spec=pltpu.PrefetchScalarGridSpec(num_scalar_...  47 us
    all_to_all x4, starting transfers between devices, spread(): return lax.all_to_all(x, CHIPS, split_axis=0, concat_axis=0, tiled=True)  21.6 us
    all_to_all x1, blocking collectives, shards(): sums = lax.all_to_all(sums, 'tp', split_axis=0, concat_axis=0, tiled=True)  14.9 us
    ppermute x6, starting transfers between devices, swap(): return lax.ppermute(x, 'c', [(0, 1), (1, 0)])  8.75 us
    all_to_all x4, waiting for transfers between devices, spread(): return lax.all_to_all(x, CHIPS, split_axis=0, concat_axis=0, tiled=True)  3.37 us
  transfers between devices with their start and end apart: 10, of which 3 were waited for; matrix products, arithmetic and copies ran while one was open for 0% of the time, Pallas kernels for 39%

profile of v3, /device:TPU:1, one launch (start us, length us, event | category | flops | bytes accessed | tf_op | source)
XLA Modules:
  0.0 97.0 jit_solution(2334057043846408240)
XLA Ops:
  0.6 2.1 %local_other.1 = (f32[8,512]{1,0:T(8,128)S(1)}, f32[4,136,128]{2,1,0:T(8,128)S(1)}, bf16[512,512]{1,0:T(8,128)(2,1)S(1)}, bf16[512,512]{1,0:T(8,128)(2,1)S(1)}) custom-call(s32[1]{0:T(128)} %bitcast.core_ref.lead_ref, f32[8,512]{1,0:T(8,128)} %bitcast.8, bf16[512,1024]{1,0:T(8,128)(2,1)} %k_hbm.7, bf16[512,1024]{1,0:T(8,128)(2,1)} %v_hbm.7), custom_call_target="tpu_custom_call" | custom-call | tf_op jit(solution)/shard_map/local_other/pallas_call | solution.py:569
  2.7 3.3 %collective-permute-start = (f32[4,136,128]{2,1,0:T(8,128)S(1)}, f32[4,136,128]{2,1,0:T(8,128)S(1)}, u32[]{:S(2)}, u32[]{:S(2)}) collective-permute-start(f32[4,136,128]{2,1,0:T(8,128)S(1)} %get-tuple-element.78), channel_id=1, source_target_pairs={{0,8},{8,0},{1,9},{9,1},{2,10},{10,2},{3,11},{11,3},{4,12},{12,4},... | collective-permute-start | bytes 835592 | tf_op jit(solution)/shard_map/ppermute | solution.py:558
  6.1 0.8 local_mine.1.mine_ref
  7.3 0.9 combine.2
  8.2 5.0 %all-to-all-start = ((f32[16,40,128]{2,1,0:T(8,128)}), f32[16,40,128]{2,1,0:T(8,128)S(1)}, u32[]{:S(2)}, u32[]{:S(2)}) async-start(f32[16,40,128]{2,1,0:T(8,128)} %get-tuple-element.79), calls=%async_computation | async-start | bytes 655360 | tf_op jit(solution)/shard_map/all_to_all | solution.py:562
  13.3 7.7 %inside.1 = (bf16[8,512,512]{2,1,0:T(8,128)(2,1)}, f32[512,1024]{1,0:T(8,128)}) custom-call(f32[8,512]{1,0:T(8,128)} %copy-done.2, bf16[512,1024]{1,0:T(8,128)(2,1)} %q_hbm.5, bf16[512,1024]{1,0:T(8,128)(2,1)} %k_hbm.7, bf16[512,1024]{1,0:T(8,128)(2,1)} %v_hbm.7), custom_call_target="tpu_custom_call" | custom-call | tf_op jit(solution)/shard_map/inside/pallas_call | solution.py:569
  21.9 6.4 %all-to-all-start.1 = ((f32[16,32,128]{2,1,0:T(8,128)}), f32[16,32,128]{2,1,0:T(8,128)S(1)}, u32[]{:S(2)}, u32[]{:S(2)}) async-start(f32[16,32,128]{2,1,0:T(8,128)} %scan.2), calls=%async_computation.1 | async-start | bytes 524288 | tf_op jit(solution)/shard_map/all_to_all | solution.py:562
  28.4 4.3 %prepare.1 = (f32[512,1024]{1,0:T(8,128)}, bf16[512,2048]{1,0:T(8,128)(2,1)}) custom-call(f32[8,512]{1,0:T(8,128)} %copy-done.2, bf16[512,1024]{1,0:T(8,128)(2,1)} %q_hbm.5, bf16[512,1024]{1,0:T(8,128)(2,1)} %gate_hbm.3, bf16[512,1024]{1,0:T(8,128)(2,1)} %up_hbm.3), custom_call_target="tpu_custom_call" | custom-call | tf_op jit(solution)/shard_map/prepare/pallas_call | solution.py:569
  32.7 3.1 %all-to-all-done.1 = f32[16,32,128]{2,1,0:T(8,128)S(1)} async-done(((f32[16,32,128]{2,1,0:T(8,128)}), f32[16,32,128]{2,1,0:T(8,128)S(1)}, u32[]{:S(2)}, u32[]{:S(2)}) %all-to-all-start.1) | async-done | bytes 262176 | tf_op jit(solution)/shard_map/all_to_all | solution.py:562
  35.8 2.3 %collective-permute-start.2 = (f32[4,136,128]{2,1,0:T(8,128)S(1)}, f32[4,136,128]{2,1,0:T(8,128)S(1)}, u32[]{:S(2)}, u32[]{:S(2)}) collective-permute-start(f32[4,136,128]{2,1,0:T(8,128)S(1)} %copy-done.4), channel_id=1, source_target_pairs={{0,8},{8,0},{1,9},{9,1},{2,10},{10,2},{3,11},{11,3},{4,12},{12,4},... | collective-permute-start | bytes 835592 | tf_op jit(solution)/shard_map/ppermute | solution.py:558
  38.1 3.0 %attn_mine.1 = (f32[512,1024]{1,0:T(8,128)S(1)}, f32[512,1024]{1,0:T(8,128)S(1)}, bf16[512,2048]{1,0:T(8,128)(2,1)S(1)}, f32[8,128,128]{2,1,0:T(8,128)S(1)}, f32...) custom-call(s32[1]{0:T(128)} %bitcast.core_ref.lead_ref, ...), custom_call_target="tpu_custom_call" | custom-call | tf_op jit(solution)/shard_map/attn_mine/pallas_call | solution.py:569
  41.1 1.3 %attn_other.1 = (f32[512,1024]{1,0:T(8,128)S(1)}, f32[8,128,128]{2,1,0:T(8,128)S(1)}, f32[8,8,128]{2,1,0:T(8,128)S(1)}) custom-call(s32[1]{0:T(128)} %bitcast.core_ref.lead_ref, f32[4,128,128]{2,1,0:T(8,128)S(1)} %collective-permute-done.1.chip_ref, ...), custom_call_target="tpu_custom_call", output_to_operand_aliasing={{0}: (8, {}), {1}: (9, {})} | custom-call | tf_op jit(solution)/shard_map/attn_other/pallas_call | solution.py:569
  42.4 14.9 %all_to_all.25.sums_ref = f32[8,8,128]{2,1,0:T(8,128)S(1)} all-to-all(f32[8,8,128]{2,1,0:T(8,128)S(1)} %get-tuple-element.103), channel_id=1, replica_groups=mesh['x'=4,'y'=4,'c'=2,'tp'=8] {'tp'}, dimensions={0} | all-to-all | bytes 65536 | tf_op jit(solution)/shard_map/all_to_all | solution.py:658
  58.0 2.0 %collective-permute-start.3 = (f32[4,136,128]{2,1,0:T(8,128)S(1)}, f32[4,136,128]{2,1,0:T(8,128)S(1)}, u32[]{:S(2)}, u32[]{:S(2)}) collective-permute-start(f32[4,136,128]{2,1,0:T(8,128)S(1)} %get-tuple-element.111), channel_id=1, source_target_pairs={{0,8},{8,0},{1,9},{9,1},{2,10},{10,2},{3,11},{11,3},{4,12},{12,4},... | collective-permute-start | bytes 835592 | tf_op jit(solution)/shard_map/ppermute | solution.py:558
  60.1 1.5 %grad_mine.1 = (bf16[512,1024]{1,0:T(8,128)(2,1)}, f32[8,128]{1,0:T(8,128)}, f32[4,136,128]{2,1,0:T(8,128)S(1)}) custom-call(s32[1]{0:T(128)} %bitcast.core_ref.lead_ref, f32[512,128]{1,0:T(8,128)S(1)} %get-tuple-element.106.scale_ref, f32[512,128]{1,0:T(8,128)S(1)} %get-tuple-element.107.center_ref, f32[8,128]{1,0:T(8,128)S(1)} %get-tuple-element.108.table_ref, ...), custom_call_target="tpu_custom_call" | custom-call | tf_op jit(solution)/shard_map/grad_mine/pallas_call | solution.py:569
  61.6 0.9 combine.3
  62.6 3.6 %all-to-all-start.3 = ((f32[16,40,128]{2,1,0:T(8,128)}), f32[16,40,128]{2,1,0:T(8,128)S(1)}, u32[]{:S(2)}, u32[]{:S(2)}) async-start(f32[16,40,128]{2,1,0:T(8,128)} %get-tuple-element.112), calls=%async_computation.3 | async-start | bytes 655360 | tf_op jit(solution)/shard_map/all_to_all | solution.py:562
  66.1 9.3 %back.1 = (bf16[512,1024]{1,0:T(8,128)(2,1)}, f32[512,1024]{1,0:T(8,128)}) custom-call(f32[8,512]{1,0:T(8,128)} %copy-done.2, bf16[512,1024]{1,0:T(8,128)(2,1)} %q_hbm.5, bf16[512,1024]{1,0:T(8,128)(2,1)} %k_hbm.7, bf16[512,1024]{1,0:T(8,128)(2,1)} %v_hbm.7, bf16[512,1024]{1,0:T(8,128)(2,1)} %get-tuple-element.122.grad_hbm, f32[8,128,128]{2,1,0:T(8,128)} %copy-done.1), custom_call_target="tpu_custom_call" | custom-call | tf_op jit(solution)/shard_map/back/pallas_call | solution.py:569
  76.2 6.6 %all-to-all-start.4 = ((f32[16,32,128]{2,1,0:T(8,128)}), f32[16,32,128]{2,1,0:T(8,128)S(1)}, u32[]{:S(2)}, u32[]{:S(2)}) async-start(f32[16,32,128]{2,1,0:T(8,128)} %scan.3), calls=%async_computation.4 | async-start | bytes 524288 | tf_op jit(solution)/shard_map/all_to_all | solution.py:562
  82.9 3.7 %gate.1 = (bf16[512,1024]{1,0:T(8,128)(2,1)}, bf16[512,1024]{1,0:T(8,128)(2,1)}) custom-call(f32[8,128]{1,0:T(8,128)} %get-tuple-element.124.table_hbm, f32[512,1024]{1,0:T(8,128)} %copy-done, bf16[512,1024]{1,0:T(8,128)(2,1)} %gate_hbm.3, bf16[512,1024]{1,0:T(8,128)(2,1)} %up_hbm.3), custom_call_target="tpu_custom_call" | custom-call | tf_op jit(solution)/shard_map/gate/pallas_call | solution.py:569
  86.6 4.6 %value.1.value_part_hbm = f32[512,1024]{1,0:T(8,128)} custom-call(bf16[512,1024]{1,0:T(8,128)(2,1)} %get-tuple-element.122.grad_hbm, bf16[8,512,512]{2,1,0:T(8,128)(2,1)} %get-tuple-element.123.probs_hbm), custom_call_target="tpu_custom_call" | custom-call | tf_op jit(solution)/shard_map/value/pallas_call | solution.py:569
  91.2 1.1 %collective-permute-start.5 = (f32[4,136,128]{2,1,0:T(8,128)S(1)}, f32[4,136,128]{2,1,0:T(8,128)S(1)}, u32[]{:S(2)}, u32[]{:S(2)}) collective-permute-start(f32[4,136,128]{2,1,0:T(8,128)S(1)} %copy-done.3), channel_id=1, source_target_pairs={{0,8},{8,0},{1,9},{9,1},{2,10},{10,2},{3,11},{11,3},{4,12},{12,4},... | collective-permute-start | bytes 835592 | tf_op jit(solution)/shard_map/ppermute | solution.py:558
  92.3 3.0 %final_mine.1 = (bf16[512,512]{1,0:T(8,128)(2,1)S(1)}, bf16[512,512]{1,0:T(8,128)(2,1)S(1)}, bf16[512,512]{1,0:T(8,128)(2,1)S(1)}, bf16[512,512]{1,0:T(8,128)(2,...) custom-call(s32[1]{0:T(128)} %bitcast.core_ref.lead_ref, ...), custom_call_target="tpu_custom_call" | custom-call | tf_op jit(solution)/shard_map/final_mine/pallas_call | solution.py:569
  95.3 1.6 %final_other.1 = (bf16[512,1024]{1,0:T(8,128)(2,1)}, bf16[512,1024]{1,0:T(8,128)(2,1)}) custom-call(s32[1]{0:T(128)} %bitcast.core_ref.lead_ref, f32[4,128,128]{2,1,0:T(8,128)S(1)} %collective-permute-done.4.chip_ref, f32[4,136,128]{2,1,0:T(8,128)S(1)} %collective-permute-done.5.lead_ref, f32[8,512]{1,0:T(8,128)S(1)} %get-tuple-element.135.within_ref, ...), custom_call_target="tpu_custom_call" | custom-call | tf_op jit(solution)/shard_map/final_other/pallas_call | solution.py:569
  (24 shorter events, 3.0 us)
Async XLA Ops:
  2.7 10.5 %copy-start.2 = (f32[8,512]{1,0:T(8,128)}, f32[8,512]{1,0:T(8,128)S(1)}, u32[]{:S(2)}) copy-start(f32[8,512]{1,0:T(8,128)S(1)} %get-tuple-element.87.within_ref.within_hbm) | copy-start | bytes 49156
  2.7 4.5 %collective-permute-start = (f32[4,136,128]{2,1,0:T(8,128)S(1)}, f32[4,136,128]{2,1,0:T(8,128)S(1)}, u32[]{:S(2)}, u32[]{:S(2)}) collective-permute-start(f32[4,136,128]{2,1,0:T(8,128)S(1)} %get-tuple-element.78), channel_id=1, source_target_pairs={{0,8},{8,0},{1,9},{9,1},{2,10},{10,2},{3,11},{11,3},{4,12},{12,4},... | collective-permute-start | bytes 835592 | tf_op jit(solution)/shard_map/ppermute | solution.py:558
  8.2 13.0 %all-to-all-start = ((f32[16,40,128]{2,1,0:T(8,128)}), f32[16,40,128]{2,1,0:T(8,128)S(1)}, u32[]{:S(2)}, u32[]{:S(2)}) async-start(f32[16,40,128]{2,1,0:T(8,128)} %get-tuple-element.79), calls=%async_computation | async-start | bytes 655360 | tf_op jit(solution)/shard_map/all_to_all | solution.py:562
  21.2 14.6 %copy-start.4 = (f32[4,136,128]{2,1,0:T(8,128)S(1)}, f32[4,136,128]{2,1,0:T(8,128)}, u32[]{:S(2)}) copy-start(f32[4,136,128]{2,1,0:T(8,128)} %get-tuple-element.91) | copy-start | bytes 835588
  21.9 13.9 %all-to-all-start.1 = ((f32[16,32,128]{2,1,0:T(8,128)}), f32[16,32,128]{2,1,0:T(8,128)S(1)}, u32[]{:S(2)}, u32[]{:S(2)}) async-start(f32[16,32,128]{2,1,0:T(8,128)} %scan.2), calls=%async_computation.1 | async-start | bytes 524288 | tf_op jit(solution)/shard_map/all_to_all | solution.py:562
  35.8 5.3 %collective-permute-start.2 = (f32[4,136,128]{2,1,0:T(8,128)S(1)}, f32[4,136,128]{2,1,0:T(8,128)S(1)}, u32[]{:S(2)}, u32[]{:S(2)}) collective-permute-start(f32[4,136,128]{2,1,0:T(8,128)S(1)} %copy-done.4), channel_id=1, source_target_pairs={{0,8},{8,0},{1,9},{9,1},{2,10},{10,2},{3,11},{11,3},{4,12},{12,4},... | collective-permute-start | bytes 835592 | tf_op jit(solution)/shard_map/ppermute | solution.py:558
  38.1 3.0 %collective-permute-start.1 = (f32[4,128,128]{2,1,0:T(8,128)S(1)}, f32[4,128,128]{2,1,0:T(8,128)S(1)}, u32[]{:S(2)}, u32[]{:S(2)}) collective-permute-start(f32[4,128,128]{2,1,0:T(8,128)S(1)} %bitcast.6), channel_id=1, source_target_pairs={{0,8},{8,0},{1,9},{9,1},{2,10},{10,2},{3,11},{11,3},{4,12},{12,4},... | collective-permute-start | bytes 786440 | tf_op jit(solution)/shard_map/ppermute | solution.py:558
  42.3 15.7 %copy-start.1 = (f32[8,128,128]{2,1,0:T(8,128)}, f32[8,128,128]{2,1,0:T(8,128)S(1)}, u32[]{:S(2)}) copy-start(f32[8,128,128]{2,1,0:T(8,128)S(1)} %get-tuple-element.114.state_hbm) | copy-start | bytes 1572868
  42.3 17.7 %copy-start = (f32[512,1024]{1,0:T(8,128)}, f32[512,1024]{1,0:T(8,128)S(1)}, u32[]{:S(2)}) copy-start(f32[512,1024]{1,0:T(8,128)S(1)} %get-tuple-element.105.attn_ref.attn_hbm) | copy-start | bytes 6291460
  58.0 3.6 %collective-permute-start.3 = (f32[4,136,128]{2,1,0:T(8,128)S(1)}, f32[4,136,128]{2,1,0:T(8,128)S(1)}, u32[]{:S(2)}, u32[]{:S(2)}) collective-permute-start(f32[4,136,128]{2,1,0:T(8,128)S(1)} %get-tuple-element.111), channel_id=1, source_target_pairs={{0,8},{8,0},{1,9},{9,1},{2,10},{10,2},{3,11},{11,3},{4,12},{12,4},... | collective-permute-start | bytes 835592 | tf_op jit(solution)/shard_map/ppermute | solution.py:558
  62.6 12.9 %all-to-all-start.3 = ((f32[16,40,128]{2,1,0:T(8,128)}), f32[16,40,128]{2,1,0:T(8,128)S(1)}, u32[]{:S(2)}, u32[]{:S(2)}) async-start(f32[16,40,128]{2,1,0:T(8,128)} %get-tuple-element.112), calls=%async_computation.3 | async-start | bytes 655360 | tf_op jit(solution)/shard_map/all_to_all | solution.py:562
  76.2 15.0 %all-to-all-start.4 = ((f32[16,32,128]{2,1,0:T(8,128)}), f32[16,32,128]{2,1,0:T(8,128)S(1)}, u32[]{:S(2)}, u32[]{:S(2)}) async-start(f32[16,32,128]{2,1,0:T(8,128)} %scan.3), calls=%async_computation.4 | async-start | bytes 524288 | tf_op jit(solution)/shard_map/all_to_all | solution.py:562
  86.6 4.6 %copy-start.3 = (f32[4,136,128]{2,1,0:T(8,128)S(1)}, f32[4,136,128]{2,1,0:T(8,128)}, u32[]{:S(2)}) copy-start(f32[4,136,128]{2,1,0:T(8,128)} %get-tuple-element.131) | copy-start | bytes 835588
  91.2 4.1 %collective-permute-start.5 = (f32[4,136,128]{2,1,0:T(8,128)S(1)}, f32[4,136,128]{2,1,0:T(8,128)S(1)}, u32[]{:S(2)}, u32[]{:S(2)}) collective-permute-start(f32[4,136,128]{2,1,0:T(8,128)S(1)} %copy-done.3), channel_id=1, source_target_pairs={{0,8},{8,0},{1,9},{9,1},{2,10},{10,2},{3,11},{11,3},{4,12},{12,4},... | collective-permute-start | bytes 835592 | tf_op jit(solution)/shard_map/ppermute | solution.py:558
  92.3 3.0 %collective-permute-start.4 = (f32[4,128,128]{2,1,0:T(8,128)S(1)}, f32[4,128,128]{2,1,0:T(8,128)S(1)}, u32[]{:S(2)}, u32[]{:S(2)}) collective-permute-start(f32[4,128,128]{2,1,0:T(8,128)S(1)} %bitcast.4), channel_id=1, source_target_pairs={{0,8},{8,0},{1,9},{9,1},{2,10},{10,2},{3,11},{11,3},{4,12},{12,4},... | collective-permute-start | bytes 786440 | tf_op jit(solution)/shard_map/ppermute | solution.py:558

commit v4 on v3

--- a/solution.py
+++ b/solution.py
@@ -89,6 +89,17 @@
         return carry
 
     lax.fori_loop(0, heads, step, 0)
+
+
+def each_pair(heads, before, work, after):
+    def step(pair, carry):
+        both = (2 * pair, 2 * pair + 1)
+        for stage in (before, work, after):
+            for head in both:
+                stage(head)
+        return carry
+
+    lax.fori_loop(0, heads // 2, step, 0)
 
 
 def head_copies(arrays, sems, head):
@@ -174,12 +185,26 @@
     wait(made)
 
 
-def decay_block(within, column, first, size, width):
-    gap = jnp.concatenate([column[first : first + size]] * (width // HEAD), axis=1)
-    gap = gap - within[:, :width]
-    rows = first + lax.broadcasted_iota(jnp.int32, gap.shape, 0)
-    cols = lax.broadcasted_iota(jnp.int32, gap.shape, 1)
-    return jnp.where(rows >= cols, jnp.exp(jnp.minimum(gap, 0.0)), 0.0)
+def decayed(scores, first, within, column):
+    width = scores.shape[1]
+    rows = lax.broadcasted_iota(jnp.int32, (HEAD, HEAD), 0)
+    cols = lax.broadcasted_iota(jnp.int32, (HEAD, HEAD), 1)
+    bands = []
+    for start_at in range(first, width, HEAD):
+        band = scores[start_at - first : start_at - first + HEAD]
+        own = column[start_at : start_at + HEAD]
+        pieces = []
+        if start_at:
+            edge = within[:, start_at - 1 : start_at]
+            grow = jnp.concatenate([jnp.exp(own - edge)] * (start_at // HEAD), axis=1)
+            pieces.append(band[:, :start_at] * jnp.exp(edge - within[:, :start_at]) * grow)
+        gap = own - within[:, start_at : start_at + HEAD]
+        inside = jnp.where(rows >= cols, jnp.exp(jnp.minimum(gap, 0.0)), 0.0)
+        pieces.append(band[:, start_at : start_at + HEAD] * inside)
+        if start_at + HEAD < width:
+            pieces.append(jnp.zeros((HEAD, width - start_at - HEAD), F32))
+        bands.append(jnp.concatenate(pieces, axis=1).astype(BF16))
+    return jnp.concatenate(bands, axis=0)
 
 
 def inside_kernel(
@@ -207,17 +232,14 @@
     def one(h):
         within = within_ref[pl.ds(h, 1), :]
         column = as_column(within)
-        wait(head_copies(loads, in_sems, h))
         q, k, v = q_ref[:, lanes(h)], k_ref[:, lanes(h)], v_ref[:, lanes(h)]
         for first in (0, size):
             width = first + size
-            scores = dot(q[first:width], k[0:width], NT)
-            probs = (scores * decay_block(within, column, first, size, width)).astype(BF16)
+            probs = decayed(dot(q[first:width], k[0:width], NT), first, within, column)
             probs_ref[h, first:width, 0:width] = probs
             intra_ref[first:width, lanes(h)] = dot(probs, v[0:width], NN)
-        start(results(h))
-
-    each_head(heads, one)
+
+    each_pair(heads, lambda h: wait(head_copies(loads, in_sems, h)), one, lambda h: start(results(h)))
     each_head(heads, lambda h: wait(results(h)))
 
 
@@ -235,15 +257,16 @@
 
     def one(h):
         grow = as_column(jnp.exp(within_ref[pl.ds(h, 1), :]))
-        wait(head_copies(loads, in_sems, h))
         dnorm_ref[:, lanes(h)] = up_ref[:, lanes(h)].astype(F32) * sigmoid(
             gate_ref[:, lanes(h)].astype(F32)
         )
         grown = q_ref[:, lanes(h)].astype(F32) * grow
         grown_ref[:, lanes(h, 2)] = jnp.concatenate(halves(grown), axis=1)
-        start(head_copies(stores, out_sems, h))
-
-    each_head(heads, one)
+
+    each_pair(
+        heads, lambda h: wait(head_copies(loads, in_sems, h)), one,
+        lambda h: start(head_copies(stores, out_sems, h)),
+    )
     each_head(heads, lambda h: wait(head_copies(stores, out_sems, h)))
 
 
@@ -379,34 +402,6 @@
     wait(made + stores)
 
 
-def gate_kernel(
-    table_hbm, attn_hbm, gate_hbm, up_hbm, output_hbm, gate_grad_hbm,
-    table_ref, attn_ref, gate_ref, up_ref, output_ref, gate_grad_ref, scale_ref, sem, in_sems, out_sems,
-):
-    heads = in_sems.shape[1]
-    small = copies([(table_hbm, table_ref)], sem)
-    start(small)
-    loads = [(attn_hbm, attn_ref, 1), (gate_hbm, gate_ref, 1), (up_hbm, up_ref, 1)]
-    stores = [(output_ref, output_hbm, 1), (gate_grad_ref, gate_grad_hbm, 1)]
-    each_head(heads, lambda h: start(head_copies(loads, in_sems, h)))
-    wait(small)
-    for i in range(4):
-        scale_ref[i * HEAD : (i + 1) * HEAD] = as_column(table_ref[i : i + 1])
-
-    def one(h):
-        wait(head_copies(loads, in_sems, h))
-        normed = attn_ref[:, lanes(h)] * scale_ref[...]
-        sig = sigmoid(gate_ref[:, lanes(h)].astype(F32))
-        output_ref[:, lanes(h)] = (normed * sig).astype(BF16)
-        gate_grad_ref[:, lanes(h)] = (
-            up_ref[:, lanes(h)].astype(F32) * normed * sig * (1.0 - sig)
-        ).astype(BF16)
-        start(head_copies(stores, out_sems, h))
-
-    each_head(heads, one)
-    each_head(heads, lambda h: wait(head_copies(stores, out_sems, h)))
-
-
 def back_kernel(
     within_hbm, q_hbm, k_hbm, v_hbm, grad_hbm, state_hbm, query_grad_hbm, key_hbm,
     within_ref, q_ref, k_ref, v_ref, grad_ref, state_ref, query_grad_ref, key_ref, sem, in_sems, out_sems,
@@ -428,15 +423,13 @@
         within = within_ref[pl.ds(h, 1), :]
         column = as_column(within)
         grow = jnp.exp(column)
-        wait(head_copies(loads, in_sems, h))
         at = lanes(h)
         q, k, v = q_ref[:, at], k_ref[:, at], v_ref[:, at]
         state = jnp.concatenate(halves(state_ref[h]), axis=0)
         for first in (0, size):
             width = first + size
             grad = grad_ref[first:width, at]
-            pgrad = dot(grad, v[0:width], NT)
-            pgrad = (pgrad * decay_block(within, column, first, size, width)).astype(BF16)
+            pgrad = decayed(dot(grad, v[0:width], NT), first, within, column)
             inter = dot(jnp.concatenate([grad, grad], axis=1), state, NN)
             query_grad_ref[first:width, at] = (
                 dot(pgrad, k[0:width], NN) + grow[first:width] * inter
@@ -447,41 +440,59 @@
             else:
                 key_ref[0:first, at] += key_part[0:first]
                 key_ref[first:width, at] = key_part[first:width]
-        start(head_copies(stores, out_sems, h))
-
-    each_head(heads, one)
+
+    each_pair(
+        heads, lambda h: wait(head_copies(loads, in_sems, h)), one,
+        lambda h: start(head_copies(stores, out_sems, h)),
+    )
     each_head(heads, lambda h: wait(head_copies(stores, out_sems, h)))
 
 
-def value_kernel(
-    grad_hbm, probs_hbm, value_hbm, grad_ref, probs_ref, value_ref, in_sems, out_sems
+def value_gate_kernel(
+    table_hbm, attn_hbm, gate_hbm, up_hbm, grad_hbm, probs_hbm, value_hbm, output_hbm, gate_grad_hbm,
+    table_ref, attn_ref, gate_ref, up_ref, grad_ref, probs_ref, value_ref, output_ref, gate_grad_ref,
+    scale_ref, sem, in_sems, out_sems,
 ):
     heads = probs_ref.shape[0]
     tokens = grad_ref.shape[0]
     size = tokens // 2
+    small = copies([(table_hbm, table_ref)], sem)
+    start(small)
 
     def loads(h):
         upper, lower = pl.ds(0, size), pl.ds(size, size)
         pairs = [
-            (grad_hbm.at[:, lanes(h)], grad_ref.at[:, lanes(h)]),
             (probs_hbm.at[h, upper, upper], probs_ref.at[h, upper, upper]),
             (probs_hbm.at[h, lower], probs_ref.at[h, lower]),
         ]
+        pairs += [
+            (a.at[:, lanes(h)], b.at[:, lanes(h)])
+            for a, b in (
+                (grad_hbm, grad_ref), (attn_hbm, attn_ref), (gate_hbm, gate_ref), (up_hbm, up_ref)
+            )
+        ]
         return [pltpu.make_async_copy(a, b, in_sems.at[i, h]) for i, (a, b) in enumerate(pairs)]
 
-    stores = [(value_ref, value_hbm, 1)]
+    stores = [(value_ref, value_hbm, 1), (output_ref, output_hbm, 1), (gate_grad_ref, gate_grad_hbm, 1)]
     each_head(heads, lambda h: start(loads(h)))
+    wait(small)
+    for i in range(4):
+        scale_ref[i * HEAD : (i + 1) * HEAD] = as_column(table_ref[i : i + 1])
 
     def one(h):
-        wait(loads(h))
         at = lanes(h)
         late = dot(probs_ref[h, size:tokens, :], grad_ref[size:tokens, at], TN)
         early = dot(probs_ref[h, 0:size, 0:size], grad_ref[0:size, at], TN)
+        normed = attn_ref[:, at] * scale_ref[...]
+        sig = sigmoid(gate_ref[:, at].astype(F32))
+        output_ref[:, at] = (normed * sig).astype(BF16)
+        gate_grad_ref[:, at] = (up_ref[:, at].astype(F32) * normed * sig * (1.0 - sig)).astype(BF16)
         value_ref[0:size, at] = late[0:size] + early
         value_ref[size:tokens, at] = late[size:tokens]
-        start(head_copies(stores, out_sems, h))
-
-    each_head(heads, one)
+
+    each_pair(
+        heads, lambda h: wait(loads(h)), one, lambda h: start(head_copies(stores, out_sems, h))
+    )
     each_head(heads, lambda h: wait(head_copies(stores, out_sems, h)))
 
 
@@ -677,12 +688,10 @@
     )
     chip_state, grad, table = lax.optimization_barrier((scanned(chip_state, True), grad, table))
     chip_mine = spread(chip_state)
-    (value_part,) = call(
-        value_kernel, "value", (), (grad, probs), (), (wide,), (narrow, table_of, wide), ((3, heads), (1, heads))
-    )
-    output, gate_grad = call(
-        gate_kernel, "gate", (), (table, attn, gate, out_grad), (), (narrow, narrow),
-        (table_rows, wide, narrow, narrow, narrow, narrow, column), ((1,), (3, heads), (2, heads)),
+    value_part, output, gate_grad = call(
+        value_gate_kernel, "value_gate", (), (table, attn, gate, out_grad, grad, probs), (), (wide, narrow, narrow),
+        (table_rows, wide, narrow, narrow, narrow, table_of, wide, narrow, narrow, column),
+        ((1,), (6, heads), (3, heads)), mib=24,
     )
     chip_mine, value_part, output, gate_grad, mine = lax.optimization_barrier(
         (chip_mine, value_part, output, gate_grad, mine)

time: 97.9 us -> 95.1 us (0.971)
  Pallas kernels: 47 us -> 42.2 us
  waiting for transfers between devices: 3.76 us -> 6.86 us
  starting transfers between devices: 30.4 us -> 29.3 us
    pallas_call x17 -> x16, Pallas kernels: 47 us -> 42.2 us  [call(): pl.pallas_call(kernel, grid_spec=pltpu.PrefetchScalarGridSpec(num_scalar_...]
    all_to_all x4, waiting for transfers between devices: 3.37 us -> 6.47 us  [spread(): return lax.all_to_all(x, CHIPS, split_axis=0, concat_axis=0, tiled=True)]
    all_to_all x4, starting transfers between devices: 21.6 us -> 19.7 us  [spread(): return lax.all_to_all(x, CHIPS, split_axis=0, concat_axis=0, tiled=True)]
  transfers between devices with their start and end apart: 10 -> 10, of which waited for: 3 -> 5; matrix products, arithmetic and copies ran while one was open for 0% -> 0% of each run, Pallas kernels for 39% -> 35%
where the time goes in v4:
time: 95.1 us; the launch traced here: 94.1 us
  Pallas kernels  42.2 us (44%)
  starting transfers between devices  29.3 us (31%)
  blocking collectives  14.9 us (16%)
  waiting for transfers between devices  6.86 us (7%)
    pallas_call x16, Pallas kernels, call(): pl.pallas_call(kernel, grid_spec=pltpu.PrefetchScalarGridSpec(num_scalar_...  42.2 us
    all_to_all x4, starting transfers between devices, spread(): return lax.all_to_all(x, CHIPS, split_axis=0, concat_axis=0, tiled=True)  19.7 us
    all_to_all x1, blocking collectives, shards(): sums = lax.all_to_all(sums, 'tp', split_axis=0, concat_axis=0, tiled=True)  14.9 us
    ppermute x6, starting transfers between devices, swap(): return lax.ppermute(x, 'c', [(0, 1), (1, 0)])  9.64 us
    all_to_all x4, waiting for transfers between devices, spread(): return lax.all_to_all(x, CHIPS, split_axis=0, concat_axis=0, tiled=True)  6.47 us
  transfers between devices with their start and end apart: 10, of which 5 were waited for; matrix products, arithmetic and copies ran while one was open for 0% of the time, Pallas kernels for 35%

profile of v4, /device:TPU:1, one launch (start us, length us, event | category | flops | bytes accessed | tf_op | source)
XLA Modules:
  0.0 94.1 jit_solution(16002429174260586503)
XLA Ops:
  0.6 2.1 %local_other.1 = (f32[8,512]{1,0:T(8,128)S(1)}, f32[4,136,128]{2,1,0:T(8,128)S(1)}, bf16[512,512]{1,0:T(8,128)(2,1)S(1)}, bf16[512,512]{1,0:T(8,128)(2,1)S(1)}) custom-call(s32[1]{0:T(128)} %bitcast.core_ref.lead_ref, f32[8,512]{1,0:T(8,128)} %bitcast.8, bf16[512,1024]{1,0:T(8,128)(2,1)} %k_hbm.7, bf16[512,1024]{1,0:T(8,128)(2,1)} %v_hbm.7), custom_call_target="tpu_custom_call" | custom-call | tf_op jit(solution)/shard_map/local_other/pallas_call | solution.py:580
  2.7 3.3 %collective-permute-start = (f32[4,136,128]{2,1,0:T(8,128)S(1)}, f32[4,136,128]{2,1,0:T(8,128)S(1)}, u32[]{:S(2)}, u32[]{:S(2)}) collective-permute-start(f32[4,136,128]{2,1,0:T(8,128)S(1)} %get-tuple-element.79), channel_id=1, source_target_pairs={{0,8},{8,0},{1,9},{9,1},{2,10},{10,2},{3,11},{11,3},{4,12},{12,4},... | collective-permute-start | bytes 835592 | tf_op jit(solution)/shard_map/ppermute | solution.py:569
  7.3 0.9 combine.2
  8.2 5.0 %all-to-all-start = ((f32[16,40,128]{2,1,0:T(8,128)}), f32[16,40,128]{2,1,0:T(8,128)S(1)}, u32[]{:S(2)}, u32[]{:S(2)}) async-start(f32[16,40,128]{2,1,0:T(8,128)} %get-tuple-element.80), calls=%async_computation | async-start | bytes 655360 | tf_op jit(solution)/shard_map/all_to_all | solution.py:573
  13.3 6.3 %inside.1 = (bf16[8,512,512]{2,1,0:T(8,128)(2,1)}, f32[512,1024]{1,0:T(8,128)}) custom-call(f32[8,512]{1,0:T(8,128)} %copy-done.2, bf16[512,1024]{1,0:T(8,128)(2,1)} %q_hbm.5, bf16[512,1024]{1,0:T(8,128)(2,1)} %k_hbm.7, bf16[512,1024]{1,0:T(8,128)(2,1)} %v_hbm.7), custom_call_target="tpu_custom_call" | custom-call | tf_op jit(solution)/shard_map/inside/pallas_call | solution.py:580
  19.6 1.6 %all-to-all-done.refs_0_ = f32[16,40,128]{2,1,0:T(8,128)S(1)} async-done(((f32[16,40,128]{2,1,0:T(8,128)}), f32[16,40,128]{2,1,0:T(8,128)S(1)}, u32[]{:S(2)}, u32[]{:S(2)}) %all-to-all-start) | async-done | bytes 327712 | tf_op jit(solution)/shard_map/all_to_all | solution.py:573
  21.9 5.1 %all-to-all-start.1 = ((f32[16,32,128]{2,1,0:T(8,128)}), f32[16,32,128]{2,1,0:T(8,128)S(1)}, u32[]{:S(2)}, u32[]{:S(2)}) async-start(f32[16,32,128]{2,1,0:T(8,128)} %scan.2), calls=%async_computation.1 | async-start | bytes 524288 | tf_op jit(solution)/shard_map/all_to_all | solution.py:573
  27.0 4.2 %prepare.1 = (f32[512,1024]{1,0:T(8,128)}, bf16[512,2048]{1,0:T(8,128)(2,1)}) custom-call(f32[8,512]{1,0:T(8,128)} %copy-done.2, bf16[512,1024]{1,0:T(8,128)(2,1)} %q_hbm.5, bf16[512,1024]{1,0:T(8,128)(2,1)} %gate_hbm.3, bf16[512,1024]{1,0:T(8,128)(2,1)} %up_hbm.3), custom_call_target="tpu_custom_call" | custom-call | tf_op jit(solution)/shard_map/prepare/pallas_call | solution.py:580
  31.2 3.2 %all-to-all-done.1 = f32[16,32,128]{2,1,0:T(8,128)S(1)} async-done(((f32[16,32,128]{2,1,0:T(8,128)}), f32[16,32,128]{2,1,0:T(8,128)S(1)}, u32[]{:S(2)}, u32[]{:S(2)}) %all-to-all-start.1) | async-done | bytes 262176 | tf_op jit(solution)/shard_map/all_to_all | solution.py:573
  34.5 2.3 %collective-permute-start.2 = (f32[4,136,128]{2,1,0:T(8,128)S(1)}, f32[4,136,128]{2,1,0:T(8,128)S(1)}, u32[]{:S(2)}, u32[]{:S(2)}) collective-permute-start(f32[4,136,128]{2,1,0:T(8,128)S(1)} %copy-done.4), channel_id=1, source_target_pairs={{0,8},{8,0},{1,9},{9,1},{2,10},{10,2},{3,11},{11,3},{4,12},{12,4},... | collective-permute-start | bytes 835592 | tf_op jit(solution)/shard_map/ppermute | solution.py:569
  36.8 3.0 %attn_mine.1 = (f32[512,1024]{1,0:T(8,128)S(1)}, f32[512,1024]{1,0:T(8,128)S(1)}, bf16[512,2048]{1,0:T(8,128)(2,1)S(1)}, f32[8,128,128]{2,1,0:T(8,128)S(1)}, f32...) custom-call(s32[1]{0:T(128)} %bitcast.core_ref.lead_ref, ...), custom_call_target="tpu_custom_call" | custom-call | tf_op jit(solution)/shard_map/attn_mine/pallas_call | solution.py:580
  39.8 1.3 %attn_other.1 = (f32[512,1024]{1,0:T(8,128)S(1)}, f32[8,128,128]{2,1,0:T(8,128)S(1)}, f32[8,8,128]{2,1,0:T(8,128)S(1)}) custom-call(s32[1]{0:T(128)} %bitcast.core_ref.lead_ref, f32[4,128,128]{2,1,0:T(8,128)S(1)} %collective-permute-done.1.chip_ref, ...), custom_call_target="tpu_custom_call", output_to_operand_aliasing={{0}: (8, {}), {1}: (9, {})} | custom-call | tf_op jit(solution)/shard_map/attn_other/pallas_call | solution.py:580
  41.0 14.9 %all_to_all.25.sums_ref = f32[8,8,128]{2,1,0:T(8,128)S(1)} all-to-all(f32[8,8,128]{2,1,0:T(8,128)S(1)} %get-tuple-element.104), channel_id=1, replica_groups=mesh['x'=4,'y'=4,'c'=2,'tp'=8] {'tp'}, dimensions={0} | all-to-all | bytes 65536 | tf_op jit(solution)/shard_map/all_to_all | solution.py:669
  56.7 2.0 %collective-permute-start.3 = (f32[4,136,128]{2,1,0:T(8,128)S(1)}, f32[4,136,128]{2,1,0:T(8,128)S(1)}, u32[]{:S(2)}, u32[]{:S(2)}) collective-permute-start(f32[4,136,128]{2,1,0:T(8,128)S(1)} %get-tuple-element.112), channel_id=1, source_target_pairs={{0,8},{8,0},{1,9},{9,1},{2,10},{10,2},{3,11},{11,3},{4,12},{12,4},... | collective-permute-start | bytes 835592 | tf_op jit(solution)/shard_map/ppermute | solution.py:569
  58.8 1.5 %grad_mine.1 = (bf16[512,1024]{1,0:T(8,128)(2,1)}, f32[8,128]{1,0:T(8,128)}, f32[4,136,128]{2,1,0:T(8,128)S(1)}) custom-call(s32[1]{0:T(128)} %bitcast.core_ref.lead_ref, f32[512,128]{1,0:T(8,128)S(1)} %get-tuple-element.107.scale_ref, f32[512,128]{1,0:T(8,128)S(1)} %get-tuple-element.108.center_ref, f32[8,128]{1,0:T(8,128)S(1)} %get-tuple-element.109.table_ref, ...), custom_call_target="tpu_custom_call" | custom-call | tf_op jit(solution)/shard_map/grad_mine/pallas_call | solution.py:580
  60.3 0.9 combine.3
  61.2 3.6 %all-to-all-start.3 = ((f32[16,40,128]{2,1,0:T(8,128)}), f32[16,40,128]{2,1,0:T(8,128)S(1)}, u32[]{:S(2)}, u32[]{:S(2)}) async-start(f32[16,40,128]{2,1,0:T(8,128)} %get-tuple-element.113), calls=%async_computation.3 | async-start | bytes 655360 | tf_op jit(solution)/shard_map/all_to_all | solution.py:573
  64.8 7.8 %back.1 = (bf16[512,1024]{1,0:T(8,128)(2,1)}, f32[512,1024]{1,0:T(8,128)}) custom-call(f32[8,512]{1,0:T(8,128)} %copy-done.2, bf16[512,1024]{1,0:T(8,128)(2,1)} %q_hbm.5, bf16[512,1024]{1,0:T(8,128)(2,1)} %k_hbm.7, bf16[512,1024]{1,0:T(8,128)(2,1)} %v_hbm.7, bf16[512,1024]{1,0:T(8,128)(2,1)} %get-tuple-element.124.grad_hbm, f32[8,128,128]{2,1,0:T(8,128)} %copy-done.1), custom_call_target="tpu_custom_call" | custom-call | tf_op jit(solution)/shard_map/back/pallas_call | solution.py:580
  74.0 6.0 %all-to-all-start.4 = ((f32[16,32,128]{2,1,0:T(8,128)}), f32[16,32,128]{2,1,0:T(8,128)S(1)}, u32[]{:S(2)}, u32[]{:S(2)}) async-start(f32[16,32,128]{2,1,0:T(8,128)} %scan.3), calls=%async_computation.4 | async-start | bytes 524288 | tf_op jit(solution)/shard_map/all_to_all | solution.py:573
  80.0 6.4 %value_gate.1 = (f32[512,1024]{1,0:T(8,128)}, bf16[512,1024]{1,0:T(8,128)(2,1)}, bf16[512,1024]{1,0:T(8,128)(2,1)}) custom-call(f32[8,128]{1,0:T(8,128)} %get-tuple-element.123.table_hbm, f32[512,1024]{1,0:T(8,128)} %copy-done, bf16[512,1024]{1,0:T(8,128)(2,1)} %gate_hbm.3, bf16[512,1024]{1,0:T(8,128)(2,1)} %up_hbm.3, ...), custom_call_target="tpu_custom_call" | custom-call | tf_op jit(solution)/shard_map/value_gate/pallas_call | solution.py:580
  86.5 1.0 %all-to-all-done.4 = f32[16,32,128]{2,1,0:T(8,128)S(1)} async-done(((f32[16,32,128]{2,1,0:T(8,128)}), f32[16,32,128]{2,1,0:T(8,128)S(1)}, u32[]{:S(2)}, u32[]{:S(2)}) %all-to-all-start.4) | async-done | bytes 262176 | tf_op jit(solution)/shard_map/all_to_all | solution.py:573
  87.5 2.0 %collective-permute-start.5 = (f32[4,136,128]{2,1,0:T(8,128)S(1)}, f32[4,136,128]{2,1,0:T(8,128)S(1)}, u32[]{:S(2)}, u32[]{:S(2)}) collective-permute-start(f32[4,136,128]{2,1,0:T(8,128)S(1)} %copy-done.3), channel_id=1, source_target_pairs={{0,8},{8,0},{1,9},{9,1},{2,10},{10,2},{3,11},{11,3},{4,12},{12,4},... | collective-permute-start | bytes 835592 | tf_op jit(solution)/shard_map/ppermute | solution.py:569
  89.5 3.0 %final_mine.1 = (bf16[512,512]{1,0:T(8,128)(2,1)S(1)}, bf16[512,512]{1,0:T(8,128)(2,1)S(1)}, bf16[512,512]{1,0:T(8,128)(2,1)S(1)}, bf16[512,512]{1,0:T(8,128)(2,...) custom-call(s32[1]{0:T(128)} %bitcast.core_ref.lead_ref, ...), custom_call_target="tpu_custom_call" | custom-call | tf_op jit(solution)/shard_map/final_mine/pallas_call | solution.py:580
  92.5 1.6 %final_other.1 = (bf16[512,1024]{1,0:T(8,128)(2,1)}, bf16[512,1024]{1,0:T(8,128)(2,1)}) custom-call(s32[1]{0:T(128)} %bitcast.core_ref.lead_ref, f32[4,128,128]{2,1,0:T(8,128)S(1)} %collective-permute-done.4.chip_ref, f32[4,136,128]{2,1,0:T(8,128)S(1)} %collective-permute-done.5.lead_ref, f32[8,512]{1,0:T(8,128)S(1)} %get-tuple-element.137.within_ref, ...), custom_call_target="tpu_custom_call" | custom-call | tf_op jit(solution)/shard_map/final_other/pallas_call | solution.py:580
  (23 shorter events, 4.1 us)
Async XLA Ops:
  2.7 10.5 %copy-start.2 = (f32[8,512]{1,0:T(8,128)}, f32[8,512]{1,0:T(8,128)S(1)}, u32[]{:S(2)}) copy-start(f32[8,512]{1,0:T(8,128)S(1)} %get-tuple-element.88.within_ref.within_hbm) | copy-start | bytes 49156
  2.7 4.5 %collective-permute-start = (f32[4,136,128]{2,1,0:T(8,128)S(1)}, f32[4,136,128]{2,1,0:T(8,128)S(1)}, u32[]{:S(2)}, u32[]{:S(2)}) collective-permute-start(f32[4,136,128]{2,1,0:T(8,128)S(1)} %get-tuple-element.79), channel_id=1, source_target_pairs={{0,8},{8,0},{1,9},{9,1},{2,10},{10,2},{3,11},{11,3},{4,12},{12,4},... | collective-permute-start | bytes 835592 | tf_op jit(solution)/shard_map/ppermute | solution.py:569
  8.2 13.0 %all-to-all-start = ((f32[16,40,128]{2,1,0:T(8,128)}), f32[16,40,128]{2,1,0:T(8,128)S(1)}, u32[]{:S(2)}, u32[]{:S(2)}) async-start(f32[16,40,128]{2,1,0:T(8,128)} %get-tuple-element.80), calls=%async_computation | async-start | bytes 655360 | tf_op jit(solution)/shard_map/all_to_all | solution.py:573
  21.2 13.3 %copy-start.4 = (f32[4,136,128]{2,1,0:T(8,128)S(1)}, f32[4,136,128]{2,1,0:T(8,128)}, u32[]{:S(2)}) copy-start(f32[4,136,128]{2,1,0:T(8,128)} %get-tuple-element.92) | copy-start | bytes 835588
  21.9 12.5 %all-to-all-start.1 = ((f32[16,32,128]{2,1,0:T(8,128)}), f32[16,32,128]{2,1,0:T(8,128)S(1)}, u32[]{:S(2)}, u32[]{:S(2)}) async-start(f32[16,32,128]{2,1,0:T(8,128)} %scan.2), calls=%async_computation.1 | async-start | bytes 524288 | tf_op jit(solution)/shard_map/all_to_all | solution.py:573
  34.5 5.3 %collective-permute-start.2 = (f32[4,136,128]{2,1,0:T(8,128)S(1)}, f32[4,136,128]{2,1,0:T(8,128)S(1)}, u32[]{:S(2)}, u32[]{:S(2)}) collective-permute-start(f32[4,136,128]{2,1,0:T(8,128)S(1)} %copy-done.4), channel_id=1, source_target_pairs={{0,8},{8,0},{1,9},{9,1},{2,10},{10,2},{3,11},{11,3},{4,12},{12,4},... | collective-permute-start | bytes 835592 | tf_op jit(solution)/shard_map/ppermute | solution.py:569
  36.8 3.0 %collective-permute-start.1 = (f32[4,128,128]{2,1,0:T(8,128)S(1)}, f32[4,128,128]{2,1,0:T(8,128)S(1)}, u32[]{:S(2)}, u32[]{:S(2)}) collective-permute-start(f32[4,128,128]{2,1,0:T(8,128)S(1)} %bitcast.6), channel_id=1, source_target_pairs={{0,8},{8,0},{1,9},{9,1},{2,10},{10,2},{3,11},{11,3},{4,12},{12,4},... | collective-permute-start | bytes 786440 | tf_op jit(solution)/shard_map/ppermute | solution.py:569
  41.0 15.7 %copy-start.1 = (f32[8,128,128]{2,1,0:T(8,128)}, f32[8,128,128]{2,1,0:T(8,128)S(1)}, u32[]{:S(2)}) copy-start(f32[8,128,128]{2,1,0:T(8,128)S(1)} %get-tuple-element.115.state_hbm) | copy-start | bytes 1572868
  41.0 17.7 %copy-start = (f32[512,1024]{1,0:T(8,128)}, f32[512,1024]{1,0:T(8,128)S(1)}, u32[]{:S(2)}) copy-start(f32[512,1024]{1,0:T(8,128)S(1)} %get-tuple-element.106.attn_ref.attn_hbm) | copy-start | bytes 6291460
  56.7 3.6 %collective-permute-start.3 = (f32[4,136,128]{2,1,0:T(8,128)S(1)}, f32[4,136,128]{2,1,0:T(8,128)S(1)}, u32[]{:S(2)}, u32[]{:S(2)}) collective-permute-start(f32[4,136,128]{2,1,0:T(8,128)S(1)} %get-tuple-element.112), channel_id=1, source_target_pairs={{0,8},{8,0},{1,9},{9,1},{2,10},{10,2},{3,11},{11,3},{4,12},{12,4},... | collective-permute-start | bytes 835592 | tf_op jit(solution)/shard_map/ppermute | solution.py:569
  61.2 12.0 %all-to-all-start.3 = ((f32[16,40,128]{2,1,0:T(8,128)}), f32[16,40,128]{2,1,0:T(8,128)S(1)}, u32[]{:S(2)}, u32[]{:S(2)}) async-start(f32[16,40,128]{2,1,0:T(8,128)} %get-tuple-element.113), calls=%async_computation.3 | async-start | bytes 655360 | tf_op jit(solution)/shard_map/all_to_all | solution.py:573
  74.0 13.5 %all-to-all-start.4 = ((f32[16,32,128]{2,1,0:T(8,128)}), f32[16,32,128]{2,1,0:T(8,128)S(1)}, u32[]{:S(2)}, u32[]{:S(2)}) async-start(f32[16,32,128]{2,1,0:T(8,128)} %scan.3), calls=%async_computation.4 | async-start | bytes 524288 | tf_op jit(solution)/shard_map/all_to_all | solution.py:573
  80.0 7.5 %copy-start.3 = (f32[4,136,128]{2,1,0:T(8,128)S(1)}, f32[4,136,128]{2,1,0:T(8,128)}, u32[]{:S(2)}) copy-start(f32[4,136,128]{2,1,0:T(8,128)} %get-tuple-element.133) | copy-start | bytes 835588
  87.5 5.0 %collective-permute-start.5 = (f32[4,136,128]{2,1,0:T(8,128)S(1)}, f32[4,136,128]{2,1,0:T(8,128)S(1)}, u32[]{:S(2)}, u32[]{:S(2)}) collective-permute-start(f32[4,136,128]{2,1,0:T(8,128)S(1)} %copy-done.3), channel_id=1, source_target_pairs={{0,8},{8,0},{1,9},{9,1},{2,10},{10,2},{3,11},{11,3},{4,12},{12,4},... | collective-permute-start | bytes 835592 | tf_op jit(solution)/shard_map/ppermute | solution.py:569
  89.5 3.0 %collective-permute-start.4 = (f32[4,128,128]{2,1,0:T(8,128)S(1)}, f32[4,128,128]{2,1,0:T(8,128)S(1)}, u32[]{:S(2)}, u32[]{:S(2)}) collective-permute-start(f32[4,128,128]{2,1,0:T(8,128)S(1)} %bitcast.4), channel_id=1, source_target_pairs={{0,8},{8,0},{1,9},{9,1},{2,10},{10,2},{3,11},{11,3},{4,12},{12,4},... | collective-permute-start | bytes 786440 | tf_op jit(solution)/shard_map/ppermute | solution.py:569

commit v5 on v4

--- a/solution.py
+++ b/solution.py
@@ -51,11 +51,12 @@
     return both[:, :HEAD] + both[:, HEAD:]
 
 
-def sum_kernel(rate_ref, within_ref):
+def sum_over(rate_ref, within_ref, rate_copy):
     heads, tokens = rate_ref.shape
     early = lax.broadcasted_iota(jnp.int32, (tokens, tokens), 0)
     late = lax.broadcasted_iota(jnp.int32, (tokens, tokens), 1)
     upto = (early <= late).astype(F32).astype(BF16)
+    rate_copy.wait()
     rate = rate_ref[...]
     high, rest = halves(rate)
     low = (rate - high.astype(F32) - rest.astype(F32)).astype(BF16)
@@ -136,8 +137,7 @@
         sems,
     )
     start(made)
-    made[0].wait()
-    sum_kernel(rate_ref, within_ref)
+    sum_over(rate_ref, within_ref, made[0])
     wait(made[1:3])
     for i in range(group):
         cols = slice(i * HEAD, (i + 1) * HEAD)
@@ -155,10 +155,9 @@
 def combine_kernel(
     lead_ref, mine_ref, other_ref, out_hbm, mine_hbm, other_hbm, out_ref, sems
 ):
-    made = copies([(mine_ref, mine_hbm), (other_ref, other_hbm), (out_ref, out_hbm)], sems)
-    start(made[:2])
+    group = mine_ref.shape[0]
+    made = copies([(mine_ref, mine_hbm), (other_ref, other_hbm)], sems)
     lead = lead_ref[0] == 1
-    group = mine_ref.shape[0]
     rows = HEAD // 4
     for i in range(group):
         own = mine_ref[i, HEAD : HEAD + PAD, :]
@@ -169,7 +168,11 @@
         for j in range(4):
             out_ref[4 * i + j, 0:rows, :] = both[j * rows : (j + 1) * rows]
             out_ref[4 * i + j, rows : rows + PAD, :] = own * far
-    made[2].start()
+        part = pl.ds(4 * i, 4)
+        store = pltpu.make_async_copy(out_ref.at[part], out_hbm.at[part], sems.at[2 + i])
+        store.start()
+        made.append(store)
+    start(made[:2])
     wait(made)
 
 
@@ -346,14 +349,15 @@
     sums_ref[...] = jnp.broadcast_to(packed[None], sums_ref.shape)
 
 
-def grad_head(head, i, within_ref, grown_ref, attn_ref, dnorm_ref, scale_ref, center_ref, out_ref):
-    tokens = attn_ref.shape[0]
+def grad_head(head, attn_ref, dnorm_ref, scale_ref, center_ref):
     scale = scale_ref[...]
     normed = attn_ref[:, lanes(head)] * scale
-    grad = (scale * (dnorm_ref[:, lanes(head)] - normed * center_ref[...])).astype(BF16)
-    last = within_ref[pl.ds(head, 1), :][:, tokens - 1 :]
+    return (scale * (dnorm_ref[:, lanes(head)] - normed * center_ref[...])).astype(BF16)
+
+
+def grad_state(head, i, grad, within_ref, grown_ref, out_ref):
+    last = within_ref[pl.ds(head, 1), :][:, grad.shape[0] - 1 :]
     put_state(out_ref, i, outer_state(grown_ref[:, lanes(head, 2)], grad), jnp.exp(last))
-    return grad
 
 
 def grad_other_kernel(
@@ -371,10 +375,10 @@
         center_ref[rows] = as_column(center[i : i + 1])
     group = out_ref.shape[0]
     for i in range(group):
-        grad_ref[:, i * HEAD : (i + 1) * HEAD] = grad_head(
-            (1 - core_ref[0]) * group + i, i, within_ref, grown_ref, attn_ref, dnorm_ref,
-            scale_ref, center_ref, out_ref,
-        )
+        head = (1 - core_ref[0]) * group + i
+        grad = grad_head(head, attn_ref, dnorm_ref, scale_ref, center_ref)
+        grad_ref[:, i * HEAD : (i + 1) * HEAD] = grad
+        grad_state(head, i, grad, within_ref, grown_ref, out_ref)
 
 
 def grad_mine_kernel(
@@ -387,19 +391,19 @@
         [(grad_far, grad_hbm.at[:, half_of(1 - core, group)]), (table_ref, table_hbm)], far_sems
     )
     start(made)
-    stores = []
     for i in range(group):
         head = core * group + i
         cols = slice(i * HEAD, (i + 1) * HEAD)
-        grad_ref[:, cols] = grad_head(
-            head, i, within_ref, grown_ref, attn_ref, dnorm_ref, scale_ref, center_ref, out_ref
-        )
+        grad_ref[:, cols] = grad_head(head, attn_ref, dnorm_ref, scale_ref, center_ref)
         store = pltpu.make_async_copy(
             grad_ref.at[:, cols], grad_hbm.at[:, lanes(head)], sems.at[i]
         )
         store.start()
-        stores.append(store)
-    wait(made + stores)
+        made.append(store)
+    for i in range(group):
+        grad = grad_ref[:, i * HEAD : (i + 1) * HEAD]
+        grad_state(core * group + i, i, grad, within_ref, grown_ref, out_ref)
+    wait(made)
 
 
 def back_kernel(
@@ -436,10 +440,10 @@
             ).astype(BF16)
             key_part = dot(pgrad, q[first:width], TN)
             if first == 0:
-                key_ref[0:width, at] = key_part
+                early = key_part
             else:
-                key_ref[0:first, at] += key_part[0:first]
-                key_ref[first:width, at] = key_part[first:width]
+                key_ref[0:first, at] = (early + key_part[0:first]).astype(BF16)
+                key_ref[first:width, at] = key_part[first:width].astype(BF16)
 
     each_pair(
         heads, lambda h: wait(head_copies(loads, in_sems, h)), one,
@@ -487,8 +491,8 @@
         sig = sigmoid(gate_ref[:, at].astype(F32))
         output_ref[:, at] = (normed * sig).astype(BF16)
         gate_grad_ref[:, at] = (up_ref[:, at].astype(F32) * normed * sig * (1.0 - sig)).astype(BF16)
-        value_ref[0:size, at] = late[0:size] + early
-        value_ref[size:tokens, at] = late[size:tokens]
+        value_ref[0:size, at] = (late[0:size] + early).astype(BF16)
+        value_ref[size:tokens, at] = late[size:tokens].astype(BF16)
 
     each_pair(
         heads, lambda h: wait(loads(h)), one, lambda h: start(head_copies(stores, out_sems, h))
@@ -506,8 +510,8 @@
     key_inter = dot(jnp.concatenate([v, v], axis=1), jnp.concatenate(state, axis=0), NN)
     value_inter = dot(jnp.concatenate([k, k], axis=1), jnp.concatenate(state, axis=1), NT)
     return (
-        (key_part_ref[:, at] + tail * key_inter).astype(BF16),
-        (value_part_ref[:, at] + tail * value_inter).astype(BF16),
+        (key_part_ref[:, at].astype(F32) + tail * key_inter).astype(BF16),
+        (value_part_ref[:, at].astype(F32) + tail * value_inter).astype(BF16),
     )
 
 
@@ -621,7 +625,7 @@
 
     def combined(lead, mine, other):
         return call(
-            combine_kernel, "combine", (mine, other), (), (), (carried, packed, packed), (carried,), ((3,),),
+            combine_kernel, "combine", (mine, other), (), (), (carried, packed, packed), (carried,), ((2 + group,),),
             lead,
         )
 
@@ -680,8 +684,8 @@
     chip_state, mine, lead_mine = combined(core, mine, lead_mine)
     chip_state = spread(chip_state)
     query_grad, key_part = call(
-        back_kernel, "back", (), (within, queries, keys, values, grad, state), (), (narrow, wide),
-        (rates, narrow, narrow, narrow, narrow, states, narrow, wide), ((1,), (5, heads), (2, heads)),
+        back_kernel, "back", (), (within, queries, keys, values, grad, state), (), (narrow, narrow),
+        (rates, narrow, narrow, narrow, narrow, states, narrow, narrow), ((1,), (5, heads), (2, heads)),
     )
     chip_state, key_part, mine, grad, table = lax.optimization_barrier(
         (chip_state, key_part, mine, grad, table)
@@ -689,8 +693,8 @@
     chip_state, grad, table = lax.optimization_barrier((scanned(chip_state, True), grad, table))
     chip_mine = spread(chip_state)
     value_part, output, gate_grad = call(
-        value_gate_kernel, "value_gate", (), (table, attn, gate, out_grad, grad, probs), (), (wide, narrow, narrow),
-        (table_rows, wide, narrow, narrow, narrow, table_of, wide, narrow, narrow, column),
+        value_gate_kernel, "value_gate", (), (table, attn, gate, out_grad, grad, probs), (), (narrow, narrow, narrow),
+        (table_rows, wide, narrow, narrow, narrow, table_of, narrow, narrow, narrow, column),
         ((1,), (6, heads), (3, heads)), mib=24,
     )
     chip_mine, value_part, output, gate_grad, mine = lax.optimization_barrier(
@@ -700,8 +704,7 @@
     chip_other, lead_other = swap(chip_mine), swap(mine)
     key_near, value_near, *far, within_near = call(
         final_mine_kernel, "final_mine", (chip_mine,), (within, lead_mine, keys, values, key_part, value_part),
-        (half_narrow, half_narrow, half_narrow, half_narrow, half, half, rates), (),
-        (packed, half_narrow, half_narrow, half, half), ((10,),), core,
+        (half_narrow,) * 6 + (rates,), (), (packed,) + (half_narrow,) * 4, ((10,),), core,
     )
     key_grad, value_grad = call(
         final_other_kernel, "final_other", (chip_other, lead_other, within_near, *far, key_near, value_near), (),

time: 95.1 us -> 93.8 us (0.986)
  Pallas kernels: 42.2 us -> 40.9 us
    pallas_call x16, Pallas kernels: 42.2 us -> 40.9 us  [call(): pl.pallas_call(kernel, grid_spec=pltpu.PrefetchScalarGridSpec(num_scalar_...]
  transfers between devices with their start and end apart: 10 -> 10, of which waited for: 5 -> 5; matrix products, arithmetic and copies ran while one was open for 0% -> 0% of each run, Pallas kernels for 35% -> 34%
where the time goes in v5:
time: 93.8 us; the launch traced here: 92.8 us
  Pallas kernels  40.9 us (44%)
  starting transfers between devices  28.5 us (30%)
  blocking collectives  14.9 us (16%)
  waiting for transfers between devices  7.69 us (8%)
    pallas_call x16, Pallas kernels, call(): pl.pallas_call(kernel, grid_spec=pltpu.PrefetchScalarGridSpec(num_scalar_...  40.9 us
    all_to_all x4, starting transfers between devices, spread(): return lax.all_to_all(x, CHIPS, split_axis=0, concat_axis=0, tiled=True)  18.9 us
    all_to_all x1, blocking collectives, shards(): sums = lax.all_to_all(sums, 'tp', split_axis=0, concat_axis=0, tiled=True)  14.9 us
    ppermute x6, starting transfers between devices, swap(): return lax.ppermute(x, 'c', [(0, 1), (1, 0)])  9.65 us
    all_to_all x4, waiting for transfers between devices, spread(): return lax.all_to_all(x, CHIPS, split_axis=0, concat_axis=0, tiled=True)  7.3 us
  transfers between devices with their start and end apart: 10, of which 5 were waited for; matrix products, arithmetic and copies ran while one was open for 0% of the time, Pallas kernels for 34%

profile of v5, /device:TPU:1, one launch (start us, length us, event | category | flops | bytes accessed | tf_op | source)
XLA Modules:
  0.0 92.8 jit_solution(6513278800012901424)
XLA Ops:
  0.6 2.1 %local_other.1 = (f32[8,512]{1,0:T(8,128)S(1)}, f32[4,136,128]{2,1,0:T(8,128)S(1)}, bf16[512,512]{1,0:T(8,128)(2,1)S(1)}, bf16[512,512]{1,0:T(8,128)(2,1)S(1)}) custom-call(s32[1]{0:T(128)} %bitcast.core_ref.lead_ref, f32[8,512]{1,0:T(8,128)} %bitcast.8, bf16[512,1024]{1,0:T(8,128)(2,1)} %k_hbm.7, bf16[512,1024]{1,0:T(8,128)(2,1)} %v_hbm.7), custom_call_target="tpu_custom_call" | custom-call | tf_op jit(solution)/shard_map/local_other/pallas_call | solution.py:584
  2.7 3.3 %collective-permute-start = (f32[4,136,128]{2,1,0:T(8,128)S(1)}, f32[4,136,128]{2,1,0:T(8,128)S(1)}, u32[]{:S(2)}, u32[]{:S(2)}) collective-permute-start(f32[4,136,128]{2,1,0:T(8,128)S(1)} %get-tuple-element.79), channel_id=1, source_target_pairs={{0,8},{8,0},{1,9},{9,1},{2,10},{10,2},{3,11},{11,3},{4,12},{12,4},... | collective-permute-start | bytes 835592 | tf_op jit(solution)/shard_map/ppermute | solution.py:573
  8.2 5.0 %all-to-all-start = ((f32[16,40,128]{2,1,0:T(8,128)}), f32[16,40,128]{2,1,0:T(8,128)S(1)}, u32[]{:S(2)}, u32[]{:S(2)}) async-start(f32[16,40,128]{2,1,0:T(8,128)} %get-tuple-element.80), calls=%async_computation | async-start | bytes 655360 | tf_op jit(solution)/shard_map/all_to_all | solution.py:577
  13.3 6.3 %inside.1 = (bf16[8,512,512]{2,1,0:T(8,128)(2,1)}, f32[512,1024]{1,0:T(8,128)}) custom-call(f32[8,512]{1,0:T(8,128)} %copy-done.2, bf16[512,1024]{1,0:T(8,128)(2,1)} %q_hbm.5, bf16[512,1024]{1,0:T(8,128)(2,1)} %k_hbm.7, bf16[512,1024]{1,0:T(8,128)(2,1)} %v_hbm.7), custom_call_target="tpu_custom_call" | custom-call | tf_op jit(solution)/shard_map/inside/pallas_call | solution.py:584
  19.6 1.6 %all-to-all-done.refs_0_ = f32[16,40,128]{2,1,0:T(8,128)S(1)} async-done(((f32[16,40,128]{2,1,0:T(8,128)}), f32[16,40,128]{2,1,0:T(8,128)S(1)}, u32[]{:S(2)}, u32[]{:S(2)}) %all-to-all-start) | async-done | bytes 327712 | tf_op jit(solution)/shard_map/all_to_all | solution.py:577
  22.0 5.1 %all-to-all-start.1 = ((f32[16,32,128]{2,1,0:T(8,128)}), f32[16,32,128]{2,1,0:T(8,128)S(1)}, u32[]{:S(2)}, u32[]{:S(2)}) async-start(f32[16,32,128]{2,1,0:T(8,128)} %scan.2), calls=%async_computation.1 | async-start | bytes 524288 | tf_op jit(solution)/shard_map/all_to_all | solution.py:577
  27.1 4.2 %prepare.1 = (f32[512,1024]{1,0:T(8,128)}, bf16[512,2048]{1,0:T(8,128)(2,1)}) custom-call(f32[8,512]{1,0:T(8,128)} %copy-done.2, bf16[512,1024]{1,0:T(8,128)(2,1)} %q_hbm.5, bf16[512,1024]{1,0:T(8,128)(2,1)} %gate_hbm.3, bf16[512,1024]{1,0:T(8,128)(2,1)} %up_hbm.3), custom_call_target="tpu_custom_call" | custom-call | tf_op jit(solution)/shard_map/prepare/pallas_call | solution.py:584
  31.3 3.2 %all-to-all-done.1 = f32[16,32,128]{2,1,0:T(8,128)S(1)} async-done(((f32[16,32,128]{2,1,0:T(8,128)}), f32[16,32,128]{2,1,0:T(8,128)S(1)}, u32[]{:S(2)}, u32[]{:S(2)}) %all-to-all-start.1) | async-done | bytes 262176 | tf_op jit(solution)/shard_map/all_to_all | solution.py:577
  34.5 2.3 %collective-permute-start.2 = (f32[4,136,128]{2,1,0:T(8,128)S(1)}, f32[4,136,128]{2,1,0:T(8,128)S(1)}, u32[]{:S(2)}, u32[]{:S(2)}) collective-permute-start(f32[4,136,128]{2,1,0:T(8,128)S(1)} %copy-done.4), channel_id=1, source_target_pairs={{0,8},{8,0},{1,9},{9,1},{2,10},{10,2},{3,11},{11,3},{4,12},{12,4},... | collective-permute-start | bytes 835592 | tf_op jit(solution)/shard_map/ppermute | solution.py:573
  36.8 3.0 %attn_mine.1 = (f32[512,1024]{1,0:T(8,128)S(1)}, f32[512,1024]{1,0:T(8,128)S(1)}, bf16[512,2048]{1,0:T(8,128)(2,1)S(1)}, f32[8,128,128]{2,1,0:T(8,128)S(1)}, f32...) custom-call(s32[1]{0:T(128)} %bitcast.core_ref.lead_ref, ...), custom_call_target="tpu_custom_call" | custom-call | tf_op jit(solution)/shard_map/attn_mine/pallas_call | solution.py:584
  39.8 1.3 %attn_other.1 = (f32[512,1024]{1,0:T(8,128)S(1)}, f32[8,128,128]{2,1,0:T(8,128)S(1)}, f32[8,8,128]{2,1,0:T(8,128)S(1)}) custom-call(s32[1]{0:T(128)} %bitcast.core_ref.lead_ref, f32[4,128,128]{2,1,0:T(8,128)S(1)} %collective-permute-done.1.chip_ref, ...), custom_call_target="tpu_custom_call", output_to_operand_aliasing={{0}: (8, {}), {1}: (9, {})} | custom-call | tf_op jit(solution)/shard_map/attn_other/pallas_call | solution.py:584
  41.1 14.9 %all_to_all.25.sums_ref = f32[8,8,128]{2,1,0:T(8,128)S(1)} all-to-all(f32[8,8,128]{2,1,0:T(8,128)S(1)} %get-tuple-element.104), channel_id=1, replica_groups=mesh['x'=4,'y'=4,'c'=2,'tp'=8] {'tp'}, dimensions={0} | all-to-all | bytes 65536 | tf_op jit(solution)/shard_map/all_to_all | solution.py:673
  56.8 2.0 %collective-permute-start.3 = (f32[4,136,128]{2,1,0:T(8,128)S(1)}, f32[4,136,128]{2,1,0:T(8,128)S(1)}, u32[]{:S(2)}, u32[]{:S(2)}) collective-permute-start(f32[4,136,128]{2,1,0:T(8,128)S(1)} %get-tuple-element.112), channel_id=1, source_target_pairs={{0,8},{8,0},{1,9},{9,1},{2,10},{10,2},{3,11},{11,3},{4,12},{12,4},... | collective-permute-start | bytes 835592 | tf_op jit(solution)/shard_map/ppermute | solution.py:573
  58.8 1.4 %grad_mine.1 = (bf16[512,1024]{1,0:T(8,128)(2,1)}, f32[8,128]{1,0:T(8,128)}, f32[4,136,128]{2,1,0:T(8,128)S(1)}) custom-call(s32[1]{0:T(128)} %bitcast.core_ref.lead_ref, f32[512,128]{1,0:T(8,128)S(1)} %get-tuple-element.107.scale_ref, f32[512,128]{1,0:T(8,128)S(1)} %get-tuple-element.108.center_ref, f32[8,128]{1,0:T(8,128)S(1)} %get-tuple-element.109.table_ref, ...), custom_call_target="tpu_custom_call" | custom-call | tf_op jit(solution)/shard_map/grad_mine/pallas_call | solution.py:584
  60.2 1.0 %combine.3 = (f32[16,40,128]{2,1,0:T(8,128)}, f32[4,136,128]{2,1,0:T(8,128)}, f32[4,136,128]{2,1,0:T(8,128)}) custom-call(s32[1]{0:T(128)} %bitcast.core_ref.lead_ref, f32[4,136,128]{2,1,0:T(8,128)S(1)} %get-tuple-element.111.mine_ref, f32[4,136,128]{2,1,0:T(8,128)S(1)} %collective-permute-done.3.other_ref), custom_call_target="tpu_custom_call" | custom-call | tf_op jit(solution)/shard_map/combine/pallas_call | solution.py:584
  61.2 3.6 %all-to-all-start.3 = ((f32[16,40,128]{2,1,0:T(8,128)}), f32[16,40,128]{2,1,0:T(8,128)S(1)}, u32[]{:S(2)}, u32[]{:S(2)}) async-start(f32[16,40,128]{2,1,0:T(8,128)} %get-tuple-element.113), calls=%async_computation.3 | async-start | bytes 655360 | tf_op jit(solution)/shard_map/all_to_all | solution.py:577
  64.8 7.1 %back.1 = (bf16[512,1024]{1,0:T(8,128)(2,1)}, bf16[512,1024]{1,0:T(8,128)(2,1)}) custom-call(f32[8,512]{1,0:T(8,128)} %copy-done.2, bf16[512,1024]{1,0:T(8,128)(2,1)} %q_hbm.5, bf16[512,1024]{1,0:T(8,128)(2,1)} %k_hbm.7, bf16[512,1024]{1,0:T(8,128)(2,1)} %v_hbm.7, bf16[512,1024]{1,0:T(8,128)(2,1)} %get-tuple-element.124.grad_hbm, f32[8,128,128]{2,1,0:T(8,128)} %copy-done.1), custom_call_target="tpu_custom_call" | custom-call | tf_op jit(solution)/shard_map/back/pallas_call | solution.py:584
  71.9 1.4 %all-to-all-done.3.refs_0_ = f32[16,40,128]{2,1,0:T(8,128)S(1)} async-done(((f32[16,40,128]{2,1,0:T(8,128)}), f32[16,40,128]{2,1,0:T(8,128)S(1)}, u32[]{:S(2)}, u32[]{:S(2)}) %all-to-all-start.3) | async-done | bytes 327712 | tf_op jit(solution)/shard_map/all_to_all | solution.py:577
  74.1 5.2 %all-to-all-start.4 = ((f32[16,32,128]{2,1,0:T(8,128)}), f32[16,32,128]{2,1,0:T(8,128)S(1)}, u32[]{:S(2)}, u32[]{:S(2)}) async-start(f32[16,32,128]{2,1,0:T(8,128)} %scan.3), calls=%async_computation.4 | async-start | bytes 524288 | tf_op jit(solution)/shard_map/all_to_all | solution.py:577
  79.3 6.4 %value_gate.1 = (bf16[512,1024]{1,0:T(8,128)(2,1)}, bf16[512,1024]{1,0:T(8,128)(2,1)}, bf16[512,1024]{1,0:T(8,128)(2,1)}) custom-call(f32[8,128]{1,0:T(8,128)} %get-tuple-element.123.table_hbm, f32[512,1024]{1,0:T(8,128)} %copy-done, bf16[512,1024]{1,0:T(8,128)(2,1)} %gate_hbm.3, bf16[512,1024]{1,0:T(8,128)(2,1)} %up_hbm.3, ...), custom_call_target="tpu_custom_call" | custom-call | tf_op jit(solution)/shard_map/value_gate/pallas_call | solution.py:584
  85.7 1.1 %all-to-all-done.4 = f32[16,32,128]{2,1,0:T(8,128)S(1)} async-done(((f32[16,32,128]{2,1,0:T(8,128)}), f32[16,32,128]{2,1,0:T(8,128)S(1)}, u32[]{:S(2)}, u32[]{:S(2)}) %all-to-all-start.4) | async-done | bytes 262176 | tf_op jit(solution)/shard_map/all_to_all | solution.py:577
  86.7 2.0 %collective-permute-start.5 = (f32[4,136,128]{2,1,0:T(8,128)S(1)}, f32[4,136,128]{2,1,0:T(8,128)S(1)}, u32[]{:S(2)}, u32[]{:S(2)}) collective-permute-start(f32[4,136,128]{2,1,0:T(8,128)S(1)} %copy-done.3), channel_id=1, source_target_pairs={{0,8},{8,0},{1,9},{9,1},{2,10},{10,2},{3,11},{11,3},{4,12},{12,4},... | collective-permute-start | bytes 835592 | tf_op jit(solution)/shard_map/ppermute | solution.py:573
  88.7 2.4 %final_mine.1 = (bf16[512,512]{1,0:T(8,128)(2,1)S(1)}, bf16[512,512]{1,0:T(8,128)(2,1)S(1)}, bf16[512,512]{1,0:T(8,128)(2,1)S(1)}, bf16[512,512]{1,0:T(8,128)(2,...) custom-call(s32[1]{0:T(128)} %bitcast.core_ref.lead_ref, ...), custom_call_target="tpu_custom_call" | custom-call | tf_op jit(solution)/shard_map/final_mine/pallas_call | solution.py:584
  91.2 1.6 %final_other.1 = (bf16[512,1024]{1,0:T(8,128)(2,1)}, bf16[512,1024]{1,0:T(8,128)(2,1)}) custom-call(s32[1]{0:T(128)} %bitcast.core_ref.lead_ref, f32[4,128,128]{2,1,0:T(8,128)S(1)} %collective-permute-done.4.chip_ref, f32[4,136,128]{2,1,0:T(8,128)S(1)} %collective-permute-done.5.lead_ref, f32[8,512]{1,0:T(8,128)S(1)} %get-tuple-element.137.within_ref, ...), custom_call_target="tpu_custom_call" | custom-call | tf_op jit(solution)/shard_map/final_other/pallas_call | solution.py:584
  (23 shorter events, 4.5 us)
Async XLA Ops:
  2.7 10.6 %copy-start.2 = (f32[8,512]{1,0:T(8,128)}, f32[8,512]{1,0:T(8,128)S(1)}, u32[]{:S(2)}) copy-start(f32[8,512]{1,0:T(8,128)S(1)} %get-tuple-element.88.within_ref.within_hbm) | copy-start | bytes 49156
  2.7 4.5 %collective-permute-start = (f32[4,136,128]{2,1,0:T(8,128)S(1)}, f32[4,136,128]{2,1,0:T(8,128)S(1)}, u32[]{:S(2)}, u32[]{:S(2)}) collective-permute-start(f32[4,136,128]{2,1,0:T(8,128)S(1)} %get-tuple-element.79), channel_id=1, source_target_pairs={{0,8},{8,0},{1,9},{9,1},{2,10},{10,2},{3,11},{11,3},{4,12},{12,4},... | collective-permute-start | bytes 835592 | tf_op jit(solution)/shard_map/ppermute | solution.py:573
  8.2 13.0 %all-to-all-start = ((f32[16,40,128]{2,1,0:T(8,128)}), f32[16,40,128]{2,1,0:T(8,128)S(1)}, u32[]{:S(2)}, u32[]{:S(2)}) async-start(f32[16,40,128]{2,1,0:T(8,128)} %get-tuple-element.80), calls=%async_computation | async-start | bytes 655360 | tf_op jit(solution)/shard_map/all_to_all | solution.py:577
  21.2 13.3 %copy-start.4 = (f32[4,136,128]{2,1,0:T(8,128)S(1)}, f32[4,136,128]{2,1,0:T(8,128)}, u32[]{:S(2)}) copy-start(f32[4,136,128]{2,1,0:T(8,128)} %get-tuple-element.92) | copy-start | bytes 835588
  22.0 12.5 %all-to-all-start.1 = ((f32[16,32,128]{2,1,0:T(8,128)}), f32[16,32,128]{2,1,0:T(8,128)S(1)}, u32[]{:S(2)}, u32[]{:S(2)}) async-start(f32[16,32,128]{2,1,0:T(8,128)} %scan.2), calls=%async_computation.1 | async-start | bytes 524288 | tf_op jit(solution)/shard_map/all_to_all | solution.py:577
  34.5 5.3 %collective-permute-start.2 = (f32[4,136,128]{2,1,0:T(8,128)S(1)}, f32[4,136,128]{2,1,0:T(8,128)S(1)}, u32[]{:S(2)}, u32[]{:S(2)}) collective-permute-start(f32[4,136,128]{2,1,0:T(8,128)S(1)} %copy-done.4), channel_id=1, source_target_pairs={{0,8},{8,0},{1,9},{9,1},{2,10},{10,2},{3,11},{11,3},{4,12},{12,4},... | collective-permute-start | bytes 835592 | tf_op jit(solution)/shard_map/ppermute | solution.py:573
  36.8 3.0 %collective-permute-start.1 = (f32[4,128,128]{2,1,0:T(8,128)S(1)}, f32[4,128,128]{2,1,0:T(8,128)S(1)}, u32[]{:S(2)}, u32[]{:S(2)}) collective-permute-start(f32[4,128,128]{2,1,0:T(8,128)S(1)} %bitcast.6), channel_id=1, source_target_pairs={{0,8},{8,0},{1,9},{9,1},{2,10},{10,2},{3,11},{11,3},{4,12},{12,4},... | collective-permute-start | bytes 786440 | tf_op jit(solution)/shard_map/ppermute | solution.py:573
  41.1 15.7 %copy-start.1 = (f32[8,128,128]{2,1,0:T(8,128)}, f32[8,128,128]{2,1,0:T(8,128)S(1)}, u32[]{:S(2)}) copy-start(f32[8,128,128]{2,1,0:T(8,128)S(1)} %get-tuple-element.115.state_hbm) | copy-start | bytes 1572868
  41.1 17.7 %copy-start = (f32[512,1024]{1,0:T(8,128)}, f32[512,1024]{1,0:T(8,128)S(1)}, u32[]{:S(2)}) copy-start(f32[512,1024]{1,0:T(8,128)S(1)} %get-tuple-element.106.attn_ref.attn_hbm) | copy-start | bytes 6291460
  56.8 3.4 %collective-permute-start.3 = (f32[4,136,128]{2,1,0:T(8,128)S(1)}, f32[4,136,128]{2,1,0:T(8,128)S(1)}, u32[]{:S(2)}, u32[]{:S(2)}) collective-permute-start(f32[4,136,128]{2,1,0:T(8,128)S(1)} %get-tuple-element.112), channel_id=1, source_target_pairs={{0,8},{8,0},{1,9},{9,1},{2,10},{10,2},{3,11},{11,3},{4,12},{12,4},... | collective-permute-start | bytes 835592 | tf_op jit(solution)/shard_map/ppermute | solution.py:573
  61.2 12.1 %all-to-all-start.3 = ((f32[16,40,128]{2,1,0:T(8,128)}), f32[16,40,128]{2,1,0:T(8,128)S(1)}, u32[]{:S(2)}, u32[]{:S(2)}) async-start(f32[16,40,128]{2,1,0:T(8,128)} %get-tuple-element.113), calls=%async_computation.3 | async-start | bytes 655360 | tf_op jit(solution)/shard_map/all_to_all | solution.py:577
  74.1 12.6 %all-to-all-start.4 = ((f32[16,32,128]{2,1,0:T(8,128)}), f32[16,32,128]{2,1,0:T(8,128)S(1)}, u32[]{:S(2)}, u32[]{:S(2)}) async-start(f32[16,32,128]{2,1,0:T(8,128)} %scan.3), calls=%async_computation.4 | async-start | bytes 524288 | tf_op jit(solution)/shard_map/all_to_all | solution.py:577
  79.3 7.5 %copy-start.3 = (f32[4,136,128]{2,1,0:T(8,128)S(1)}, f32[4,136,128]{2,1,0:T(8,128)}, u32[]{:S(2)}) copy-start(f32[4,136,128]{2,1,0:T(8,128)} %get-tuple-element.133) | copy-start | bytes 835588
  86.7 4.5 %collective-permute-start.5 = (f32[4,136,128]{2,1,0:T(8,128)S(1)}, f32[4,136,128]{2,1,0:T(8,128)S(1)}, u32[]{:S(2)}, u32[]{:S(2)}) collective-permute-start(f32[4,136,128]{2,1,0:T(8,128)S(1)} %copy-done.3), channel_id=1, source_target_pairs={{0,8},{8,0},{1,9},{9,1},{2,10},{10,2},{3,11},{11,3},{4,12},{12,4},... | collective-permute-start | bytes 835592 | tf_op jit(solution)/shard_map/ppermute | solution.py:573
  88.7 2.5 %collective-permute-start.4 = (f32[4,128,128]{2,1,0:T(8,128)S(1)}, f32[4,128,128]{2,1,0:T(8,128)S(1)}, u32[]{:S(2)}, u32[]{:S(2)}) collective-permute-start(f32[4,128,128]{2,1,0:T(8,128)S(1)} %bitcast.4), channel_id=1, source_target_pairs={{0,8},{8,0},{1,9},{9,1},{2,10},{10,2},{3,11},{11,3},{4,12},{12,4},... | collective-permute-start | bytes 786440 | tf_op jit(solution)/shard_map/ppermute | solution.py:573

commit v6 on v5

--- a/solution.py
+++ b/solution.py
@@ -188,24 +188,26 @@
     wait(made)
 
 
-def decayed(scores, first, within, column):
-    width = scores.shape[1]
+def decayed(scores, left, within, column):
+    size = scores.shape[1]
     rows = lax.broadcasted_iota(jnp.int32, (HEAD, HEAD), 0)
     cols = lax.broadcasted_iota(jnp.int32, (HEAD, HEAD), 1)
     bands = []
-    for start_at in range(first, width, HEAD):
-        band = scores[start_at - first : start_at - first + HEAD]
-        own = column[start_at : start_at + HEAD]
+    for at in range(0, scores.shape[0], HEAD):
+        band = scores[at : at + HEAD]
+        own = column[left + at : left + at + HEAD]
         pieces = []
-        if start_at:
-            edge = within[:, start_at - 1 : start_at]
-            grow = jnp.concatenate([jnp.exp(own - edge)] * (start_at // HEAD), axis=1)
-            pieces.append(band[:, :start_at] * jnp.exp(edge - within[:, :start_at]) * grow)
-        gap = own - within[:, start_at : start_at + HEAD]
-        inside = jnp.where(rows >= cols, jnp.exp(jnp.minimum(gap, 0.0)), 0.0)
-        pieces.append(band[:, start_at : start_at + HEAD] * inside)
-        if start_at + HEAD < width:
-            pieces.append(jnp.zeros((HEAD, width - start_at - HEAD), F32))
+        before = min(at, size)
+        if before:
+            edge = within[:, left + at - 1 : left + at]
+            grow = jnp.concatenate([jnp.exp(own - edge)] * (before // HEAD), axis=1)
+            pieces.append(band[:, :before] * jnp.exp(edge - within[:, left : left + before]) * grow)
+        if at < size:
+            gap = own - within[:, left + at : left + at + HEAD]
+            inside = jnp.where(rows >= cols, jnp.exp(jnp.minimum(gap, 0.0)), 0.0)
+            pieces.append(band[:, at : at + HEAD] * inside)
+        if at + HEAD < size:
+            pieces.append(jnp.zeros((HEAD, size - at - HEAD), F32))
         bands.append(jnp.concatenate(pieces, axis=1).astype(BF16))
     return jnp.concatenate(bands, axis=0)
 
@@ -236,11 +238,13 @@
         within = within_ref[pl.ds(h, 1), :]
         column = as_column(within)
         q, k, v = q_ref[:, lanes(h)], k_ref[:, lanes(h)], v_ref[:, lanes(h)]
-        for first in (0, size):
-            width = first + size
-            probs = decayed(dot(q[first:width], k[0:width], NT), first, within, column)
-            probs_ref[h, first:width, 0:width] = probs
-            intra_ref[first:width, lanes(h)] = dot(probs, v[0:width], NN)
+        early = decayed(dot(q, k[0:size], NT), 0, within, column)
+        late = decayed(dot(q[size:], k[size:], NT), size, within, column)
+        probs_ref[h, :, 0:size] = early
+        probs_ref[h, size:tokens, size:tokens] = late
+        intra = dot(early, v[0:size], NN)
+        intra_ref[0:size, lanes(h)] = intra[0:size]
+        intra_ref[size:tokens, lanes(h)] = intra[size:] + dot(late, v[size:], NN)
 
     each_pair(heads, lambda h: wait(head_copies(loads, in_sems, h)), one, lambda h: start(results(h)))
     each_head(heads, lambda h: wait(results(h)))
@@ -430,20 +434,15 @@
         at = lanes(h)
         q, k, v = q_ref[:, at], k_ref[:, at], v_ref[:, at]
         state = jnp.concatenate(halves(state_ref[h]), axis=0)
-        for first in (0, size):
-            width = first + size
-            grad = grad_ref[first:width, at]
-            pgrad = decayed(dot(grad, v[0:width], NT), first, within, column)
-            inter = dot(jnp.concatenate([grad, grad], axis=1), state, NN)
-            query_grad_ref[first:width, at] = (
-                dot(pgrad, k[0:width], NN) + grow[first:width] * inter
-            ).astype(BF16)
-            key_part = dot(pgrad, q[first:width], TN)
-            if first == 0:
-                early = key_part
-            else:
-                key_ref[0:first, at] = (early + key_part[0:first]).astype(BF16)
-                key_ref[first:width, at] = key_part[first:width].astype(BF16)
+        grad = grad_ref[:, at]
+        early = decayed(dot(grad, v[0:size], NT), 0, within, column)
+        late = decayed(dot(grad[size:], v[size:], NT), size, within, column)
+        query = dot(early, k[0:size], NN)
+        query = jnp.concatenate([query[0:size], query[size:] + dot(late, k[size:], NN)], axis=0)
+        inter = dot(jnp.concatenate([grad, grad], axis=1), state, NN)
+        query_grad_ref[:, at] = (query + grow * inter).astype(BF16)
+        key_ref[0:size, at] = dot(early, q, TN).astype(BF16)
+        key_ref[size:tokens, at] = dot(late, q[size:], TN).astype(BF16)
 
     each_pair(
         heads, lambda h: wait(head_copies(loads, in_sems, h)), one,
@@ -485,14 +484,14 @@
 
     def one(h):
         at = lanes(h)
-        late = dot(probs_ref[h, size:tokens, :], grad_ref[size:tokens, at], TN)
-        early = dot(probs_ref[h, 0:size, 0:size], grad_ref[0:size, at], TN)
+        early = dot(probs_ref[h, :, 0:size], grad_ref[:, at], TN)
+        late = dot(probs_ref[h, size:tokens, size:tokens], grad_ref[size:tokens, at], TN)
         normed = attn_ref[:, at] * scale_ref[...]
         sig = sigmoid(gate_ref[:, at].astype(F32))
         output_ref[:, at] = (normed * sig).astype(BF16)
         gate_grad_ref[:, at] = (up_ref[:, at].astype(F32) * normed * sig * (1.0 - sig)).astype(BF16)
-        value_ref[0:size, at] = (late[0:size] + early).astype(BF16)
-        value_ref[size:tokens, at] = late[size:tokens].astype(BF16)
+        value_ref[0:size, at] = early.astype(BF16)
+        value_ref[size:tokens, at] = late.astype(BF16)
 
     each_pair(
         heads, lambda h: wait(loads(h)), one, lambda h: start(head_copies(stores, out_sems, h))

time: 93.8 us -> 92.9 us (level)
  Pallas kernels: 40.9 us -> 39.5 us
  waiting for transfers between devices: 7.69 us -> 9 us
    all_to_all x4, starting transfers between devices: 18.9 us -> 17.4 us  [spread(): return lax.all_to_all(x, CHIPS, split_axis=0, concat_axis=0, tiled=True)]
    pallas_call x16, Pallas kernels: 40.9 us -> 39.5 us  [call(): pl.pallas_call(kernel, grid_spec=pltpu.PrefetchScalarGridSpec(num_scalar_...]
    all_to_all x4, waiting for transfers between devices: 7.3 us -> 8.61 us  [spread(): return lax.all_to_all(x, CHIPS, split_axis=0, concat_axis=0, tiled=True)]
  transfers between devices with their start and end apart: 10 -> 10, of which waited for: 5 -> 5; matrix products, arithmetic and copies ran while one was open for 0% -> 0% of each run, Pallas kernels for 34% -> 33%
where the time goes in v6:
time: 92.9 us; the launch traced here: 91.9 us
  Pallas kernels  39.5 us (43%)
  starting transfers between devices  27.7 us (30%)
  blocking collectives  14.9 us (16%)
  waiting for transfers between devices  9 us (10%)
    pallas_call x16, Pallas kernels, call(): pl.pallas_call(kernel, grid_spec=pltpu.PrefetchScalarGridSpec(num_scalar_...  39.5 us
    all_to_all x4, starting transfers between devices, spread(): return lax.all_to_all(x, CHIPS, split_axis=0, concat_axis=0, tiled=True)  17.4 us
    all_to_all x1, blocking collectives, shards(): sums = lax.all_to_all(sums, 'tp', split_axis=0, concat_axis=0, tiled=True)  14.9 us
    ppermute x6, starting transfers between devices, swap(): return lax.ppermute(x, 'c', [(0, 1), (1, 0)])  10.3 us
    all_to_all x4, waiting for transfers between devices, spread(): return lax.all_to_all(x, CHIPS, split_axis=0, concat_axis=0, tiled=True)  8.61 us
  transfers between devices with their start and end apart: 10, of which 5 were waited for; matrix products, arithmetic and copies ran while one was open for 0% of the time, Pallas kernels for 33%

profile of v6, /device:TPU:1, one launch (start us, length us, event | category | flops | bytes accessed | tf_op | source)
XLA Modules:
  0.0 91.9 jit_solution(8422176423364169748)
XLA Ops:
  0.6 2.1 %local_other.1 = (f32[8,512]{1,0:T(8,128)S(1)}, f32[4,136,128]{2,1,0:T(8,128)S(1)}, bf16[512,512]{1,0:T(8,128)(2,1)S(1)}, bf16[512,512]{1,0:T(8,128)(2,1)S(1)}) custom-call(s32[1]{0:T(128)} %bitcast.core_ref.lead_ref, f32[8,512]{1,0:T(8,128)} %bitcast.8, bf16[512,1024]{1,0:T(8,128)(2,1)} %k_hbm.7, bf16[512,1024]{1,0:T(8,128)(2,1)} %v_hbm.7), custom_call_target="tpu_custom_call" | custom-call | tf_op jit(solution)/shard_map/local_other/pallas_call | solution.py:583
  2.7 3.3 %collective-permute-start = (f32[4,136,128]{2,1,0:T(8,128)S(1)}, f32[4,136,128]{2,1,0:T(8,128)S(1)}, u32[]{:S(2)}, u32[]{:S(2)}) collective-permute-start(f32[4,136,128]{2,1,0:T(8,128)S(1)} %get-tuple-element.79), channel_id=1, source_target_pairs={{0,8},{8,0},{1,9},{9,1},{2,10},{10,2},{3,11},{11,3},{4,12},{12,4},... | collective-permute-start | bytes 835592 | tf_op jit(solution)/shard_map/ppermute | solution.py:572
  8.2 5.0 %all-to-all-start = ((f32[16,40,128]{2,1,0:T(8,128)}), f32[16,40,128]{2,1,0:T(8,128)S(1)}, u32[]{:S(2)}, u32[]{:S(2)}) async-start(f32[16,40,128]{2,1,0:T(8,128)} %get-tuple-element.80), calls=%async_computation | async-start | bytes 655360 | tf_op jit(solution)/shard_map/all_to_all | solution.py:576
  13.3 5.3 %inside.1 = (bf16[8,512,512]{2,1,0:T(8,128)(2,1)}, f32[512,1024]{1,0:T(8,128)}) custom-call(f32[8,512]{1,0:T(8,128)} %copy-done.2, bf16[512,1024]{1,0:T(8,128)(2,1)} %q_hbm.5, bf16[512,1024]{1,0:T(8,128)(2,1)} %k_hbm.7, bf16[512,1024]{1,0:T(8,128)(2,1)} %v_hbm.7), custom_call_target="tpu_custom_call" | custom-call | tf_op jit(solution)/shard_map/inside/pallas_call | solution.py:583
  18.6 2.6 %all-to-all-done.refs_0_ = f32[16,40,128]{2,1,0:T(8,128)S(1)} async-done(((f32[16,40,128]{2,1,0:T(8,128)}), f32[16,40,128]{2,1,0:T(8,128)S(1)}, u32[]{:S(2)}, u32[]{:S(2)}) %all-to-all-start) | async-done | bytes 327712 | tf_op jit(solution)/shard_map/all_to_all | solution.py:576
  22.0 4.1 %all-to-all-start.1 = ((f32[16,32,128]{2,1,0:T(8,128)}), f32[16,32,128]{2,1,0:T(8,128)S(1)}, u32[]{:S(2)}, u32[]{:S(2)}) async-start(f32[16,32,128]{2,1,0:T(8,128)} %scan.2), calls=%async_computation.1 | async-start | bytes 524288 | tf_op jit(solution)/shard_map/all_to_all | solution.py:576
  26.1 4.2 %prepare.1 = (f32[512,1024]{1,0:T(8,128)}, bf16[512,2048]{1,0:T(8,128)(2,1)}) custom-call(f32[8,512]{1,0:T(8,128)} %copy-done.2, bf16[512,1024]{1,0:T(8,128)(2,1)} %q_hbm.5, bf16[512,1024]{1,0:T(8,128)(2,1)} %gate_hbm.3, bf16[512,1024]{1,0:T(8,128)(2,1)} %up_hbm.3), custom_call_target="tpu_custom_call" | custom-call | tf_op jit(solution)/shard_map/prepare/pallas_call | solution.py:583
  30.3 3.1 %all-to-all-done.1 = f32[16,32,128]{2,1,0:T(8,128)S(1)} async-done(((f32[16,32,128]{2,1,0:T(8,128)}), f32[16,32,128]{2,1,0:T(8,128)S(1)}, u32[]{:S(2)}, u32[]{:S(2)}) %all-to-all-start.1) | async-done | bytes 262176 | tf_op jit(solution)/shard_map/all_to_all | solution.py:576
  33.4 2.9 %collective-permute-start.2 = (f32[4,136,128]{2,1,0:T(8,128)S(1)}, f32[4,136,128]{2,1,0:T(8,128)S(1)}, u32[]{:S(2)}, u32[]{:S(2)}) collective-permute-start(f32[4,136,128]{2,1,0:T(8,128)S(1)} %copy-done.4), channel_id=1, source_target_pairs={{0,8},{8,0},{1,9},{9,1},{2,10},{10,2},{3,11},{11,3},{4,12},{12,4},... | collective-permute-start | bytes 835592 | tf_op jit(solution)/shard_map/ppermute | solution.py:572
  36.3 3.0 %attn_mine.1 = (f32[512,1024]{1,0:T(8,128)S(1)}, f32[512,1024]{1,0:T(8,128)S(1)}, bf16[512,2048]{1,0:T(8,128)(2,1)S(1)}, f32[8,128,128]{2,1,0:T(8,128)S(1)}, f32...) custom-call(s32[1]{0:T(128)} %bitcast.core_ref.lead_ref, ...), custom_call_target="tpu_custom_call" | custom-call | tf_op jit(solution)/shard_map/attn_mine/pallas_call | solution.py:583
  39.3 1.3 %attn_other.1 = (f32[512,1024]{1,0:T(8,128)S(1)}, f32[8,128,128]{2,1,0:T(8,128)S(1)}, f32[8,8,128]{2,1,0:T(8,128)S(1)}) custom-call(s32[1]{0:T(128)} %bitcast.core_ref.lead_ref, f32[4,128,128]{2,1,0:T(8,128)S(1)} %collective-permute-done.1.chip_ref, ...), custom_call_target="tpu_custom_call", output_to_operand_aliasing={{0}: (8, {}), {1}: (9, {})} | custom-call | tf_op jit(solution)/shard_map/attn_other/pallas_call | solution.py:583
  40.6 14.9 %all_to_all.25.sums_ref = f32[8,8,128]{2,1,0:T(8,128)S(1)} all-to-all(f32[8,8,128]{2,1,0:T(8,128)S(1)} %get-tuple-element.104), channel_id=1, replica_groups=mesh['x'=4,'y'=4,'c'=2,'tp'=8] {'tp'}, dimensions={0} | all-to-all | bytes 65536 | tf_op jit(solution)/shard_map/all_to_all | solution.py:672
  56.3 2.0 %collective-permute-start.3 = (f32[4,136,128]{2,1,0:T(8,128)S(1)}, f32[4,136,128]{2,1,0:T(8,128)S(1)}, u32[]{:S(2)}, u32[]{:S(2)}) collective-permute-start(f32[4,136,128]{2,1,0:T(8,128)S(1)} %get-tuple-element.112), channel_id=1, source_target_pairs={{0,8},{8,0},{1,9},{9,1},{2,10},{10,2},{3,11},{11,3},{4,12},{12,4},... | collective-permute-start | bytes 835592 | tf_op jit(solution)/shard_map/ppermute | solution.py:572
  58.3 1.4 %grad_mine.1 = (bf16[512,1024]{1,0:T(8,128)(2,1)}, f32[8,128]{1,0:T(8,128)}, f32[4,136,128]{2,1,0:T(8,128)S(1)}) custom-call(s32[1]{0:T(128)} %bitcast.core_ref.lead_ref, f32[512,128]{1,0:T(8,128)S(1)} %get-tuple-element.107.scale_ref, f32[512,128]{1,0:T(8,128)S(1)} %get-tuple-element.108.center_ref, f32[8,128]{1,0:T(8,128)S(1)} %get-tuple-element.109.table_ref, ...), custom_call_target="tpu_custom_call" | custom-call | tf_op jit(solution)/shard_map/grad_mine/pallas_call | solution.py:583
  59.7 1.0 %combine.3 = (f32[16,40,128]{2,1,0:T(8,128)}, f32[4,136,128]{2,1,0:T(8,128)}, f32[4,136,128]{2,1,0:T(8,128)}) custom-call(s32[1]{0:T(128)} %bitcast.core_ref.lead_ref, f32[4,136,128]{2,1,0:T(8,128)S(1)} %get-tuple-element.111.mine_ref, f32[4,136,128]{2,1,0:T(8,128)S(1)} %collective-permute-done.3.other_ref), custom_call_target="tpu_custom_call" | custom-call | tf_op jit(solution)/shard_map/combine/pallas_call | solution.py:583
  60.7 3.6 %all-to-all-start.3 = ((f32[16,40,128]{2,1,0:T(8,128)}), f32[16,40,128]{2,1,0:T(8,128)S(1)}, u32[]{:S(2)}, u32[]{:S(2)}) async-start(f32[16,40,128]{2,1,0:T(8,128)} %get-tuple-element.113), calls=%async_computation.3 | async-start | bytes 655360 | tf_op jit(solution)/shard_map/all_to_all | solution.py:576
  64.3 6.7 %back.1 = (bf16[512,1024]{1,0:T(8,128)(2,1)}, bf16[512,1024]{1,0:T(8,128)(2,1)}) custom-call(f32[8,512]{1,0:T(8,128)} %copy-done.2, bf16[512,1024]{1,0:T(8,128)(2,1)} %q_hbm.5, bf16[512,1024]{1,0:T(8,128)(2,1)} %k_hbm.7, bf16[512,1024]{1,0:T(8,128)(2,1)} %v_hbm.7, bf16[512,1024]{1,0:T(8,128)(2,1)} %get-tuple-element.124.grad_hbm, f32[8,128,128]{2,1,0:T(8,128)} %copy-done.1), custom_call_target="tpu_custom_call" | custom-call | tf_op jit(solution)/shard_map/back/pallas_call | solution.py:583
  71.0 1.8 %all-to-all-done.3.refs_0_ = f32[16,40,128]{2,1,0:T(8,128)S(1)} async-done(((f32[16,40,128]{2,1,0:T(8,128)}), f32[16,40,128]{2,1,0:T(8,128)S(1)}, u32[]{:S(2)}, u32[]{:S(2)}) %all-to-all-start.3) | async-done | bytes 327712 | tf_op jit(solution)/shard_map/all_to_all | solution.py:576
  73.6 4.8 %all-to-all-start.4 = ((f32[16,32,128]{2,1,0:T(8,128)}), f32[16,32,128]{2,1,0:T(8,128)S(1)}, u32[]{:S(2)}, u32[]{:S(2)}) async-start(f32[16,32,128]{2,1,0:T(8,128)} %scan.3), calls=%async_computation.4 | async-start | bytes 524288 | tf_op jit(solution)/shard_map/all_to_all | solution.py:576
  78.4 6.4 %value_gate.1 = (bf16[512,1024]{1,0:T(8,128)(2,1)}, bf16[512,1024]{1,0:T(8,128)(2,1)}, bf16[512,1024]{1,0:T(8,128)(2,1)}) custom-call(f32[8,128]{1,0:T(8,128)} %get-tuple-element.123.table_hbm, f32[512,1024]{1,0:T(8,128)} %copy-done, bf16[512,1024]{1,0:T(8,128)(2,1)} %gate_hbm.3, bf16[512,1024]{1,0:T(8,128)(2,1)} %up_hbm.3, ...), custom_call_target="tpu_custom_call" | custom-call | tf_op jit(solution)/shard_map/value_gate/pallas_call | solution.py:583
  84.8 1.0 %all-to-all-done.4 = f32[16,32,128]{2,1,0:T(8,128)S(1)} async-done(((f32[16,32,128]{2,1,0:T(8,128)}), f32[16,32,128]{2,1,0:T(8,128)S(1)}, u32[]{:S(2)}, u32[]{:S(2)}) %all-to-all-start.4) | async-done | bytes 262176 | tf_op jit(solution)/shard_map/all_to_all | solution.py:576
  85.8 2.0 %collective-permute-start.5 = (f32[4,136,128]{2,1,0:T(8,128)S(1)}, f32[4,136,128]{2,1,0:T(8,128)S(1)}, u32[]{:S(2)}, u32[]{:S(2)}) collective-permute-start(f32[4,136,128]{2,1,0:T(8,128)S(1)} %copy-done.3), channel_id=1, source_target_pairs={{0,8},{8,0},{1,9},{9,1},{2,10},{10,2},{3,11},{11,3},{4,12},{12,4},... | collective-permute-start | bytes 835592 | tf_op jit(solution)/shard_map/ppermute | solution.py:572
  87.8 2.4 %final_mine.1 = (bf16[512,512]{1,0:T(8,128)(2,1)S(1)}, bf16[512,512]{1,0:T(8,128)(2,1)S(1)}, bf16[512,512]{1,0:T(8,128)(2,1)S(1)}, bf16[512,512]{1,0:T(8,128)(2,...) custom-call(s32[1]{0:T(128)} %bitcast.core_ref.lead_ref, ...), custom_call_target="tpu_custom_call" | custom-call | tf_op jit(solution)/shard_map/final_mine/pallas_call | solution.py:583
  90.3 1.6 %final_other.1 = (bf16[512,1024]{1,0:T(8,128)(2,1)}, bf16[512,1024]{1,0:T(8,128)(2,1)}) custom-call(s32[1]{0:T(128)} %bitcast.core_ref.lead_ref, f32[4,128,128]{2,1,0:T(8,128)S(1)} %collective-permute-done.4.chip_ref, f32[4,136,128]{2,1,0:T(8,128)S(1)} %collective-permute-done.5.lead_ref, f32[8,512]{1,0:T(8,128)S(1)} %get-tuple-element.137.within_ref, ...), custom_call_target="tpu_custom_call" | custom-call | tf_op jit(solution)/shard_map/final_other/pallas_call | solution.py:583
  (23 shorter events, 4.5 us)
Async XLA Ops:
  2.7 10.6 %copy-start.2 = (f32[8,512]{1,0:T(8,128)}, f32[8,512]{1,0:T(8,128)S(1)}, u32[]{:S(2)}) copy-start(f32[8,512]{1,0:T(8,128)S(1)} %get-tuple-element.88.within_ref.within_hbm) | copy-start | bytes 49156
  2.7 4.5 %collective-permute-start = (f32[4,136,128]{2,1,0:T(8,128)S(1)}, f32[4,136,128]{2,1,0:T(8,128)S(1)}, u32[]{:S(2)}, u32[]{:S(2)}) collective-permute-start(f32[4,136,128]{2,1,0:T(8,128)S(1)} %get-tuple-element.79), channel_id=1, source_target_pairs={{0,8},{8,0},{1,9},{9,1},{2,10},{10,2},{3,11},{11,3},{4,12},{12,4},... | collective-permute-start | bytes 835592 | tf_op jit(solution)/shard_map/ppermute | solution.py:572
  8.2 13.0 %all-to-all-start = ((f32[16,40,128]{2,1,0:T(8,128)}), f32[16,40,128]{2,1,0:T(8,128)S(1)}, u32[]{:S(2)}, u32[]{:S(2)}) async-start(f32[16,40,128]{2,1,0:T(8,128)} %get-tuple-element.80), calls=%async_computation | async-start | bytes 655360 | tf_op jit(solution)/shard_map/all_to_all | solution.py:576
  21.2 12.2 %copy-start.4 = (f32[4,136,128]{2,1,0:T(8,128)S(1)}, f32[4,136,128]{2,1,0:T(8,128)}, u32[]{:S(2)}) copy-start(f32[4,136,128]{2,1,0:T(8,128)} %get-tuple-element.92) | copy-start | bytes 835588
  22.0 11.4 %all-to-all-start.1 = ((f32[16,32,128]{2,1,0:T(8,128)}), f32[16,32,128]{2,1,0:T(8,128)S(1)}, u32[]{:S(2)}, u32[]{:S(2)}) async-start(f32[16,32,128]{2,1,0:T(8,128)} %scan.2), calls=%async_computation.1 | async-start | bytes 524288 | tf_op jit(solution)/shard_map/all_to_all | solution.py:576
  33.4 5.9 %collective-permute-start.2 = (f32[4,136,128]{2,1,0:T(8,128)S(1)}, f32[4,136,128]{2,1,0:T(8,128)S(1)}, u32[]{:S(2)}, u32[]{:S(2)}) collective-permute-start(f32[4,136,128]{2,1,0:T(8,128)S(1)} %copy-done.4), channel_id=1, source_target_pairs={{0,8},{8,0},{1,9},{9,1},{2,10},{10,2},{3,11},{11,3},{4,12},{12,4},... | collective-permute-start | bytes 835592 | tf_op jit(solution)/shard_map/ppermute | solution.py:572
  36.3 3.0 %collective-permute-start.1 = (f32[4,128,128]{2,1,0:T(8,128)S(1)}, f32[4,128,128]{2,1,0:T(8,128)S(1)}, u32[]{:S(2)}, u32[]{:S(2)}) collective-permute-start(f32[4,128,128]{2,1,0:T(8,128)S(1)} %bitcast.6), channel_id=1, source_target_pairs={{0,8},{8,0},{1,9},{9,1},{2,10},{10,2},{3,11},{11,3},{4,12},{12,4},... | collective-permute-start | bytes 786440 | tf_op jit(solution)/shard_map/ppermute | solution.py:572
  40.6 15.7 %copy-start.1 = (f32[8,128,128]{2,1,0:T(8,128)}, f32[8,128,128]{2,1,0:T(8,128)S(1)}, u32[]{:S(2)}) copy-start(f32[8,128,128]{2,1,0:T(8,128)S(1)} %get-tuple-element.115.state_hbm) | copy-start | bytes 1572868
  40.6 17.7 %copy-start = (f32[512,1024]{1,0:T(8,128)}, f32[512,1024]{1,0:T(8,128)S(1)}, u32[]{:S(2)}) copy-start(f32[512,1024]{1,0:T(8,128)S(1)} %get-tuple-element.106.attn_ref.attn_hbm) | copy-start | bytes 6291460
  56.3 3.4 %collective-permute-start.3 = (f32[4,136,128]{2,1,0:T(8,128)S(1)}, f32[4,136,128]{2,1,0:T(8,128)S(1)}, u32[]{:S(2)}, u32[]{:S(2)}) collective-permute-start(f32[4,136,128]{2,1,0:T(8,128)S(1)} %get-tuple-element.112), channel_id=1, source_target_pairs={{0,8},{8,0},{1,9},{9,1},{2,10},{10,2},{3,11},{11,3},{4,12},{12,4},... | collective-permute-start | bytes 835592 | tf_op jit(solution)/shard_map/ppermute | solution.py:572
  60.7 12.1 %all-to-all-start.3 = ((f32[16,40,128]{2,1,0:T(8,128)}), f32[16,40,128]{2,1,0:T(8,128)S(1)}, u32[]{:S(2)}, u32[]{:S(2)}) async-start(f32[16,40,128]{2,1,0:T(8,128)} %get-tuple-element.113), calls=%async_computation.3 | async-start | bytes 655360 | tf_op jit(solution)/shard_map/all_to_all | solution.py:576
  73.6 12.2 %all-to-all-start.4 = ((f32[16,32,128]{2,1,0:T(8,128)}), f32[16,32,128]{2,1,0:T(8,128)S(1)}, u32[]{:S(2)}, u32[]{:S(2)}) async-start(f32[16,32,128]{2,1,0:T(8,128)} %scan.3), calls=%async_computation.4 | async-start | bytes 524288 | tf_op jit(solution)/shard_map/all_to_all | solution.py:576
  78.4 7.5 %copy-start.3 = (f32[4,136,128]{2,1,0:T(8,128)S(1)}, f32[4,136,128]{2,1,0:T(8,128)}, u32[]{:S(2)}) copy-start(f32[4,136,128]{2,1,0:T(8,128)} %get-tuple-element.133) | copy-start | bytes 835588
  85.8 4.5 %collective-permute-start.5 = (f32[4,136,128]{2,1,0:T(8,128)S(1)}, f32[4,136,128]{2,1,0:T(8,128)S(1)}, u32[]{:S(2)}, u32[]{:S(2)}) collective-permute-start(f32[4,136,128]{2,1,0:T(8,128)S(1)} %copy-done.3), channel_id=1, source_target_pairs={{0,8},{8,0},{1,9},{9,1},{2,10},{10,2},{3,11},{11,3},{4,12},{12,4},... | collective-permute-start | bytes 835592 | tf_op jit(solution)/shard_map/ppermute | solution.py:572
  87.8 2.5 %collective-permute-start.4 = (f32[4,128,128]{2,1,0:T(8,128)S(1)}, f32[4,128,128]{2,1,0:T(8,128)S(1)}, u32[]{:S(2)}, u32[]{:S(2)}) collective-permute-start(f32[4,128,128]{2,1,0:T(8,128)S(1)} %bitcast.4), channel_id=1, source_target_pairs={{0,8},{8,0},{1,9},{9,1},{2,10},{10,2},{3,11},{11,3},{4,12},{12,4},... | collective-permute-start | bytes 786440 | tf_op jit(solution)/shard_map/ppermute | solution.py:572

commit v7 on v6

--- a/solution.py
+++ b/solution.py
@@ -411,8 +411,8 @@
 
 
 def back_kernel(
-    within_hbm, q_hbm, k_hbm, v_hbm, grad_hbm, state_hbm, query_grad_hbm, key_hbm,
-    within_ref, q_ref, k_ref, v_ref, grad_ref, state_ref, query_grad_ref, key_ref, sem, in_sems, out_sems,
+    within_hbm, q_hbm, k_hbm, v_hbm, grad_hbm, state_hbm, query_grad_hbm, key_ref,
+    within_ref, q_ref, k_ref, v_ref, grad_ref, state_ref, query_grad_ref, sem, in_sems, out_sems,
 ):
     heads = within_ref.shape[0]
     tokens = q_ref.shape[0]
@@ -423,7 +423,7 @@
         (grad_hbm, grad_ref, 1), (v_hbm, v_ref, 1), (k_hbm, k_ref, 1), (q_hbm, q_ref, 1),
         (state_hbm, state_ref, 0),
     ]
-    stores = [(query_grad_ref, query_grad_hbm, 1), (key_ref, key_hbm, 1)]
+    stores = [(query_grad_ref, query_grad_hbm, 1)]
     each_head(heads, lambda h: start(head_copies(loads, in_sems, h)))
     wait(small)
 
@@ -452,8 +452,8 @@
 
 
 def value_gate_kernel(
-    table_hbm, attn_hbm, gate_hbm, up_hbm, grad_hbm, probs_hbm, value_hbm, output_hbm, gate_grad_hbm,
-    table_ref, attn_ref, gate_ref, up_ref, grad_ref, probs_ref, value_ref, output_ref, gate_grad_ref,
+    table_hbm, attn_hbm, gate_hbm, up_hbm, grad_hbm, probs_hbm, output_hbm, gate_grad_hbm, value_ref,
+    table_ref, attn_ref, gate_ref, up_ref, grad_ref, probs_ref, output_ref, gate_grad_ref,
     scale_ref, sem, in_sems, out_sems,
 ):
     heads = probs_ref.shape[0]
@@ -476,7 +476,7 @@
         ]
         return [pltpu.make_async_copy(a, b, in_sems.at[i, h]) for i, (a, b) in enumerate(pairs)]
 
-    stores = [(value_ref, value_hbm, 1), (output_ref, output_hbm, 1), (gate_grad_ref, gate_grad_hbm, 1)]
+    stores = [(output_ref, output_hbm, 1), (gate_grad_ref, gate_grad_hbm, 1)]
     each_head(heads, lambda h: start(loads(h)))
     wait(small)
     for i in range(4):
@@ -502,6 +502,7 @@
 def final_head(core, head, i, within_ref, k_ref, v_ref, key_part_ref, value_part_ref, chip_ref, lead_ref):
     tokens = k_ref.shape[0]
     at = slice(i * HEAD, (i + 1) * HEAD)
+    own = lanes(head)
     state = halves(pick_state(core == 0, chip_ref, lead_ref, i))
     within = within_ref[pl.ds(head, 1), :]
     tail = as_column(jnp.exp(within[:, tokens - 1 :] - within))
@@ -509,33 +510,31 @@
     key_inter = dot(jnp.concatenate([v, v], axis=1), jnp.concatenate(state, axis=0), NN)
     value_inter = dot(jnp.concatenate([k, k], axis=1), jnp.concatenate(state, axis=1), NT)
     return (
-        (key_part_ref[:, at].astype(F32) + tail * key_inter).astype(BF16),
-        (value_part_ref[:, at].astype(F32) + tail * value_inter).astype(BF16),
+        (key_part_ref[:, own].astype(F32) + tail * key_inter).astype(BF16),
+        (value_part_ref[:, own].astype(F32) + tail * value_inter).astype(BF16),
     )
 
 
 def final_mine_kernel(
-    core_ref, chip_ref, within_hbm, lead_hbm, k_hbm, v_hbm, key_part_hbm, value_part_hbm,
-    key_grad_ref, value_grad_ref, k_far, v_far, key_part_far, value_part_far, within_ref,
-    lead_ref, k_ref, v_ref, key_part_ref, value_part_ref, sems,
+    core_ref, chip_ref, key_part_ref, value_part_ref, within_hbm, lead_hbm, k_hbm, v_hbm,
+    key_grad_ref, value_grad_ref, k_far, v_far, within_ref, lead_ref, k_ref, v_ref, sems,
 ):
     core = core_ref[0]
     group = chip_ref.shape[0]
-    sources = (k_hbm, v_hbm, key_part_hbm, value_part_hbm)
     near, far = half_of(core, group), half_of(1 - core, group)
     pairs = [(within_hbm, within_ref), (lead_hbm, lead_ref)]
-    pairs += [(a.at[:, near], b) for a, b in zip(sources, (k_ref, v_ref, key_part_ref, value_part_ref))]
-    pairs += [(a.at[:, far], b) for a, b in zip(sources, (k_far, v_far, key_part_far, value_part_far))]
+    pairs += [(v_hbm.at[:, near], v_ref), (k_hbm.at[:, near], k_ref)]
+    pairs += [(v_hbm.at[:, far], v_far), (k_hbm.at[:, far], k_far)]
     made = copies(pairs, sems)
     start(made)
-    wait(made[:6])
+    wait(made[:4])
     for i in range(group):
         cols = slice(i * HEAD, (i + 1) * HEAD)
         key_grad_ref[:, cols], value_grad_ref[:, cols] = final_head(
             core, core * group + i, i, within_ref, k_ref, v_ref, key_part_ref, value_part_ref,
             chip_ref, lead_ref,
         )
-    wait(made[6:])
+    wait(made[4:])
 
 
 def final_other_kernel(
@@ -683,30 +682,31 @@
     chip_state, mine, lead_mine = combined(core, mine, lead_mine)
     chip_state = spread(chip_state)
     query_grad, key_part = call(
-        back_kernel, "back", (), (within, queries, keys, values, grad, state), (), (narrow, narrow),
-        (rates, narrow, narrow, narrow, narrow, states, narrow, narrow), ((1,), (5, heads), (2, heads)),
+        back_kernel, "back", (), (within, queries, keys, values, grad, state), (narrow,), (narrow,),
+        (rates, narrow, narrow, narrow, narrow, states, narrow), ((1,), (5, heads), (1, heads)),
     )
     chip_state, key_part, mine, grad, table = lax.optimization_barrier(
         (chip_state, key_part, mine, grad, table)
     )
     chip_state, grad, table = lax.optimization_barrier((scanned(chip_state, True), grad, table))
     chip_mine = spread(chip_state)
-    value_part, output, gate_grad = call(
-        value_gate_kernel, "value_gate", (), (table, attn, gate, out_grad, grad, probs), (), (narrow, narrow, narrow),
-        (table_rows, wide, narrow, narrow, narrow, table_of, narrow, narrow, narrow, column),
-        ((1,), (6, heads), (3, heads)), mib=24,
+    output, gate_grad, value_part = call(
+        value_gate_kernel, "value_gate", (), (table, attn, gate, out_grad, grad, probs), (narrow,), (narrow, narrow),
+        (table_rows, wide, narrow, narrow, narrow, table_of, narrow, narrow, column),
+        ((1,), (6, heads), (2, heads)), mib=24,
     )
     chip_mine, value_part, output, gate_grad, mine = lax.optimization_barrier(
         (chip_mine, value_part, output, gate_grad, mine)
     )
     chip_mine = chip_mine.reshape(group, HEAD, HEAD)
     chip_other, lead_other = swap(chip_mine), swap(mine)
-    key_near, value_near, *far, within_near = call(
-        final_mine_kernel, "final_mine", (chip_mine,), (within, lead_mine, keys, values, key_part, value_part),
-        (half_narrow,) * 6 + (rates,), (), (packed,) + (half_narrow,) * 4, ((10,),), core,
+    key_near, value_near, k_far, v_far, within_near = call(
+        final_mine_kernel, "final_mine", (chip_mine, key_part, value_part), (within, lead_mine, keys, values),
+        (half_narrow,) * 4 + (rates,), (), (packed, half_narrow, half_narrow), ((6,),), core,
     )
     key_grad, value_grad = call(
-        final_other_kernel, "final_other", (chip_other, lead_other, within_near, *far, key_near, value_near), (),
+        final_other_kernel, "final_other",
+        (chip_other, lead_other, within_near, k_far, v_far, key_part, value_part, key_near, value_near), (),
         (), (narrow, narrow), (half_narrow, half_narrow), ((2,), (2, group)), core,
     )
     return output, query_grad, key_grad, value_grad, gate_grad

time: 92.9 us -> 92.3 us (level)
  transfers between devices with their start and end apart: 10 -> 10, of which waited for: 5 -> 5; matrix products, arithmetic and copies ran while one was open for 0% -> 0% of each run, Pallas kernels for 33% -> 32%
where the time goes in v7:
time: 92.3 us; the launch traced here: 91.4 us
  Pallas kernels  38.8 us (42%)
  starting transfers between devices  27.5 us (30%)
  blocking collectives  14.9 us (16%)
  waiting for transfers between devices  9.29 us (10%)
    pallas_call x16, Pallas kernels, call(): pl.pallas_call(kernel, grid_spec=pltpu.PrefetchScalarGridSpec(num_scalar_...  38.8 us
    all_to_all x4, starting transfers between devices, spread(): return lax.all_to_all(x, CHIPS, split_axis=0, concat_axis=0, tiled=True)  17.2 us
    all_to_all x1, blocking collectives, shards(): sums = lax.all_to_all(sums, 'tp', split_axis=0, concat_axis=0, tiled=True)  14.9 us
    ppermute x6, starting transfers between devices, swap(): return lax.ppermute(x, 'c', [(0, 1), (1, 0)])  10.3 us
    all_to_all x4, waiting for transfers between devices, spread(): return lax.all_to_all(x, CHIPS, split_axis=0, concat_axis=0, tiled=True)  8.9 us
  transfers between devices with their start and end apart: 10, of which 5 were waited for; matrix products, arithmetic and copies ran while one was open for 0% of the time, Pallas kernels for 32%

profile of v7, /device:TPU:1, one launch (start us, length us, event | category | flops | bytes accessed | tf_op | source)
XLA Modules:
  0.0 91.4 jit_solution(2063706235455829658)
XLA Ops:
  0.6 2.1 %local_other.1 = (f32[8,512]{1,0:T(8,128)S(1)}, f32[4,136,128]{2,1,0:T(8,128)S(1)}, bf16[512,512]{1,0:T(8,128)(2,1)S(1)}, bf16[512,512]{1,0:T(8,128)(2,1)S(1)}) custom-call(s32[1]{0:T(128)} %bitcast.core_ref.lead_ref, f32[8,512]{1,0:T(8,128)} %bitcast.8, bf16[512,1024]{1,0:T(8,128)(2,1)} %k_hbm.7, bf16[512,1024]{1,0:T(8,128)(2,1)} %v_hbm.7), custom_call_target="tpu_custom_call" | custom-call | tf_op jit(solution)/shard_map/local_other/pallas_call | solution.py:582
  2.7 3.3 %collective-permute-start = (f32[4,136,128]{2,1,0:T(8,128)S(1)}, f32[4,136,128]{2,1,0:T(8,128)S(1)}, u32[]{:S(2)}, u32[]{:S(2)}) collective-permute-start(f32[4,136,128]{2,1,0:T(8,128)S(1)} %get-tuple-element.77), channel_id=1, source_target_pairs={{0,8},{8,0},{1,9},{9,1},{2,10},{10,2},{3,11},{11,3},{4,12},{12,4},... | collective-permute-start | bytes 835592 | tf_op jit(solution)/shard_map/ppermute | solution.py:571
  8.2 5.0 %all-to-all-start = ((f32[16,40,128]{2,1,0:T(8,128)}), f32[16,40,128]{2,1,0:T(8,128)S(1)}, u32[]{:S(2)}, u32[]{:S(2)}) async-start(f32[16,40,128]{2,1,0:T(8,128)} %get-tuple-element.78), calls=%async_computation | async-start | bytes 655360 | tf_op jit(solution)/shard_map/all_to_all | solution.py:575
  13.3 5.3 %inside.1 = (bf16[8,512,512]{2,1,0:T(8,128)(2,1)}, f32[512,1024]{1,0:T(8,128)}) custom-call(f32[8,512]{1,0:T(8,128)} %copy-done.2, bf16[512,1024]{1,0:T(8,128)(2,1)} %q_hbm.5, bf16[512,1024]{1,0:T(8,128)(2,1)} %k_hbm.7, bf16[512,1024]{1,0:T(8,128)(2,1)} %v_hbm.7), custom_call_target="tpu_custom_call" | custom-call | tf_op jit(solution)/shard_map/inside/pallas_call | solution.py:582
  18.6 2.6 %all-to-all-done.refs_0_ = f32[16,40,128]{2,1,0:T(8,128)S(1)} async-done(((f32[16,40,128]{2,1,0:T(8,128)}), f32[16,40,128]{2,1,0:T(8,128)S(1)}, u32[]{:S(2)}, u32[]{:S(2)}) %all-to-all-start) | async-done | bytes 327712 | tf_op jit(solution)/shard_map/all_to_all | solution.py:575
  22.0 4.1 %all-to-all-start.1 = ((f32[16,32,128]{2,1,0:T(8,128)}), f32[16,32,128]{2,1,0:T(8,128)S(1)}, u32[]{:S(2)}, u32[]{:S(2)}) async-start(f32[16,32,128]{2,1,0:T(8,128)} %scan.2), calls=%async_computation.1 | async-start | bytes 524288 | tf_op jit(solution)/shard_map/all_to_all | solution.py:575
  26.1 4.2 %prepare.1 = (f32[512,1024]{1,0:T(8,128)}, bf16[512,2048]{1,0:T(8,128)(2,1)}) custom-call(f32[8,512]{1,0:T(8,128)} %copy-done.2, bf16[512,1024]{1,0:T(8,128)(2,1)} %q_hbm.5, bf16[512,1024]{1,0:T(8,128)(2,1)} %gate_hbm.3, bf16[512,1024]{1,0:T(8,128)(2,1)} %up_hbm.3), custom_call_target="tpu_custom_call" | custom-call | tf_op jit(solution)/shard_map/prepare/pallas_call | solution.py:582
  30.3 3.1 %all-to-all-done.1 = f32[16,32,128]{2,1,0:T(8,128)S(1)} async-done(((f32[16,32,128]{2,1,0:T(8,128)}), f32[16,32,128]{2,1,0:T(8,128)S(1)}, u32[]{:S(2)}, u32[]{:S(2)}) %all-to-all-start.1) | async-done | bytes 262176 | tf_op jit(solution)/shard_map/all_to_all | solution.py:575
  33.4 2.9 %collective-permute-start.2 = (f32[4,136,128]{2,1,0:T(8,128)S(1)}, f32[4,136,128]{2,1,0:T(8,128)S(1)}, u32[]{:S(2)}, u32[]{:S(2)}) collective-permute-start(f32[4,136,128]{2,1,0:T(8,128)S(1)} %copy-done.4), channel_id=1, source_target_pairs={{0,8},{8,0},{1,9},{9,1},{2,10},{10,2},{3,11},{11,3},{4,12},{12,4},... | collective-permute-start | bytes 835592 | tf_op jit(solution)/shard_map/ppermute | solution.py:571
  36.3 3.0 %attn_mine.1 = (f32[512,1024]{1,0:T(8,128)S(1)}, f32[512,1024]{1,0:T(8,128)S(1)}, bf16[512,2048]{1,0:T(8,128)(2,1)S(1)}, f32[8,128,128]{2,1,0:T(8,128)S(1)}, f32...) custom-call(s32[1]{0:T(128)} %bitcast.core_ref.lead_ref, ...), custom_call_target="tpu_custom_call" | custom-call | tf_op jit(solution)/shard_map/attn_mine/pallas_call | solution.py:582
  39.3 1.3 %attn_other.1 = (f32[512,1024]{1,0:T(8,128)S(1)}, f32[8,128,128]{2,1,0:T(8,128)S(1)}, f32[8,8,128]{2,1,0:T(8,128)S(1)}) custom-call(s32[1]{0:T(128)} %bitcast.core_ref.lead_ref, f32[4,128,128]{2,1,0:T(8,128)S(1)} %collective-permute-done.1.chip_ref, ...), custom_call_target="tpu_custom_call", output_to_operand_aliasing={{0}: (8, {}), {1}: (9, {})} | custom-call | tf_op jit(solution)/shard_map/attn_other/pallas_call | solution.py:582
  40.6 14.9 %all_to_all.25.sums_ref = f32[8,8,128]{2,1,0:T(8,128)S(1)} all-to-all(f32[8,8,128]{2,1,0:T(8,128)S(1)} %get-tuple-element.102), channel_id=1, replica_groups=mesh['x'=4,'y'=4,'c'=2,'tp'=8] {'tp'}, dimensions={0} | all-to-all | bytes 65536 | tf_op jit(solution)/shard_map/all_to_all | solution.py:671
  56.3 2.0 %collective-permute-start.3 = (f32[4,136,128]{2,1,0:T(8,128)S(1)}, f32[4,136,128]{2,1,0:T(8,128)S(1)}, u32[]{:S(2)}, u32[]{:S(2)}) collective-permute-start(f32[4,136,128]{2,1,0:T(8,128)S(1)} %get-tuple-element.110), channel_id=1, source_target_pairs={{0,8},{8,0},{1,9},{9,1},{2,10},{10,2},{3,11},{11,3},{4,12},{12,4},... | collective-permute-start | bytes 835592 | tf_op jit(solution)/shard_map/ppermute | solution.py:571
  58.3 1.4 %grad_mine.1 = (bf16[512,1024]{1,0:T(8,128)(2,1)}, f32[8,128]{1,0:T(8,128)}, f32[4,136,128]{2,1,0:T(8,128)S(1)}) custom-call(s32[1]{0:T(128)} %bitcast.core_ref.lead_ref, f32[512,128]{1,0:T(8,128)S(1)} %get-tuple-element.105.scale_ref, f32[512,128]{1,0:T(8,128)S(1)} %get-tuple-element.106.center_ref, f32[8,128]{1,0:T(8,128)S(1)} %get-tuple-element.107.table_ref, ...), custom_call_target="tpu_custom_call" | custom-call | tf_op jit(solution)/shard_map/grad_mine/pallas_call | solution.py:582
  59.7 1.0 %combine.3 = (f32[16,40,128]{2,1,0:T(8,128)}, f32[4,136,128]{2,1,0:T(8,128)}, f32[4,136,128]{2,1,0:T(8,128)}) custom-call(s32[1]{0:T(128)} %bitcast.core_ref.lead_ref, f32[4,136,128]{2,1,0:T(8,128)S(1)} %get-tuple-element.109.mine_ref, f32[4,136,128]{2,1,0:T(8,128)S(1)} %collective-permute-done.3.other_ref), custom_call_target="tpu_custom_call" | custom-call | tf_op jit(solution)/shard_map/combine/pallas_call | solution.py:582
  60.7 3.6 %all-to-all-start.3 = ((f32[16,40,128]{2,1,0:T(8,128)}), f32[16,40,128]{2,1,0:T(8,128)S(1)}, u32[]{:S(2)}, u32[]{:S(2)}) async-start(f32[16,40,128]{2,1,0:T(8,128)} %get-tuple-element.111), calls=%async_computation.3 | async-start | bytes 655360 | tf_op jit(solution)/shard_map/all_to_all | solution.py:575
  64.3 6.5 %back.1 = (bf16[512,1024]{1,0:T(8,128)(2,1)}, bf16[512,1024]{1,0:T(8,128)(2,1)S(1)}) custom-call(f32[8,512]{1,0:T(8,128)} %copy-done.2, bf16[512,1024]{1,0:T(8,128)(2,1)} %q_hbm.5, bf16[512,1024]{1,0:T(8,128)(2,1)} %k_hbm.7, bf16[512,1024]{1,0:T(8,128)(2,1)} %v_hbm.7, bf16[512,1024]{1,0:T(8,128)(2,1)} %get-tuple-element.122.grad_hbm, f32[8,128,128]{2,1,0:T(8,128)} %copy-done.1), custom_call_target="tpu_custom_call" | custom-call | tf_op jit(solution)/shard_map/back/pallas_call | solution.py:582
  70.8 2.1 %all-to-all-done.3.refs_0_ = f32[16,40,128]{2,1,0:T(8,128)S(1)} async-done(((f32[16,40,128]{2,1,0:T(8,128)}), f32[16,40,128]{2,1,0:T(8,128)S(1)}, u32[]{:S(2)}, u32[]{:S(2)}) %all-to-all-start.3) | async-done | bytes 327712 | tf_op jit(solution)/shard_map/all_to_all | solution.py:575
  73.6 4.6 %all-to-all-start.4 = ((f32[16,32,128]{2,1,0:T(8,128)}), f32[16,32,128]{2,1,0:T(8,128)S(1)}, u32[]{:S(2)}, u32[]{:S(2)}) async-start(f32[16,32,128]{2,1,0:T(8,128)} %scan.3), calls=%async_computation.4 | async-start | bytes 524288 | tf_op jit(solution)/shard_map/all_to_all | solution.py:575
  78.2 6.3 %value_gate.1 = (bf16[512,1024]{1,0:T(8,128)(2,1)}, bf16[512,1024]{1,0:T(8,128)(2,1)}, bf16[512,1024]{1,0:T(8,128)(2,1)S(1)}) custom-call(f32[8,128]{1,0:T(8,128)} %get-tuple-element.121.table_hbm, f32[512,1024]{1,0:T(8,128)} %copy-done, bf16[512,1024]{1,0:T(8,128)(2,1)} %gate_hbm.3, bf16[512,1024]{1,0:T(8,128)(2,1)} %up_hbm.3, ...), custom_call_target="tpu_custom_call" | custom-call | tf_op jit(solution)/shard_map/value_gate/pallas_call | solution.py:582
  84.5 1.1 %all-to-all-done.4 = f32[16,32,128]{2,1,0:T(8,128)S(1)} async-done(((f32[16,32,128]{2,1,0:T(8,128)}), f32[16,32,128]{2,1,0:T(8,128)S(1)}, u32[]{:S(2)}, u32[]{:S(2)}) %all-to-all-start.4) | async-done | bytes 262176 | tf_op jit(solution)/shard_map/all_to_all | solution.py:575
  85.7 2.0 %collective-permute-start.5 = (f32[4,136,128]{2,1,0:T(8,128)S(1)}, f32[4,136,128]{2,1,0:T(8,128)S(1)}, u32[]{:S(2)}, u32[]{:S(2)}) collective-permute-start(f32[4,136,128]{2,1,0:T(8,128)S(1)} %copy-done.3), channel_id=1, source_target_pairs={{0,8},{8,0},{1,9},{9,1},{2,10},{10,2},{3,11},{11,3},{4,12},{12,4},... | collective-permute-start | bytes 835592 | tf_op jit(solution)/shard_map/ppermute | solution.py:571
  87.7 2.1 %final_mine.1 = (bf16[512,512]{1,0:T(8,128)(2,1)S(1)}, bf16[512,512]{1,0:T(8,128)(2,1)S(1)}, bf16[512,512]{1,0:T(8,128)(2,1)S(1)}, bf16[512,512]{1,0:T(8,128)(2,1)S(1)}, f32[8,512]{1,0:T(8,128)S(1)}) custom-call(s32[1]{0:T(128)} %bitcast.core_ref.lead_ref, f32[4,128,128]{2,1,0:T(8,128)S(1)} %bitcast.7, ...), custom_call_target="tpu_custom_call" | custom-call | tf_op jit(solution)/shard_map/final_mine/pallas_call | solution.py:582
  89.8 1.6 %final_other.1 = (bf16[512,1024]{1,0:T(8,128)(2,1)}, bf16[512,1024]{1,0:T(8,128)(2,1)}) custom-call(s32[1]{0:T(128)} %bitcast.core_ref.lead_ref, f32[4,128,128]{2,1,0:T(8,128)S(1)} %collective-permute-done.4.chip_ref, f32[4,136,128]{2,1,0:T(8,128)S(1)} %collective-permute-done.5.lead_ref, f32[8,512]{1,0:T(8,128)S(1)} %get-tuple-element.135.within_ref, ...), custom_call_target="tpu_custom_call" | custom-call | tf_op jit(solution)/shard_map/final_other/pallas_call | solution.py:582
  (23 shorter events, 4.5 us)
Async XLA Ops:
  2.7 10.6 %copy-start.2 = (f32[8,512]{1,0:T(8,128)}, f32[8,512]{1,0:T(8,128)S(1)}, u32[]{:S(2)}) copy-start(f32[8,512]{1,0:T(8,128)S(1)} %get-tuple-element.86.within_ref.within_hbm) | copy-start | bytes 49156
  2.7 4.5 %collective-permute-start = (f32[4,136,128]{2,1,0:T(8,128)S(1)}, f32[4,136,128]{2,1,0:T(8,128)S(1)}, u32[]{:S(2)}, u32[]{:S(2)}) collective-permute-start(f32[4,136,128]{2,1,0:T(8,128)S(1)} %get-tuple-element.77), channel_id=1, source_target_pairs={{0,8},{8,0},{1,9},{9,1},{2,10},{10,2},{3,11},{11,3},{4,12},{12,4},... | collective-permute-start | bytes 835592 | tf_op jit(solution)/shard_map/ppermute | solution.py:571
  8.2 13.0 %all-to-all-start = ((f32[16,40,128]{2,1,0:T(8,128)}), f32[16,40,128]{2,1,0:T(8,128)S(1)}, u32[]{:S(2)}, u32[]{:S(2)}) async-start(f32[16,40,128]{2,1,0:T(8,128)} %get-tuple-element.78), calls=%async_computation | async-start | bytes 655360 | tf_op jit(solution)/shard_map/all_to_all | solution.py:575
  21.2 12.2 %copy-start.4 = (f32[4,136,128]{2,1,0:T(8,128)S(1)}, f32[4,136,128]{2,1,0:T(8,128)}, u32[]{:S(2)}) copy-start(f32[4,136,128]{2,1,0:T(8,128)} %get-tuple-element.90) | copy-start | bytes 835588
  22.0 11.4 %all-to-all-start.1 = ((f32[16,32,128]{2,1,0:T(8,128)}), f32[16,32,128]{2,1,0:T(8,128)S(1)}, u32[]{:S(2)}, u32[]{:S(2)}) async-start(f32[16,32,128]{2,1,0:T(8,128)} %scan.2), calls=%async_computation.1 | async-start | bytes 524288 | tf_op jit(solution)/shard_map/all_to_all | solution.py:575
  33.4 5.9 %collective-permute-start.2 = (f32[4,136,128]{2,1,0:T(8,128)S(1)}, f32[4,136,128]{2,1,0:T(8,128)S(1)}, u32[]{:S(2)}, u32[]{:S(2)}) collective-permute-start(f32[4,136,128]{2,1,0:T(8,128)S(1)} %copy-done.4), channel_id=1, source_target_pairs={{0,8},{8,0},{1,9},{9,1},{2,10},{10,2},{3,11},{11,3},{4,12},{12,4},... | collective-permute-start | bytes 835592 | tf_op jit(solution)/shard_map/ppermute | solution.py:571
  36.3 3.0 %collective-permute-start.1 = (f32[4,128,128]{2,1,0:T(8,128)S(1)}, f32[4,128,128]{2,1,0:T(8,128)S(1)}, u32[]{:S(2)}, u32[]{:S(2)}) collective-permute-start(f32[4,128,128]{2,1,0:T(8,128)S(1)} %bitcast.4), channel_id=1, source_target_pairs={{0,8},{8,0},{1,9},{9,1},{2,10},{10,2},{3,11},{11,3},{4,12},{12,4},... | collective-permute-start | bytes 786440 | tf_op jit(solution)/shard_map/ppermute | solution.py:571
  40.6 15.7 %copy-start.1 = (f32[8,128,128]{2,1,0:T(8,128)}, f32[8,128,128]{2,1,0:T(8,128)S(1)}, u32[]{:S(2)}) copy-start(f32[8,128,128]{2,1,0:T(8,128)S(1)} %get-tuple-element.113.state_hbm) | copy-start | bytes 1572868
  40.6 17.7 %copy-start = (f32[512,1024]{1,0:T(8,128)}, f32[512,1024]{1,0:T(8,128)S(1)}, u32[]{:S(2)}) copy-start(f32[512,1024]{1,0:T(8,128)S(1)} %get-tuple-element.104.attn_ref.attn_hbm) | copy-start | bytes 6291460
  56.3 3.4 %collective-permute-start.3 = (f32[4,136,128]{2,1,0:T(8,128)S(1)}, f32[4,136,128]{2,1,0:T(8,128)S(1)}, u32[]{:S(2)}, u32[]{:S(2)}) collective-permute-start(f32[4,136,128]{2,1,0:T(8,128)S(1)} %get-tuple-element.110), channel_id=1, source_target_pairs={{0,8},{8,0},{1,9},{9,1},{2,10},{10,2},{3,11},{11,3},{4,12},{12,4},... | collective-permute-start | bytes 835592 | tf_op jit(solution)/shard_map/ppermute | solution.py:571
  60.7 12.1 %all-to-all-start.3 = ((f32[16,40,128]{2,1,0:T(8,128)}), f32[16,40,128]{2,1,0:T(8,128)S(1)}, u32[]{:S(2)}, u32[]{:S(2)}) async-start(f32[16,40,128]{2,1,0:T(8,128)} %get-tuple-element.111), calls=%async_computation.3 | async-start | bytes 655360 | tf_op jit(solution)/shard_map/all_to_all | solution.py:575
  73.6 12.0 %all-to-all-start.4 = ((f32[16,32,128]{2,1,0:T(8,128)}), f32[16,32,128]{2,1,0:T(8,128)S(1)}, u32[]{:S(2)}, u32[]{:S(2)}) async-start(f32[16,32,128]{2,1,0:T(8,128)} %scan.3), calls=%async_computation.4 | async-start | bytes 524288 | tf_op jit(solution)/shard_map/all_to_all | solution.py:575
  78.2 7.5 %copy-start.3 = (f32[4,136,128]{2,1,0:T(8,128)S(1)}, f32[4,136,128]{2,1,0:T(8,128)}, u32[]{:S(2)}) copy-start(f32[4,136,128]{2,1,0:T(8,128)} %get-tuple-element.131) | copy-start | bytes 835588
  85.7 4.1 %collective-permute-start.5 = (f32[4,136,128]{2,1,0:T(8,128)S(1)}, f32[4,136,128]{2,1,0:T(8,128)S(1)}, u32[]{:S(2)}, u32[]{:S(2)}) collective-permute-start(f32[4,136,128]{2,1,0:T(8,128)S(1)} %copy-done.3), channel_id=1, source_target_pairs={{0,8},{8,0},{1,9},{9,1},{2,10},{10,2},{3,11},{11,3},{4,12},{12,4},... | collective-permute-start | bytes 835592 | tf_op jit(solution)/shard_map/ppermute | solution.py:571
  87.6 2.1 %collective-permute-start.4 = (f32[4,128,128]{2,1,0:T(8,128)S(1)}, f32[4,128,128]{2,1,0:T(8,128)S(1)}, u32[]{:S(2)}, u32[]{:S(2)}) collective-permute-start(f32[4,128,128]{2,1,0:T(8,128)S(1)} %bitcast.6), channel_id=1, source_target_pairs={{0,8},{8,0},{1,9},{9,1},{2,10},{10,2},{3,11},{11,3},{4,12},{12,4},... | collective-permute-start | bytes 786440 | tf_op jit(solution)/shard_map/ppermute | solution.py:571

commit v8 on v7

--- a/solution.py
+++ b/solution.py
@@ -167,7 +167,8 @@
         both = jnp.where(lead, far[0:1] * mine + other, own[0:1] * other + mine)
         for j in range(4):
             out_ref[4 * i + j, 0:rows, :] = both[j * rows : (j + 1) * rows]
-            out_ref[4 * i + j, rows : rows + PAD, :] = own * far
+            if out_ref.shape[1] > rows:
+                out_ref[4 * i + j, rows : rows + PAD, :] = own * far
         part = pl.ds(4 * i, 4)
         store = pltpu.make_async_copy(out_ref.at[part], out_hbm.at[part], sems.at[2 + i])
         store.start()
@@ -176,13 +177,24 @@
     wait(made)
 
 
-def scan_kernel(reverse, in_ref, out_hbm, out_ref, sems):
+def scan_kernel(in_ref, out_hbm, decay_ref, out_ref, sems):
     chips, rows = out_ref.shape[0], out_ref.shape[1]
     state = jnp.zeros(out_ref.shape[1:], F32)
-    made = []
-    for n in reversed(range(chips)) if reverse else range(chips):
+    for n in range(chips):
         out_ref[n] = state
         state = in_ref[n, rows : rows + 1, :] * state + in_ref[n, 0:rows, :]
+        decay_ref[n] = in_ref[n, rows : rows + PAD, :]
+    made = copies([(out_ref, out_hbm)], sems)
+    start(made)
+    wait(made)
+
+
+def scan_back_kernel(in_ref, decay_ref, out_hbm, out_ref, sems):
+    chips = out_ref.shape[0]
+    state = jnp.zeros(out_ref.shape[1:], F32)
+    for n in reversed(range(chips)):
+        out_ref[n] = state
+        state = decay_ref[n, 0:1, :] * state + in_ref[n]
     made = copies([(out_ref, out_hbm)], sems)
     start(made)
     wait(made)
@@ -250,25 +262,16 @@
     each_head(heads, lambda h: wait(results(h)))
 
 
-def prepare_kernel(
-    within_hbm, q_hbm, gate_hbm, up_hbm, dnorm_hbm, grown_hbm,
-    within_ref, q_ref, gate_ref, up_ref, dnorm_ref, grown_ref, sem, in_sems, out_sems,
-):
-    heads = within_ref.shape[0]
-    small = copies([(within_hbm, within_ref)], sem)
-    start(small)
-    loads = [(q_hbm, q_ref, 1), (gate_hbm, gate_ref, 1), (up_hbm, up_ref, 1)]
-    stores = [(dnorm_ref, dnorm_hbm, 1), (grown_ref, grown_hbm, 2)]
+def prepare_kernel(gate_hbm, up_hbm, dnorm_hbm, gate_ref, up_ref, dnorm_ref, in_sems, out_sems):
+    heads = in_sems.shape[1]
+    loads = [(gate_hbm, gate_ref, 1), (up_hbm, up_ref, 1)]
+    stores = [(dnorm_ref, dnorm_hbm, 1)]
     each_head(heads, lambda h: start(head_copies(loads, in_sems, h)))
-    wait(small)
 
     def one(h):
-        grow = as_column(jnp.exp(within_ref[pl.ds(h, 1), :]))
         dnorm_ref[:, lanes(h)] = up_ref[:, lanes(h)].astype(F32) * sigmoid(
             gate_ref[:, lanes(h)].astype(F32)
         )
-        grown = q_ref[:, lanes(h)].astype(F32) * grow
-        grown_ref[:, lanes(h, 2)] = jnp.concatenate(halves(grown), axis=1)
 
     each_pair(
         heads, lambda h: wait(head_copies(loads, in_sems, h)), one,
@@ -298,34 +301,45 @@
     return attn * attn, dnorm_ref[:, lanes(head)] * attn
 
 
+def make_grown(head, q, within_ref, grown_ref):
+    grown = q.astype(F32) * as_column(jnp.exp(within_ref[pl.ds(head, 1), :]))
+    grown_ref[:, lanes(head, 2)] = jnp.concatenate(halves(grown), axis=1)
+
+
 def attn_mine_kernel(
-    core_ref, chip_ref, within_hbm, lead_hbm, grown_hbm, intra_hbm, dnorm_hbm,
+    core_ref, chip_ref, within_hbm, lead_hbm, q_hbm, intra_hbm, dnorm_hbm,
     attn_ref, dnorm_ref, grown_ref, state_ref, square_ref, inner_ref, intra_far, within_ref,
-    lead_ref, intra_ref, sems,
+    lead_ref, intra_ref, q_ref, q_far, sems,
 ):
     core = core_ref[0]
     group = chip_ref.shape[0]
-    pairs = [(lead_hbm, lead_ref)]
-    for half, target in ((core, intra_ref), (1 - core, intra_far)):
-        wide, two = half_of(half, group), half_of(half, group, 2)
+    pairs = [(within_hbm, within_ref), (lead_hbm, lead_ref)]
+    for half, q, intra in ((core, q_ref, intra_ref), (1 - core, q_far, intra_far)):
+        wide = half_of(half, group)
         pairs += [
-            (grown_hbm.at[:, two], grown_ref.at[:, two]),
-            (intra_hbm.at[:, wide], target),
+            (q_hbm.at[:, wide], q),
+            (intra_hbm.at[:, wide], intra),
             (dnorm_hbm.at[:, wide], dnorm_ref.at[:, wide]),
         ]
-    made = copies(pairs + [(within_hbm, within_ref)], sems)
+    made = copies(pairs, sems)
     start(made)
-    wait(made[:4])
+    wait(made[:5])
     square = inner = jnp.zeros(square_ref.shape, F32)
     for i in range(group):
+        cols = slice(i * HEAD, (i + 1) * HEAD)
+        head = core * group + i
+        make_grown(head, q_ref[:, cols], within_ref, grown_ref)
         more = attn_head(
-            core, core * group + i, i, slice(i * HEAD, (i + 1) * HEAD), grown_ref, intra_ref,
-            dnorm_ref, chip_ref, lead_ref, attn_ref, state_ref,
+            core, head, i, cols, grown_ref, intra_ref, dnorm_ref, chip_ref, lead_ref, attn_ref, state_ref
         )
         square, inner = square + more[0], inner + more[1]
     square_ref[...] = square
     inner_ref[...] = inner
-    wait(made[4:])
+    made[5].wait()
+    for i in range(group):
+        cols = slice(i * HEAD, (i + 1) * HEAD)
+        make_grown((1 - core) * group + i, q_far[:, cols], within_ref, grown_ref)
+    wait(made[6:])
 
 
 def attn_other_kernel(
@@ -621,16 +635,18 @@
     rates = shape((heads, tokens))
     table_of = shape((heads, tokens, tokens), BF16)
 
-    def combined(lead, mine, other):
+    def combined(lead, mine, other, sent):
         return call(
-            combine_kernel, "combine", (mine, other), (), (), (carried, packed, packed), (carried,), ((2 + group,),),
+            combine_kernel, "combine", (mine, other), (), (), (sent, packed, packed), (sent,), ((2 + group,),),
             lead,
         )
 
-    def scanned(x, reverse):
-        (out,) = call(
-            lambda *refs: scan_kernel(reverse, *refs), "scan", (x,), (), (), (sliced,), (sliced,), ((1,),)
-        )
+    def scanned(x, decays=None):
+        if decays is None:
+            return call(
+                scan_kernel, "scan", (x,), (), (shape((chips, PAD, HEAD)),), (sliced,), (sliced,), ((1,),)
+            )
+        (out,) = call(scan_back_kernel, "scan_back", (x, decays), (), (), (sliced,), (sliced,), ((1,),))
         return out
 
     within, theirs, k_near, v_near = call(
@@ -641,27 +657,28 @@
     (mine,) = call(
         local_mine_kernel, "local_mine", (within, k_near, v_near), (), (packed,), (), (), (), core
     )
-    chip_state, mine, lead_mine = combined(1 - core, mine, lead_mine)
+    chip_state, mine, lead_mine = combined(1 - core, mine, lead_mine, carried)
     chip_state = spread(chip_state)
+    lead_other = swap(mine)
     probs, intra = call(
         inside_kernel, "inside", (), (within, queries, keys, values), (), (table_of, wide),
         (rates, narrow, narrow, narrow, table_of, wide), ((1,), (3, heads), (3, heads)),
     )
-    chip_state, probs, intra, mine, within = lax.optimization_barrier(
-        (chip_state, probs, intra, mine, within)
-    )
-    chip_state, within = lax.optimization_barrier((scanned(chip_state, False), within))
+    chip_state, probs, intra = lax.optimization_barrier((chip_state, probs, intra))
+    chip_state, decays = scanned(chip_state)
+    chip_state, out_grad = lax.optimization_barrier((chip_state, out_grad))
     chip_mine = spread(chip_state)
-    dnorm, grown = call(
-        prepare_kernel, "prepare", (), (within, queries, gate, out_grad), (), (wide, double),
-        (rates, narrow, narrow, narrow, wide, double), ((1,), (3, heads), (2, heads)),
-    )
-    chip_mine, mine, dnorm, grown = lax.optimization_barrier((chip_mine, mine, dnorm, grown))
+    (dnorm,) = call(
+        prepare_kernel, "prepare", (), (gate, out_grad), (), (wide,), (narrow, narrow, wide),
+        ((2, heads), (1, heads)),
+    )
+    chip_mine, dnorm = lax.optimization_barrier((chip_mine, dnorm))
     chip_mine = chip_mine.reshape(group, HEAD, HEAD)
-    chip_other, lead_other = swap(chip_mine), swap(mine)
+    chip_other = swap(chip_mine)
     attn, dnorm, grown, state, square, inner, intra_far, within_near = call(
-        attn_mine_kernel, "attn_mine", (chip_mine,), (within, lead_mine, grown, intra, dnorm),
-        (wide, wide, double, states, column, column, half, rates), (), (packed, half), ((8,),), core,
+        attn_mine_kernel, "attn_mine", (chip_mine,), (within, lead_mine, queries, intra, dnorm),
+        (wide, wide, double, states, column, column, half, rates), (), (packed, half, half_narrow, half_narrow),
+        ((8,),), core,
     )
     attn, state, sums = call(
         attn_other_kernel, "attn_other",
@@ -679,27 +696,26 @@
         (scale, center, table, within_near, grown, attn, dnorm, grad_far), (),
         (packed,), (narrow, table_rows), (half_narrow,), ((group,), (2,)), core,
     )
-    chip_state, mine, lead_mine = combined(core, mine, lead_mine)
+    chip_state, mine, lead_mine = combined(core, mine, lead_mine, sliced)
     chip_state = spread(chip_state)
+    lead_other = swap(mine)
     query_grad, key_part = call(
         back_kernel, "back", (), (within, queries, keys, values, grad, state), (narrow,), (narrow,),
         (rates, narrow, narrow, narrow, narrow, states, narrow), ((1,), (5, heads), (1, heads)),
     )
-    chip_state, key_part, mine, grad, table = lax.optimization_barrier(
-        (chip_state, key_part, mine, grad, table)
-    )
-    chip_state, grad, table = lax.optimization_barrier((scanned(chip_state, True), grad, table))
+    chip_state, key_part, grad, table = lax.optimization_barrier((chip_state, key_part, grad, table))
+    chip_state, grad, table = lax.optimization_barrier((scanned(chip_state, decays), grad, table))
     chip_mine = spread(chip_state)
     output, gate_grad, value_part = call(
         value_gate_kernel, "value_gate", (), (table, attn, gate, out_grad, grad, probs), (narrow,), (narrow, narrow),
         (table_rows, wide, narrow, narrow, narrow, table_of, narrow, narrow, column),
         ((1,), (6, heads), (2, heads)), mib=24,
     )
-    chip_mine, value_part, output, gate_grad, mine = lax.optimization_barrier(
-        (chip_mine, value_part, output, gate_grad, mine)
+    chip_mine, value_part, output, gate_grad = lax.optimization_barrier(
+        (chip_mine, value_part, output, gate_grad)
     )
     chip_mine = chip_mine.reshape(group, HEAD, HEAD)
-    chip_other, lead_other = swap(chip_mine), swap(mine)
+    chip_other = swap(chip_mine)
     key_near, value_near, k_far, v_far, within_near = call(
         final_mine_kernel, "final_mine", (chip_mine, key_part, value_part), (within, lead_mine, keys, values),
         (half_narrow,) * 4 + (rates,), (), (packed, half_narrow, half_narrow), ((6,),), core,

time: 92.3 us -> 92 us (level)
  starting transfers between devices: 27.5 us -> 30.9 us
  waiting for transfers between devices: 9.29 us -> 6.72 us
  Pallas kernels: 38.8 us -> 37.6 us
    all_to_all x4, waiting for transfers between devices: 8.9 us -> 6.33 us  [spread(): return lax.all_to_all(x, CHIPS, split_axis=0, concat_axis=0, tiled=True)]
    ppermute x6, starting transfers between devices: 10.3 us -> 12.7 us  [swap(): return lax.ppermute(x, 'c', [(0, 1), (1, 0)])]
    pallas_call x16, Pallas kernels: 38.8 us -> 37.6 us  [call(): pl.pallas_call(kernel, grid_spec=pltpu.PrefetchScalarGridSpec(num_scalar_...]
    all_to_all x4, starting transfers between devices: 17.2 us -> 18.2 us  [spread(): return lax.all_to_all(x, CHIPS, split_axis=0, concat_axis=0, tiled=True)]
  transfers between devices with their start and end apart: 10 -> 10, of which waited for: 5 -> 4; matrix products, arithmetic and copies ran while one was open for 0% -> 0% of each run, Pallas kernels for 32% -> 31%
where the time goes in v8:
time: 92 us; the launch traced here: 91.2 us
  Pallas kernels  37.6 us (41%)
  starting transfers between devices  30.9 us (34%)
  blocking collectives  14.9 us (16%)
  waiting for transfers between devices  6.72 us (7%)
  between operations  1.06 us (1%)
    pallas_call x16, Pallas kernels, call(): pl.pallas_call(kernel, grid_spec=pltpu.PrefetchScalarGridSpec(num_scalar_...  37.6 us
    all_to_all x4, starting transfers between devices, spread(): return lax.all_to_all(x, CHIPS, split_axis=0, concat_axis=0, tiled=True)  18.2 us
    all_to_all x1, blocking collectives, shards(): sums = lax.all_to_all(sums, 'tp', split_axis=0, concat_axis=0, tiled=True)  14.9 us
    ppermute x6, starting transfers between devices, swap(): return lax.ppermute(x, 'c', [(0, 1), (1, 0)])  12.7 us
    all_to_all x4, waiting for transfers between devices, spread(): return lax.all_to_all(x, CHIPS, split_axis=0, concat_axis=0, tiled=True)  6.33 us
  transfers between devices with their start and end apart: 10, of which 4 were waited for; matrix products, arithmetic and copies ran while one was open for 0% of the time, Pallas kernels for 31%

profile of v8, /device:TPU:1, one launch (start us, length us, event | category | flops | bytes accessed | tf_op | source)
XLA Modules:
  0.0 91.2 jit_solution(9813738758383635426)
XLA Ops:
  0.6 2.1 %local_other.1 = (f32[8,512]{1,0:T(8,128)S(1)}, f32[4,136,128]{2,1,0:T(8,128)S(1)}, bf16[512,512]{1,0:T(8,128)(2,1)S(1)}, bf16[512,512]{1,0:T(8,128)(2,1)S(1)}) custom-call(s32[1]{0:T(128)} %bitcast.core_ref.lead_ref, f32[8,512]{1,0:T(8,128)} %bitcast.8, bf16[512,1024]{1,0:T(8,128)(2,1)} %k_hbm.7, bf16[512,1024]{1,0:T(8,128)(2,1)} %v_hbm.7), custom_call_target="tpu_custom_call" | custom-call | tf_op jit(solution)/shard_map/local_other/pallas_call | solution.py:596
  2.7 3.3 %collective-permute-start = (f32[4,136,128]{2,1,0:T(8,128)S(1)}, f32[4,136,128]{2,1,0:T(8,128)S(1)}, u32[]{:S(2)}, u32[]{:S(2)}) collective-permute-start(f32[4,136,128]{2,1,0:T(8,128)S(1)} %get-tuple-element.71), channel_id=1, source_target_pairs={{0,8},{8,0},{1,9},{9,1},{2,10},{10,2},{3,11},{11,3},{4,12},{12,4},... | collective-permute-start | bytes 835592 | tf_op jit(solution)/shard_map/ppermute | solution.py:585
  8.3 5.0 %all-to-all-start = ((f32[16,40,128]{2,1,0:T(8,128)}), f32[16,40,128]{2,1,0:T(8,128)S(1)}, u32[]{:S(2)}, u32[]{:S(2)}) async-start(f32[16,40,128]{2,1,0:T(8,128)} %get-tuple-element.72), calls=%async_computation | async-start | bytes 655360 | tf_op jit(solution)/shard_map/all_to_all | solution.py:589
  13.3 5.3 %inside.1 = (bf16[8,512,512]{2,1,0:T(8,128)(2,1)}, f32[512,1024]{1,0:T(8,128)}) custom-call(f32[8,512]{1,0:T(8,128)} %copy-done.2, bf16[512,1024]{1,0:T(8,128)(2,1)} %q_hbm.5, bf16[512,1024]{1,0:T(8,128)(2,1)} %k_hbm.7, bf16[512,1024]{1,0:T(8,128)(2,1)} %v_hbm.7), custom_call_target="tpu_custom_call" | custom-call | tf_op jit(solution)/shard_map/inside/pallas_call | solution.py:596
  18.7 2.6 %all-to-all-done.in_ref = f32[16,40,128]{2,1,0:T(8,128)S(1)} async-done(((f32[16,40,128]{2,1,0:T(8,128)}), f32[16,40,128]{2,1,0:T(8,128)S(1)}, u32[]{:S(2)}, u32[]{:S(2)}) %all-to-all-start) | async-done | bytes 327712 | tf_op jit(solution)/shard_map/all_to_all | solution.py:589
  22.0 4.1 %all-to-all-start.1 = ((f32[16,32,128]{2,1,0:T(8,128)}), f32[16,32,128]{2,1,0:T(8,128)S(1)}, u32[]{:S(2)}, u32[]{:S(2)}) async-start(f32[16,32,128]{2,1,0:T(8,128)} %get-tuple-element.77), calls=%async_computation.1 | async-start | bytes 524288 | tf_op jit(solution)/shard_map/all_to_all | solution.py:589
  26.1 1.8 %collective-permute-start.2 = (f32[4,136,128]{2,1,0:T(8,128)S(1)}, f32[4,136,128]{2,1,0:T(8,128)S(1)}, u32[]{:S(2)}, u32[]{:S(2)}) collective-permute-start(f32[4,136,128]{2,1,0:T(8,128)S(1)} %copy-done.4), channel_id=1, source_target_pairs={{0,8},{8,0},{1,9},{9,1},{2,10},{10,2},{3,11},{11,3},{4,12},{12,4},... | collective-permute-start | bytes 835592 | tf_op jit(solution)/shard_map/ppermute | solution.py:585
  27.9 2.9 %prepare.1.dnorm_hbm = f32[512,1024]{1,0:T(8,128)} custom-call(bf16[512,1024]{1,0:T(8,128)(2,1)} %gate_hbm.3, bf16[512,1024]{1,0:T(8,128)(2,1)} %up_hbm.1), custom_call_target="tpu_custom_call" | custom-call | tf_op jit(solution)/shard_map/prepare/pallas_call | solution.py:596
  30.8 2.6 %all-to-all-done.1 = f32[16,32,128]{2,1,0:T(8,128)S(1)} async-done(((f32[16,32,128]{2,1,0:T(8,128)}), f32[16,32,128]{2,1,0:T(8,128)S(1)}, u32[]{:S(2)}, u32[]{:S(2)}) %all-to-all-start.1) | async-done | bytes 262176 | tf_op jit(solution)/shard_map/all_to_all | solution.py:589
  33.4 2.9 %collective-permute-start.1 = (f32[4,128,128]{2,1,0:T(8,128)S(1)}, f32[4,128,128]{2,1,0:T(8,128)S(1)}, u32[]{:S(2)}, u32[]{:S(2)}) collective-permute-start(f32[4,128,128]{2,1,0:T(8,128)S(1)} %bitcast.6), channel_id=1, source_target_pairs={{0,8},{8,0},{1,9},{9,1},{2,10},{10,2},{3,11},{11,3},{4,12},{12,4},... | collective-permute-start | bytes 786440 | tf_op jit(solution)/shard_map/ppermute | solution.py:585
  36.3 3.1 %attn_mine.1 = (f32[512,1024]{1,0:T(8,128)S(1)}, f32[512,1024]{1,0:T(8,128)S(1)}, bf16[512,2048]{1,0:T(8,128)(2,1)S(1)}, f32[8,128,128]{2,1,0:T(8,128)S(1)}, f32...) custom-call(s32[1]{0:T(128)} %bitcast.core_ref.lead_ref, ...), custom_call_target="tpu_custom_call" | custom-call | tf_op jit(solution)/shard_map/attn_mine/pallas_call | solution.py:596
  39.4 1.3 %attn_other.1 = (f32[512,1024]{1,0:T(8,128)S(1)}, f32[8,128,128]{2,1,0:T(8,128)S(1)}, f32[8,8,128]{2,1,0:T(8,128)S(1)}) custom-call(s32[1]{0:T(128)} %bitcast.core_ref.lead_ref, f32[4,128,128]{2,1,0:T(8,128)S(1)} %collective-permute-done.1.chip_ref, ...), custom_call_target="tpu_custom_call", output_to_operand_aliasing={{0}: (8, {}), {1}: (9, {})} | custom-call | tf_op jit(solution)/shard_map/attn_other/pallas_call | solution.py:596
  40.7 14.9 %all_to_all.25.sums_ref = f32[8,8,128]{2,1,0:T(8,128)S(1)} all-to-all(f32[8,8,128]{2,1,0:T(8,128)S(1)} %get-tuple-element.91), channel_id=1, replica_groups=mesh['x'=4,'y'=4,'c'=2,'tp'=8] {'tp'}, dimensions={0} | all-to-all | bytes 65536 | tf_op jit(solution)/shard_map/all_to_all | solution.py:688
  56.4 1.5 %collective-permute-start.3 = (f32[4,136,128]{2,1,0:T(8,128)S(1)}, f32[4,136,128]{2,1,0:T(8,128)S(1)}, u32[]{:S(2)}, u32[]{:S(2)}) collective-permute-start(f32[4,136,128]{2,1,0:T(8,128)S(1)} %get-tuple-element.99), channel_id=1, source_target_pairs={{0,8},{8,0},{1,9},{9,1},{2,10},{10,2},{3,11},{11,3},{4,12},{12,4},... | collective-permute-start | bytes 835592 | tf_op jit(solution)/shard_map/ppermute | solution.py:585
  57.9 1.4 %grad_mine.1 = (bf16[512,1024]{1,0:T(8,128)(2,1)}, f32[8,128]{1,0:T(8,128)}, f32[4,136,128]{2,1,0:T(8,128)S(1)}) custom-call(s32[1]{0:T(128)} %bitcast.core_ref.lead_ref, f32[512,128]{1,0:T(8,128)S(1)} %get-tuple-element.94.scale_ref, f32[512,128]{1,0:T(8,128)S(1)} %get-tuple-element.95.center_ref, f32[8,128]{1,0:T(8,128)S(1)} %get-tuple-element.96.table_ref, ...), custom_call_target="tpu_custom_call" | custom-call | tf_op jit(solution)/shard_map/grad_mine/pallas_call | solution.py:596
  60.3 3.5 %all-to-all-start.3 = ((f32[16,32,128]{2,1,0:T(8,128)}), f32[16,32,128]{2,1,0:T(8,128)S(1)}, u32[]{:S(2)}, u32[]{:S(2)}) async-start(f32[16,32,128]{2,1,0:T(8,128)} %get-tuple-element.100), calls=%async_computation.3 | async-start | bytes 524288 | tf_op jit(solution)/shard_map/all_to_all | solution.py:589
  63.9 6.5 %back.1 = (bf16[512,1024]{1,0:T(8,128)(2,1)}, bf16[512,1024]{1,0:T(8,128)(2,1)S(1)}) custom-call(f32[8,512]{1,0:T(8,128)} %copy-done.2, bf16[512,1024]{1,0:T(8,128)(2,1)} %q_hbm.5, bf16[512,1024]{1,0:T(8,128)(2,1)} %k_hbm.7, bf16[512,1024]{1,0:T(8,128)(2,1)} %v_hbm.7, bf16[512,1024]{1,0:T(8,128)(2,1)} %get-tuple-element.111.grad_hbm, f32[8,128,128]{2,1,0:T(8,128)} %copy-done.1), custom_call_target="tpu_custom_call" | custom-call | tf_op jit(solution)/shard_map/back/pallas_call | solution.py:596
  70.4 1.2 %all-to-all-done.3.in_ref = f32[16,32,128]{2,1,0:T(8,128)S(1)} async-done(((f32[16,32,128]{2,1,0:T(8,128)}), f32[16,32,128]{2,1,0:T(8,128)S(1)}, u32[]{:S(2)}, u32[]{:S(2)}) %all-to-all-start.3) | async-done | bytes 262176 | tf_op jit(solution)/shard_map/all_to_all | solution.py:589
  72.3 5.5 %all-to-all-start.4 = ((f32[16,32,128]{2,1,0:T(8,128)}), f32[16,32,128]{2,1,0:T(8,128)S(1)}, u32[]{:S(2)}, u32[]{:S(2)}) async-start(f32[16,32,128]{2,1,0:T(8,128)} %scan_back.1), calls=%async_computation.4 | async-start | bytes 524288 | tf_op jit(solution)/shard_map/all_to_all | solution.py:589
  77.8 1.2 %collective-permute-start.5 = (f32[4,136,128]{2,1,0:T(8,128)S(1)}, f32[4,136,128]{2,1,0:T(8,128)S(1)}, u32[]{:S(2)}, u32[]{:S(2)}) collective-permute-start(f32[4,136,128]{2,1,0:T(8,128)S(1)} %copy-done.3), channel_id=1, source_target_pairs={{0,8},{8,0},{1,9},{9,1},{2,10},{10,2},{3,11},{11,3},{4,12},{12,4},... | collective-permute-start | bytes 835592 | tf_op jit(solution)/shard_map/ppermute | solution.py:585
  79.0 6.3 %value_gate.1 = (bf16[512,1024]{1,0:T(8,128)(2,1)}, bf16[512,1024]{1,0:T(8,128)(2,1)}, bf16[512,1024]{1,0:T(8,128)(2,1)S(1)}) custom-call(f32[8,128]{1,0:T(8,128)} %get-tuple-element.110.table_hbm, f32[512,1024]{1,0:T(8,128)} %copy-done, bf16[512,1024]{1,0:T(8,128)(2,1)} %gate_hbm.3, bf16[512,1024]{1,0:T(8,128)(2,1)} %up_hbm.1, ...), custom_call_target="tpu_custom_call" | custom-call | tf_op jit(solution)/shard_map/value_gate/pallas_call | solution.py:596
  85.3 2.0 %collective-permute-start.4 = (f32[4,128,128]{2,1,0:T(8,128)S(1)}, f32[4,128,128]{2,1,0:T(8,128)S(1)}, u32[]{:S(2)}, u32[]{:S(2)}) collective-permute-start(f32[4,128,128]{2,1,0:T(8,128)S(1)} %bitcast.4), channel_id=1, source_target_pairs={{0,8},{8,0},{1,9},{9,1},{2,10},{10,2},{3,11},{11,3},{4,12},{12,4},... | collective-permute-start | bytes 786440 | tf_op jit(solution)/shard_map/ppermute | solution.py:585
  87.3 2.1 %final_mine.1 = (bf16[512,512]{1,0:T(8,128)(2,1)S(1)}, bf16[512,512]{1,0:T(8,128)(2,1)S(1)}, bf16[512,512]{1,0:T(8,128)(2,1)S(1)}, bf16[512,512]{1,0:T(8,128)(2,1)S(1)}, f32[8,512]{1,0:T(8,128)S(1)}) custom-call(s32[1]{0:T(128)} %bitcast.core_ref.lead_ref, f32[4,128,128]{2,1,0:T(8,128)S(1)} %bitcast.5, ...), custom_call_target="tpu_custom_call" | custom-call | tf_op jit(solution)/shard_map/final_mine/pallas_call | solution.py:596
  89.4 1.6 %final_other.1 = (bf16[512,1024]{1,0:T(8,128)(2,1)}, bf16[512,1024]{1,0:T(8,128)(2,1)}) custom-call(s32[1]{0:T(128)} %bitcast.core_ref.lead_ref, f32[4,128,128]{2,1,0:T(8,128)S(1)} %collective-permute-done.4.chip_ref, f32[4,136,128]{2,1,0:T(8,128)S(1)} %collective-permute-done.5.lead_ref, f32[8,512]{1,0:T(8,128)S(1)} %get-tuple-element.123.within_ref, ...), custom_call_target="tpu_custom_call" | custom-call | tf_op jit(solution)/shard_map/final_other/pallas_call | solution.py:596
  (23 shorter events, 5.5 us)
Async XLA Ops:
  2.7 10.6 %copy-start.2 = (f32[8,512]{1,0:T(8,128)}, f32[8,512]{1,0:T(8,128)S(1)}, u32[]{:S(2)}) copy-start(f32[8,512]{1,0:T(8,128)S(1)} %get-tuple-element.68.within_ref.within_hbm) | copy-start | bytes 49156
  2.7 4.5 %collective-permute-start = (f32[4,136,128]{2,1,0:T(8,128)S(1)}, f32[4,136,128]{2,1,0:T(8,128)S(1)}, u32[]{:S(2)}, u32[]{:S(2)}) collective-permute-start(f32[4,136,128]{2,1,0:T(8,128)S(1)} %get-tuple-element.71), channel_id=1, source_target_pairs={{0,8},{8,0},{1,9},{9,1},{2,10},{10,2},{3,11},{11,3},{4,12},{12,4},... | collective-permute-start | bytes 835592 | tf_op jit(solution)/shard_map/ppermute | solution.py:585
  8.3 13.0 %all-to-all-start = ((f32[16,40,128]{2,1,0:T(8,128)}), f32[16,40,128]{2,1,0:T(8,128)S(1)}, u32[]{:S(2)}, u32[]{:S(2)}) async-start(f32[16,40,128]{2,1,0:T(8,128)} %get-tuple-element.72), calls=%async_computation | async-start | bytes 655360 | tf_op jit(solution)/shard_map/all_to_all | solution.py:589
  13.3 12.8 %copy-start.4 = (f32[4,136,128]{2,1,0:T(8,128)S(1)}, f32[4,136,128]{2,1,0:T(8,128)}, u32[]{:S(2)}) copy-start(f32[4,136,128]{2,1,0:T(8,128)} %get-tuple-element.80) | copy-start | bytes 835588
  22.0 11.5 %all-to-all-start.1 = ((f32[16,32,128]{2,1,0:T(8,128)}), f32[16,32,128]{2,1,0:T(8,128)S(1)}, u32[]{:S(2)}, u32[]{:S(2)}) async-start(f32[16,32,128]{2,1,0:T(8,128)} %get-tuple-element.77), calls=%async_computation.1 | async-start | bytes 524288 | tf_op jit(solution)/shard_map/all_to_all | solution.py:589
  26.1 13.3 %collective-permute-start.2 = (f32[4,136,128]{2,1,0:T(8,128)S(1)}, f32[4,136,128]{2,1,0:T(8,128)S(1)}, u32[]{:S(2)}, u32[]{:S(2)}) collective-permute-start(f32[4,136,128]{2,1,0:T(8,128)S(1)} %copy-done.4), channel_id=1, source_target_pairs={{0,8},{8,0},{1,9},{9,1},{2,10},{10,2},{3,11},{11,3},{4,12},{12,4},... | collective-permute-start | bytes 835592 | tf_op jit(solution)/shard_map/ppermute | solution.py:585
  33.4 6.0 %collective-permute-start.1 = (f32[4,128,128]{2,1,0:T(8,128)S(1)}, f32[4,128,128]{2,1,0:T(8,128)S(1)}, u32[]{:S(2)}, u32[]{:S(2)}) collective-permute-start(f32[4,128,128]{2,1,0:T(8,128)S(1)} %bitcast.6), channel_id=1, source_target_pairs={{0,8},{8,0},{1,9},{9,1},{2,10},{10,2},{3,11},{11,3},{4,12},{12,4},... | collective-permute-start | bytes 786440 | tf_op jit(solution)/shard_map/ppermute | solution.py:585
  40.7 15.7 %copy-start.1 = (f32[8,128,128]{2,1,0:T(8,128)}, f32[8,128,128]{2,1,0:T(8,128)S(1)}, u32[]{:S(2)}) copy-start(f32[8,128,128]{2,1,0:T(8,128)S(1)} %get-tuple-element.102.state_hbm) | copy-start | bytes 1572868
  40.7 17.2 %copy-start = (f32[512,1024]{1,0:T(8,128)}, f32[512,1024]{1,0:T(8,128)S(1)}, u32[]{:S(2)}) copy-start(f32[512,1024]{1,0:T(8,128)S(1)} %get-tuple-element.93.attn_ref.attn_hbm) | copy-start | bytes 6291460
  56.4 2.9 %collective-permute-start.3 = (f32[4,136,128]{2,1,0:T(8,128)S(1)}, f32[4,136,128]{2,1,0:T(8,128)S(1)}, u32[]{:S(2)}, u32[]{:S(2)}) collective-permute-start(f32[4,136,128]{2,1,0:T(8,128)S(1)} %get-tuple-element.99), channel_id=1, source_target_pairs={{0,8},{8,0},{1,9},{9,1},{2,10},{10,2},{3,11},{11,3},{4,12},{12,4},... | collective-permute-start | bytes 835592 | tf_op jit(solution)/shard_map/ppermute | solution.py:585
  60.3 11.3 %all-to-all-start.3 = ((f32[16,32,128]{2,1,0:T(8,128)}), f32[16,32,128]{2,1,0:T(8,128)S(1)}, u32[]{:S(2)}, u32[]{:S(2)}) async-start(f32[16,32,128]{2,1,0:T(8,128)} %get-tuple-element.100), calls=%async_computation.3 | async-start | bytes 524288 | tf_op jit(solution)/shard_map/all_to_all | solution.py:589
  63.9 13.9 %copy-start.3 = (f32[4,136,128]{2,1,0:T(8,128)S(1)}, f32[4,136,128]{2,1,0:T(8,128)}, u32[]{:S(2)}) copy-start(f32[4,136,128]{2,1,0:T(8,128)} %get-tuple-element.119) | copy-start | bytes 835588
  72.3 12.9 %all-to-all-start.4 = ((f32[16,32,128]{2,1,0:T(8,128)}), f32[16,32,128]{2,1,0:T(8,128)S(1)}, u32[]{:S(2)}, u32[]{:S(2)}) async-start(f32[16,32,128]{2,1,0:T(8,128)} %scan_back.1), calls=%async_computation.4 | async-start | bytes 524288 | tf_op jit(solution)/shard_map/all_to_all | solution.py:589
  77.8 11.6 %collective-permute-start.5 = (f32[4,136,128]{2,1,0:T(8,128)S(1)}, f32[4,136,128]{2,1,0:T(8,128)S(1)}, u32[]{:S(2)}, u32[]{:S(2)}) collective-permute-start(f32[4,136,128]{2,1,0:T(8,128)S(1)} %copy-done.3), channel_id=1, source_target_pairs={{0,8},{8,0},{1,9},{9,1},{2,10},{10,2},{3,11},{11,3},{4,12},{12,4},... | collective-permute-start | bytes 835592 | tf_op jit(solution)/shard_map/ppermute | solution.py:585
  85.3 4.1 %collective-permute-start.4 = (f32[4,128,128]{2,1,0:T(8,128)S(1)}, f32[4,128,128]{2,1,0:T(8,128)S(1)}, u32[]{:S(2)}, u32[]{:S(2)}) collective-permute-start(f32[4,128,128]{2,1,0:T(8,128)S(1)} %bitcast.4), channel_id=1, source_target_pairs={{0,8},{8,0},{1,9},{9,1},{2,10},{10,2},{3,11},{11,3},{4,12},{12,4},... | collective-permute-start | bytes 786440 | tf_op jit(solution)/shard_map/ppermute | solution.py:585

commit v9 on v8

--- a/solution.py
+++ b/solution.py
@@ -92,15 +92,14 @@
     lax.fori_loop(0, heads, step, 0)
 
 
-def each_pair(heads, before, work, after):
-    def step(pair, carry):
-        both = (2 * pair, 2 * pair + 1)
+def each_pair(heads, before, work, after, count=2):
+    def step(first, carry):
         for stage in (before, work, after):
-            for head in both:
-                stage(head)
+            for i in range(count):
+                stage(count * first + i)
         return carry
 
-    lax.fori_loop(0, heads // 2, step, 0)
+    lax.fori_loop(0, heads // count, step, 0)
 
 
 def head_copies(arrays, sems, head):
@@ -240,8 +239,8 @@
     def results(h):
         upper, lower = pl.ds(0, size), pl.ds(size, size)
         pairs = [
-            (probs_ref.at[h, upper, upper], probs_hbm.at[h, upper, upper]),
-            (probs_ref.at[h, lower], probs_hbm.at[h, lower]),
+            (probs_ref.at[h, upper], probs_hbm.at[h, upper]),
+            (probs_ref.at[h, lower, lower], probs_hbm.at[h, lower, lower]),
             (intra_ref.at[:, lanes(h)], intra_hbm.at[:, lanes(h)]),
         ]
         return [pltpu.make_async_copy(a, b, out_sems.at[i, h]) for i, (a, b) in enumerate(pairs)]
@@ -252,8 +251,8 @@
         q, k, v = q_ref[:, lanes(h)], k_ref[:, lanes(h)], v_ref[:, lanes(h)]
         early = decayed(dot(q, k[0:size], NT), 0, within, column)
         late = decayed(dot(q[size:], k[size:], NT), size, within, column)
-        probs_ref[h, :, 0:size] = early
-        probs_ref[h, size:tokens, size:tokens] = late
+        probs_ref[h, 0:size, :] = jnp.transpose(early)
+        probs_ref[h, size:tokens, size:tokens] = jnp.transpose(late)
         intra = dot(early, v[0:size], NN)
         intra_ref[0:size, lanes(h)] = intra[0:size]
         intra_ref[size:tokens, lanes(h)] = intra[size:] + dot(late, v[size:], NN)
@@ -313,24 +312,32 @@
 ):
     core = core_ref[0]
     group = chip_ref.shape[0]
-    pairs = [(within_hbm, within_ref), (lead_hbm, lead_ref)]
-    for half, q, intra in ((core, q_ref, intra_ref), (1 - core, q_far, intra_far)):
-        wide = half_of(half, group)
-        pairs += [
-            (q_hbm.at[:, wide], q),
-            (intra_hbm.at[:, wide], intra),
-            (dnorm_hbm.at[:, wide], dnorm_ref.at[:, wide]),
-        ]
-    made = copies(pairs, sems)
+    near, far = half_of(core, group), half_of(1 - core, group)
+    made = copies(
+        [
+            (within_hbm, within_ref),
+            (q_hbm.at[:, near], q_ref),
+            (lead_hbm, lead_ref),
+            (intra_hbm.at[:, near], intra_ref),
+            (dnorm_hbm.at[:, near], dnorm_ref.at[:, near]),
+            (q_hbm.at[:, far], q_far),
+            (intra_hbm.at[:, far], intra_far),
+            (dnorm_hbm.at[:, far], dnorm_ref.at[:, far]),
+        ],
+        sems,
+    )
     start(made)
-    wait(made[:5])
+    wait(made[:2])
+    for i in range(group):
+        cols = slice(i * HEAD, (i + 1) * HEAD)
+        make_grown(core * group + i, q_ref[:, cols], within_ref, grown_ref)
+    wait(made[2:5])
     square = inner = jnp.zeros(square_ref.shape, F32)
     for i in range(group):
         cols = slice(i * HEAD, (i + 1) * HEAD)
-        head = core * group + i
-        make_grown(head, q_ref[:, cols], within_ref, grown_ref)
         more = attn_head(
-            core, head, i, cols, grown_ref, intra_ref, dnorm_ref, chip_ref, lead_ref, attn_ref, state_ref
+            core, core * group + i, i, cols, grown_ref, intra_ref, dnorm_ref, chip_ref, lead_ref, attn_ref,
+            state_ref,
         )
         square, inner = square + more[0], inner + more[1]
     square_ref[...] = square
@@ -395,38 +402,28 @@
     for i in range(group):
         head = (1 - core_ref[0]) * group + i
         grad = grad_head(head, attn_ref, dnorm_ref, scale_ref, center_ref)
-        grad_ref[:, i * HEAD : (i + 1) * HEAD] = grad
+        grad_ref[:, lanes(head)] = grad
         grad_state(head, i, grad, within_ref, grown_ref, out_ref)
 
 
 def grad_mine_kernel(
-    core_ref, scale_ref, center_ref, table_ref, within_ref, grown_ref, attn_ref, dnorm_ref, grad_far,
-    grad_hbm, table_hbm, out_ref, grad_ref, sems, far_sems,
-):
-    core = core_ref[0]
+    core_ref, scale_ref, center_ref, table_ref, within_ref, grown_ref, attn_ref, dnorm_ref, grad_in,
+    table_hbm, grad_ref, out_ref, sems,
+):
+    made = copies([(table_ref, table_hbm)], sems)
+    start(made)
     group = out_ref.shape[0]
-    made = copies(
-        [(grad_far, grad_hbm.at[:, half_of(1 - core, group)]), (table_ref, table_hbm)], far_sems
-    )
-    start(made)
-    for i in range(group):
-        head = core * group + i
-        cols = slice(i * HEAD, (i + 1) * HEAD)
-        grad_ref[:, cols] = grad_head(head, attn_ref, dnorm_ref, scale_ref, center_ref)
-        store = pltpu.make_async_copy(
-            grad_ref.at[:, cols], grad_hbm.at[:, lanes(head)], sems.at[i]
-        )
-        store.start()
-        made.append(store)
-    for i in range(group):
-        grad = grad_ref[:, i * HEAD : (i + 1) * HEAD]
-        grad_state(core * group + i, i, grad, within_ref, grown_ref, out_ref)
+    for i in range(group):
+        head = core_ref[0] * group + i
+        grad = grad_head(head, attn_ref, dnorm_ref, scale_ref, center_ref)
+        grad_ref[:, lanes(head)] = grad
+        grad_state(head, i, grad, within_ref, grown_ref, out_ref)
     wait(made)
 
 
 def back_kernel(
-    within_hbm, q_hbm, k_hbm, v_hbm, grad_hbm, state_hbm, query_grad_hbm, key_ref,
-    within_ref, q_ref, k_ref, v_ref, grad_ref, state_ref, query_grad_ref, sem, in_sems, out_sems,
+    grad_ref, within_hbm, q_hbm, k_hbm, v_hbm, state_hbm, query_grad_hbm, key_ref,
+    within_ref, q_ref, k_ref, v_ref, state_ref, query_grad_ref, sem, in_sems, out_sems,
 ):
     heads = within_ref.shape[0]
     tokens = q_ref.shape[0]
@@ -434,8 +431,7 @@
     small = copies([(within_hbm, within_ref)], sem)
     start(small)
     loads = [
-        (grad_hbm, grad_ref, 1), (v_hbm, v_ref, 1), (k_hbm, k_ref, 1), (q_hbm, q_ref, 1),
-        (state_hbm, state_ref, 0),
+        (v_hbm, v_ref, 1), (k_hbm, k_ref, 1), (q_hbm, q_ref, 1), (state_hbm, state_ref, 0),
     ]
     stores = [(query_grad_ref, query_grad_hbm, 1)]
     each_head(heads, lambda h: start(head_copies(loads, in_sems, h)))
@@ -466,8 +462,8 @@
 
 
 def value_gate_kernel(
-    table_hbm, attn_hbm, gate_hbm, up_hbm, grad_hbm, probs_hbm, output_hbm, gate_grad_hbm, value_ref,
-    table_ref, attn_ref, gate_ref, up_ref, grad_ref, probs_ref, output_ref, gate_grad_ref,
+    grad_ref, table_hbm, attn_hbm, gate_hbm, up_hbm, probs_hbm, output_hbm, gate_grad_hbm, value_ref,
+    table_ref, attn_ref, gate_ref, up_ref, probs_ref, output_ref, gate_grad_ref,
     scale_ref, sem, in_sems, out_sems,
 ):
     heads = probs_ref.shape[0]
@@ -479,13 +475,13 @@
     def loads(h):
         upper, lower = pl.ds(0, size), pl.ds(size, size)
         pairs = [
-            (probs_hbm.at[h, upper, upper], probs_ref.at[h, upper, upper]),
-            (probs_hbm.at[h, lower], probs_ref.at[h, lower]),
+            (probs_hbm.at[h, upper], probs_ref.at[h, upper]),
+            (probs_hbm.at[h, lower, lower], probs_ref.at[h, lower, lower]),
         ]
         pairs += [
             (a.at[:, lanes(h)], b.at[:, lanes(h)])
             for a, b in (
-                (grad_hbm, grad_ref), (attn_hbm, attn_ref), (gate_hbm, gate_ref), (up_hbm, up_ref)
+                (attn_hbm, attn_ref), (gate_hbm, gate_ref), (up_hbm, up_ref)
             )
         ]
         return [pltpu.make_async_copy(a, b, in_sems.at[i, h]) for i, (a, b) in enumerate(pairs)]
@@ -498,8 +494,8 @@
 
     def one(h):
         at = lanes(h)
-        early = dot(probs_ref[h, :, 0:size], grad_ref[:, at], TN)
-        late = dot(probs_ref[h, size:tokens, size:tokens], grad_ref[size:tokens, at], TN)
+        early = dot(probs_ref[h, 0:size, :], grad_ref[:, at], NN)
+        late = dot(probs_ref[h, size:tokens, size:tokens], grad_ref[size:tokens, at], NN)
         normed = attn_ref[:, at] * scale_ref[...]
         sig = sigmoid(gate_ref[:, at].astype(F32))
         output_ref[:, at] = (normed * sig).astype(BF16)
@@ -508,7 +504,7 @@
         value_ref[size:tokens, at] = late.astype(BF16)
 
     each_pair(
-        heads, lambda h: wait(loads(h)), one, lambda h: start(head_copies(stores, out_sems, h))
+        heads, lambda h: wait(loads(h)), one, lambda h: start(head_copies(stores, out_sems, h)), 1
     )
     each_head(heads, lambda h: wait(head_copies(stores, out_sems, h)))
 
@@ -686,36 +682,35 @@
         (wide, states, sums_rows), (), (), (), core, {8: 0, 9: 1},
     )
     sums = lax.all_to_all(sums, "tp", split_axis=0, concat_axis=0, tiled=True)
-    grad_far, theirs, scale, center, table = call(
+    grad, theirs, scale, center, table = call(
         grad_other_kernel, "grad_other", (sums, within_near, grown, attn, dnorm), (),
-        (half_narrow, packed, column, column, table_rows), (), (), (), core,
+        (narrow, packed, column, column, table_rows), (), (), (), core,
     )
     lead_mine = swap(theirs)
-    grad, table, mine = call(
+    table, grad, mine = call(
         grad_mine_kernel, "grad_mine",
-        (scale, center, table, within_near, grown, attn, dnorm, grad_far), (),
-        (packed,), (narrow, table_rows), (half_narrow,), ((group,), (2,)), core,
+        (scale, center, table, within_near, grown, attn, dnorm, grad), (),
+        (narrow, packed), (table_rows,), (), ((1,),), core, {8: 1},
     )
     chip_state, mine, lead_mine = combined(core, mine, lead_mine, sliced)
     chip_state = spread(chip_state)
-    lead_other = swap(mine)
     query_grad, key_part = call(
-        back_kernel, "back", (), (within, queries, keys, values, grad, state), (narrow,), (narrow,),
-        (rates, narrow, narrow, narrow, narrow, states, narrow), ((1,), (5, heads), (1, heads)),
+        back_kernel, "back", (grad,), (within, queries, keys, values, state), (narrow,), (narrow,),
+        (rates, narrow, narrow, narrow, states, narrow), ((1,), (4, heads), (1, heads)),
     )
     chip_state, key_part, grad, table = lax.optimization_barrier((chip_state, key_part, grad, table))
     chip_state, grad, table = lax.optimization_barrier((scanned(chip_state, decays), grad, table))
     chip_mine = spread(chip_state)
     output, gate_grad, value_part = call(
-        value_gate_kernel, "value_gate", (), (table, attn, gate, out_grad, grad, probs), (narrow,), (narrow, narrow),
-        (table_rows, wide, narrow, narrow, narrow, table_of, narrow, narrow, column),
-        ((1,), (6, heads), (2, heads)), mib=24,
-    )
-    chip_mine, value_part, output, gate_grad = lax.optimization_barrier(
-        (chip_mine, value_part, output, gate_grad)
+        value_gate_kernel, "value_gate", (grad,), (table, attn, gate, out_grad, probs), (narrow,), (narrow, narrow),
+        (table_rows, wide, narrow, narrow, table_of, narrow, narrow, column),
+        ((1,), (5, heads), (2, heads)), mib=24,
+    )
+    chip_mine, value_part, output, gate_grad, mine = lax.optimization_barrier(
+        (chip_mine, value_part, output, gate_grad, mine)
     )
     chip_mine = chip_mine.reshape(group, HEAD, HEAD)
-    chip_other = swap(chip_mine)
+    chip_other, lead_other = swap(chip_mine), swap(mine)
     key_near, value_near, k_far, v_far, within_near = call(
         final_mine_kernel, "final_mine", (chip_mine, key_part, value_part), (within, lead_mine, keys, values),
         (half_narrow,) * 4 + (rates,), (), (packed, half_narrow, half_narrow), ((6,),), core,

time: 92 us -> 91.7 us (level)
  waiting for transfers between devices: 6.72 us -> 8.57 us
  Pallas kernels: 37.6 us -> 36.5 us
  starting transfers between devices: 30.9 us -> 29.9 us
    all_to_all x4, waiting for transfers between devices: 6.33 us -> 7.8 us  [spread(): return lax.all_to_all(x, CHIPS, split_axis=0, concat_axis=0, tiled=True)]
    pallas_call x16, Pallas kernels: 37.6 us -> 36.5 us  [call(): pl.pallas_call(kernel, grid_spec=pltpu.PrefetchScalarGridSpec(num_scalar_...]
    ppermute x6, starting transfers between devices: 12.7 us -> 11.7 us  [swap(): return lax.ppermute(x, 'c', [(0, 1), (1, 0)])]
  transfers between devices with their start and end apart: 10 -> 10, of which waited for: 4 -> 6; matrix products, arithmetic and copies ran while one was open for 0% -> 0% of each run, Pallas kernels for 31% -> 30%
where the time goes in v9:
time: 91.7 us; the launch traced here: 90.7 us
  Pallas kernels  36.5 us (40%)
  starting transfers between devices  29.9 us (33%)
  blocking collectives  14.9 us (16%)
  waiting for transfers between devices  8.57 us (9%)
    pallas_call x16, Pallas kernels, call(): pl.pallas_call(kernel, grid_spec=pltpu.PrefetchScalarGridSpec(num_scalar_...  36.5 us
    all_to_all x4, starting transfers between devices, spread(): return lax.all_to_all(x, CHIPS, split_axis=0, concat_axis=0, tiled=True)  18.2 us
    all_to_all x1, blocking collectives, shards(): sums = lax.all_to_all(sums, 'tp', split_axis=0, concat_axis=0, tiled=True)  14.9 us
    ppermute x6, starting transfers between devices, swap(): return lax.ppermute(x, 'c', [(0, 1), (1, 0)])  11.7 us
    all_to_all x4, waiting for transfers between devices, spread(): return lax.all_to_all(x, CHIPS, split_axis=0, concat_axis=0, tiled=True)  7.8 us
  transfers between devices with their start and end apart: 10, of which 6 were waited for; matrix products, arithmetic and copies ran while one was open for 0% of the time, Pallas kernels for 30%

profile of v9, /device:TPU:1, one launch (start us, length us, event | category | flops | bytes accessed | tf_op | source)
XLA Modules:
  0.0 90.7 jit_solution(4440744406483101098)
XLA Ops:
  0.6 2.1 %local_other.1 = (f32[8,512]{1,0:T(8,128)S(1)}, f32[4,136,128]{2,1,0:T(8,128)S(1)}, bf16[512,512]{1,0:T(8,128)(2,1)S(1)}, bf16[512,512]{1,0:T(8,128)(2,1)S(1)}) custom-call(s32[1]{0:T(128)} %bitcast.core_ref.lead_ref, f32[8,512]{1,0:T(8,128)} %bitcast.8, bf16[512,1024]{1,0:T(8,128)(2,1)} %k_hbm.7, bf16[512,1024]{1,0:T(8,128)(2,1)} %v_hbm.7), custom_call_target="tpu_custom_call" | custom-call | tf_op jit(solution)/shard_map/local_other/pallas_call | solution.py:592
  2.7 3.3 %collective-permute-start = (f32[4,136,128]{2,1,0:T(8,128)S(1)}, f32[4,136,128]{2,1,0:T(8,128)S(1)}, u32[]{:S(2)}, u32[]{:S(2)}) collective-permute-start(f32[4,136,128]{2,1,0:T(8,128)S(1)} %get-tuple-element.72), channel_id=1, source_target_pairs={{0,8},{8,0},{1,9},{9,1},{2,10},{10,2},{3,11},{11,3},{4,12},{12,4},... | collective-permute-start | bytes 835592 | tf_op jit(solution)/shard_map/ppermute | solution.py:581
  7.3 1.0 %combine.2 = (f32[16,40,128]{2,1,0:T(8,128)}, f32[4,136,128]{2,1,0:T(8,128)}, f32[4,136,128]{2,1,0:T(8,128)}) custom-call(s32[1]{0:T(128)S(6)} %sub.3.lead_ref, f32[4,136,128]{2,1,0:T(8,128)S(1)} %local_mine.1.mine_ref, f32[4,136,128]{2,1,0:T(8,128)S(1)} %collective-permute-done.other_ref), custom_call_target="tpu_custom_call" | custom-call | tf_op jit(solution)/shard_map/combine/pallas_call | solution.py:592
  8.2 5.0 %all-to-all-start = ((f32[16,40,128]{2,1,0:T(8,128)}), f32[16,40,128]{2,1,0:T(8,128)S(1)}, u32[]{:S(2)}, u32[]{:S(2)}) async-start(f32[16,40,128]{2,1,0:T(8,128)} %get-tuple-element.73), calls=%async_computation | async-start | bytes 655360 | tf_op jit(solution)/shard_map/all_to_all | solution.py:585
  13.3 5.4 %inside.1 = (bf16[8,512,512]{2,1,0:T(8,128)(2,1)}, f32[512,1024]{1,0:T(8,128)}) custom-call(f32[8,512]{1,0:T(8,128)} %copy-done.2, bf16[512,1024]{1,0:T(8,128)(2,1)} %q_hbm.5, bf16[512,1024]{1,0:T(8,128)(2,1)} %k_hbm.7, bf16[512,1024]{1,0:T(8,128)(2,1)} %v_hbm.7), custom_call_target="tpu_custom_call" | custom-call | tf_op jit(solution)/shard_map/inside/pallas_call | solution.py:592
  18.8 2.5 %all-to-all-done.in_ref = f32[16,40,128]{2,1,0:T(8,128)S(1)} async-done(((f32[16,40,128]{2,1,0:T(8,128)}), f32[16,40,128]{2,1,0:T(8,128)S(1)}, u32[]{:S(2)}, u32[]{:S(2)}) %all-to-all-start) | async-done | bytes 327712 | tf_op jit(solution)/shard_map/all_to_all | solution.py:585
  22.0 4.2 %all-to-all-start.1 = ((f32[16,32,128]{2,1,0:T(8,128)}), f32[16,32,128]{2,1,0:T(8,128)S(1)}, u32[]{:S(2)}, u32[]{:S(2)}) async-start(f32[16,32,128]{2,1,0:T(8,128)} %get-tuple-element.78), calls=%async_computation.1 | async-start | bytes 524288 | tf_op jit(solution)/shard_map/all_to_all | solution.py:585
  26.2 1.7 %collective-permute-start.2 = (f32[4,136,128]{2,1,0:T(8,128)S(1)}, f32[4,136,128]{2,1,0:T(8,128)S(1)}, u32[]{:S(2)}, u32[]{:S(2)}) collective-permute-start(f32[4,136,128]{2,1,0:T(8,128)S(1)} %copy-done.3), channel_id=1, source_target_pairs={{0,8},{8,0},{1,9},{9,1},{2,10},{10,2},{3,11},{11,3},{4,12},{12,4},... | collective-permute-start | bytes 835592 | tf_op jit(solution)/shard_map/ppermute | solution.py:581
  27.9 2.9 %prepare.1.dnorm_hbm = f32[512,1024]{1,0:T(8,128)} custom-call(bf16[512,1024]{1,0:T(8,128)(2,1)} %gate_hbm.3, bf16[512,1024]{1,0:T(8,128)(2,1)} %up_hbm.1), custom_call_target="tpu_custom_call" | custom-call | tf_op jit(solution)/shard_map/prepare/pallas_call | solution.py:592
  30.9 2.6 %all-to-all-done.1 = f32[16,32,128]{2,1,0:T(8,128)S(1)} async-done(((f32[16,32,128]{2,1,0:T(8,128)}), f32[16,32,128]{2,1,0:T(8,128)S(1)}, u32[]{:S(2)}, u32[]{:S(2)}) %all-to-all-start.1) | async-done | bytes 262176 | tf_op jit(solution)/shard_map/all_to_all | solution.py:585
  33.5 2.8 %collective-permute-start.1 = (f32[4,128,128]{2,1,0:T(8,128)S(1)}, f32[4,128,128]{2,1,0:T(8,128)S(1)}, u32[]{:S(2)}, u32[]{:S(2)}) collective-permute-start(f32[4,128,128]{2,1,0:T(8,128)S(1)} %bitcast.4), channel_id=1, source_target_pairs={{0,8},{8,0},{1,9},{9,1},{2,10},{10,2},{3,11},{11,3},{4,12},{12,4},... | collective-permute-start | bytes 786440 | tf_op jit(solution)/shard_map/ppermute | solution.py:581
  36.3 2.9 %attn_mine.1 = (f32[512,1024]{1,0:T(8,128)S(1)}, f32[512,1024]{1,0:T(8,128)S(1)}, bf16[512,2048]{1,0:T(8,128)(2,1)S(1)}, f32[8,128,128]{2,1,0:T(8,128)S(1)}, f32...) custom-call(s32[1]{0:T(128)} %bitcast.core_ref.lead_ref, ...), custom_call_target="tpu_custom_call" | custom-call | tf_op jit(solution)/shard_map/attn_mine/pallas_call | solution.py:592
  39.3 1.3 %attn_other.1 = (f32[512,1024]{1,0:T(8,128)S(1)}, f32[8,128,128]{2,1,0:T(8,128)S(1)}, f32[8,8,128]{2,1,0:T(8,128)S(1)}) custom-call(s32[1]{0:T(128)} %bitcast.core_ref.lead_ref, f32[4,128,128]{2,1,0:T(8,128)S(1)} %collective-permute-done.1.chip_ref, ...), custom_call_target="tpu_custom_call", output_to_operand_aliasing={{0}: (8, {}), {1}: (9, {})} | custom-call | tf_op jit(solution)/shard_map/attn_other/pallas_call | solution.py:592
  40.6 14.9 %all_to_all.25.sums_ref = f32[8,8,128]{2,1,0:T(8,128)S(1)} all-to-all(f32[8,8,128]{2,1,0:T(8,128)S(1)} %get-tuple-element.92), channel_id=1, replica_groups=mesh['x'=4,'y'=4,'c'=2,'tp'=8] {'tp'}, dimensions={0} | all-to-all | bytes 65536 | tf_op jit(solution)/shard_map/all_to_all | solution.py:684
  56.4 1.5 %collective-permute-start.3 = (f32[4,136,128]{2,1,0:T(8,128)S(1)}, f32[4,136,128]{2,1,0:T(8,128)S(1)}, u32[]{:S(2)}, u32[]{:S(2)}) collective-permute-start(f32[4,136,128]{2,1,0:T(8,128)S(1)} %get-tuple-element.100), channel_id=1, source_target_pairs={{0,8},{8,0},{1,9},{9,1},{2,10},{10,2},{3,11},{11,3},{4,12},{12,4},... | collective-permute-start | bytes 835592 | tf_op jit(solution)/shard_map/ppermute | solution.py:581
  60.0 3.5 %all-to-all-start.3 = ((f32[16,32,128]{2,1,0:T(8,128)}), f32[16,32,128]{2,1,0:T(8,128)S(1)}, u32[]{:S(2)}, u32[]{:S(2)}) async-start(f32[16,32,128]{2,1,0:T(8,128)} %get-tuple-element.101), calls=%async_computation.3 | async-start | bytes 524288 | tf_op jit(solution)/shard_map/all_to_all | solution.py:585
  63.6 6.3 %back.1 = (bf16[512,1024]{1,0:T(8,128)(2,1)}, bf16[512,1024]{1,0:T(8,128)(2,1)S(1)}) custom-call(bf16[512,1024]{1,0:T(8,128)(2,1)S(1)} %get-tuple-element.111.grad_ref, f32[8,512]{1,0:T(8,128)} %copy-done.2, bf16[512,1024]{1,0:T(8,128)(2,1)} %q_hbm.5, bf16[512,1024]{1,0:T(8,128)(2,1)} %k_hbm.7, bf16[512,1024]{1,0:T(8,128)(2,1)} %v_hbm.7, ...), custom_call_target="tpu_custom_call" | custom-call | tf_op jit(solution)/shard_map/back/pallas_call | solution.py:592
  69.9 1.2 %all-to-all-done.3.in_ref = f32[16,32,128]{2,1,0:T(8,128)S(1)} async-done(((f32[16,32,128]{2,1,0:T(8,128)}), f32[16,32,128]{2,1,0:T(8,128)S(1)}, u32[]{:S(2)}, u32[]{:S(2)}) %all-to-all-start.3) | async-done | bytes 262176 | tf_op jit(solution)/shard_map/all_to_all | solution.py:585
  71.9 5.4 %all-to-all-start.4 = ((f32[16,32,128]{2,1,0:T(8,128)}), f32[16,32,128]{2,1,0:T(8,128)S(1)}, u32[]{:S(2)}, u32[]{:S(2)}) async-start(f32[16,32,128]{2,1,0:T(8,128)} %scan_back.1), calls=%async_computation.4 | async-start | bytes 524288 | tf_op jit(solution)/shard_map/all_to_all | solution.py:585
  77.3 5.9 %value_gate.1 = (bf16[512,1024]{1,0:T(8,128)(2,1)}, bf16[512,1024]{1,0:T(8,128)(2,1)}, bf16[512,1024]{1,0:T(8,128)(2,1)S(1)}) custom-call(bf16[512,1024]{1,0:T(8,128)(2,1)S(1)} %get-tuple-element.111.grad_ref, f32[8,128]{1,0:T(8,128)} %get-tuple-element.112.table_hbm, f32[512,1024]{1,0:T(8,128)} %copy-done, bf16[512,1024]{1,0:T(8,128)(2,1)} %gate_hbm.3, ...), custom_call_target="tpu_custom_call" | custom-call | tf_op jit(solution)/shard_map/value_gate/pallas_call | solution.py:592
  83.2 1.5 %all-to-all-done.4 = f32[16,32,128]{2,1,0:T(8,128)S(1)} async-done(((f32[16,32,128]{2,1,0:T(8,128)}), f32[16,32,128]{2,1,0:T(8,128)S(1)}, u32[]{:S(2)}, u32[]{:S(2)}) %all-to-all-start.4) | async-done | bytes 262176 | tf_op jit(solution)/shard_map/all_to_all | solution.py:585
  84.7 2.3 %collective-permute-start.5 = (f32[4,136,128]{2,1,0:T(8,128)}, f32[4,136,128]{2,1,0:T(8,128)S(1)}, u32[]{:S(2)}, u32[]{:S(2)}) collective-permute-start(f32[4,136,128]{2,1,0:T(8,128)} %get-tuple-element.121), channel_id=1, source_target_pairs={{0,8},{8,0},{1,9},{9,1},{2,10},{10,2},{3,11},{11,3},{4,12},{12,4},... | collective-permute-start | bytes 835592 | tf_op jit(solution)/shard_map/ppermute | solution.py:581
  87.0 2.1 %final_mine.1 = (bf16[512,512]{1,0:T(8,128)(2,1)S(1)}, bf16[512,512]{1,0:T(8,128)(2,1)S(1)}, bf16[512,512]{1,0:T(8,128)(2,1)S(1)}, bf16[512,512]{1,0:T(8,128)(2,1)S(1)}, f32[8,512]{1,0:T(8,128)S(1)}) custom-call(s32[1]{0:T(128)} %bitcast.core_ref.lead_ref, f32[4,128,128]{2,1,0:T(8,128)S(1)} %bitcast.7, ...), custom_call_target="tpu_custom_call" | custom-call | tf_op jit(solution)/shard_map/final_mine/pallas_call | solution.py:592
  89.1 1.6 %final_other.1 = (bf16[512,1024]{1,0:T(8,128)(2,1)}, bf16[512,1024]{1,0:T(8,128)(2,1)}) custom-call(s32[1]{0:T(128)} %bitcast.core_ref.lead_ref, f32[4,128,128]{2,1,0:T(8,128)S(1)} %collective-permute-done.4.chip_ref, f32[4,136,128]{2,1,0:T(8,128)S(1)} %collective-permute-done.5.lead_ref, f32[8,512]{1,0:T(8,128)S(1)} %get-tuple-element.125.within_ref, ...), custom_call_target="tpu_custom_call" | custom-call | tf_op jit(solution)/shard_map/final_other/pallas_call | solution.py:592
  (21 shorter events, 5.7 us)
Async XLA Ops:
  2.7 10.6 %copy-start.2 = (f32[8,512]{1,0:T(8,128)}, f32[8,512]{1,0:T(8,128)S(1)}, u32[]{:S(2)}) copy-start(f32[8,512]{1,0:T(8,128)S(1)} %get-tuple-element.69.within_ref.within_hbm) | copy-start | bytes 49156
  2.7 4.5 %collective-permute-start = (f32[4,136,128]{2,1,0:T(8,128)S(1)}, f32[4,136,128]{2,1,0:T(8,128)S(1)}, u32[]{:S(2)}, u32[]{:S(2)}) collective-permute-start(f32[4,136,128]{2,1,0:T(8,128)S(1)} %get-tuple-element.72), channel_id=1, source_target_pairs={{0,8},{8,0},{1,9},{9,1},{2,10},{10,2},{3,11},{11,3},{4,12},{12,4},... | collective-permute-start | bytes 835592 | tf_op jit(solution)/shard_map/ppermute | solution.py:581
  8.2 13.0 %all-to-all-start = ((f32[16,40,128]{2,1,0:T(8,128)}), f32[16,40,128]{2,1,0:T(8,128)S(1)}, u32[]{:S(2)}, u32[]{:S(2)}) async-start(f32[16,40,128]{2,1,0:T(8,128)} %get-tuple-element.73), calls=%async_computation | async-start | bytes 655360 | tf_op jit(solution)/shard_map/all_to_all | solution.py:585
  13.3 12.9 %copy-start.3 = (f32[4,136,128]{2,1,0:T(8,128)S(1)}, f32[4,136,128]{2,1,0:T(8,128)}, u32[]{:S(2)}) copy-start(f32[4,136,128]{2,1,0:T(8,128)} %get-tuple-element.81) | copy-start | bytes 835588
  22.0 11.5 %all-to-all-start.1 = ((f32[16,32,128]{2,1,0:T(8,128)}), f32[16,32,128]{2,1,0:T(8,128)S(1)}, u32[]{:S(2)}, u32[]{:S(2)}) async-start(f32[16,32,128]{2,1,0:T(8,128)} %get-tuple-element.78), calls=%async_computation.1 | async-start | bytes 524288 | tf_op jit(solution)/shard_map/all_to_all | solution.py:585
  26.2 13.1 %collective-permute-start.2 = (f32[4,136,128]{2,1,0:T(8,128)S(1)}, f32[4,136,128]{2,1,0:T(8,128)S(1)}, u32[]{:S(2)}, u32[]{:S(2)}) collective-permute-start(f32[4,136,128]{2,1,0:T(8,128)S(1)} %copy-done.3), channel_id=1, source_target_pairs={{0,8},{8,0},{1,9},{9,1},{2,10},{10,2},{3,11},{11,3},{4,12},{12,4},... | collective-permute-start | bytes 835592 | tf_op jit(solution)/shard_map/ppermute | solution.py:581
  33.5 5.8 %collective-permute-start.1 = (f32[4,128,128]{2,1,0:T(8,128)S(1)}, f32[4,128,128]{2,1,0:T(8,128)S(1)}, u32[]{:S(2)}, u32[]{:S(2)}) collective-permute-start(f32[4,128,128]{2,1,0:T(8,128)S(1)} %bitcast.4), channel_id=1, source_target_pairs={{0,8},{8,0},{1,9},{9,1},{2,10},{10,2},{3,11},{11,3},{4,12},{12,4},... | collective-permute-start | bytes 786440 | tf_op jit(solution)/shard_map/ppermute | solution.py:581
  40.5 15.8 %copy-start.1 = (f32[8,128,128]{2,1,0:T(8,128)}, f32[8,128,128]{2,1,0:T(8,128)S(1)}, u32[]{:S(2)}) copy-start(f32[8,128,128]{2,1,0:T(8,128)S(1)} %get-tuple-element.103.state_hbm) | copy-start | bytes 1572868
  40.5 17.3 %copy-start = (f32[512,1024]{1,0:T(8,128)}, f32[512,1024]{1,0:T(8,128)S(1)}, u32[]{:S(2)}) copy-start(f32[512,1024]{1,0:T(8,128)S(1)} %get-tuple-element.94.attn_ref.attn_hbm) | copy-start | bytes 6291460
  56.4 2.7 %collective-permute-start.3 = (f32[4,136,128]{2,1,0:T(8,128)S(1)}, f32[4,136,128]{2,1,0:T(8,128)S(1)}, u32[]{:S(2)}, u32[]{:S(2)}) collective-permute-start(f32[4,136,128]{2,1,0:T(8,128)S(1)} %get-tuple-element.100), channel_id=1, source_target_pairs={{0,8},{8,0},{1,9},{9,1},{2,10},{10,2},{3,11},{11,3},{4,12},{12,4},... | collective-permute-start | bytes 835592 | tf_op jit(solution)/shard_map/ppermute | solution.py:581
  60.0 11.1 %all-to-all-start.3 = ((f32[16,32,128]{2,1,0:T(8,128)}), f32[16,32,128]{2,1,0:T(8,128)S(1)}, u32[]{:S(2)}, u32[]{:S(2)}) async-start(f32[16,32,128]{2,1,0:T(8,128)} %get-tuple-element.101), calls=%async_computation.3 | async-start | bytes 524288 | tf_op jit(solution)/shard_map/all_to_all | solution.py:585
  71.9 12.8 %all-to-all-start.4 = ((f32[16,32,128]{2,1,0:T(8,128)}), f32[16,32,128]{2,1,0:T(8,128)S(1)}, u32[]{:S(2)}, u32[]{:S(2)}) async-start(f32[16,32,128]{2,1,0:T(8,128)} %scan_back.1), calls=%async_computation.4 | async-start | bytes 524288 | tf_op jit(solution)/shard_map/all_to_all | solution.py:585
  84.7 4.4 %collective-permute-start.5 = (f32[4,136,128]{2,1,0:T(8,128)}, f32[4,136,128]{2,1,0:T(8,128)S(1)}, u32[]{:S(2)}, u32[]{:S(2)}) collective-permute-start(f32[4,136,128]{2,1,0:T(8,128)} %get-tuple-element.121), channel_id=1, source_target_pairs={{0,8},{8,0},{1,9},{9,1},{2,10},{10,2},{3,11},{11,3},{4,12},{12,4},... | collective-permute-start | bytes 835592 | tf_op jit(solution)/shard_map/ppermute | solution.py:581
  87.0 2.1 %collective-permute-start.4 = (f32[4,128,128]{2,1,0:T(8,128)S(1)}, f32[4,128,128]{2,1,0:T(8,128)S(1)}, u32[]{:S(2)}, u32[]{:S(2)}) collective-permute-start(f32[4,128,128]{2,1,0:T(8,128)S(1)} %bitcast.6), channel_id=1, source_target_pairs={{0,8},{8,0},{1,9},{9,1},{2,10},{10,2},{3,11},{11,3},{4,12},{12,4},... | collective-permute-start | bytes 786440 | tf_op jit(solution)/shard_map/ppermute | solution.py:581
